TPU v7x, 32 devices: a whole 2x2x4 slice. The times are simulated.
32 devices in a mesh: img: 8 (over z, y), band: 4 (over x, core).
Axes of the slice: x: 2, y: 2, z: 4, core: 2. Of those that a mesh axis runs over, the one named last changes fastest.
Arguments:
- tokens: bfloat16 [8, 1024, 2, 768], P('img', 'band'), may hold values from -6 to 6
- slot_kind: int32 [8, 2], P('img'), may hold values from 0 to 2
- w_qkv: bfloat16 [768, 2304], P('band', 'img'), may hold values from -0.3125 to 0.3125
- w_out: bfloat16 [768, 768], P('band', 'img'), may hold values from -1.75 to 1.75
- w_up: bfloat16 [768, 3072], P('band', 'img'), may hold values from -0.21875 to 0.21875
- w_down: bfloat16 [3072, 768], P('band', 'img'), may hold values from -0.109375 to 0.109375
- bias_qv: bfloat16 [1536], P('img'), may hold values from -2 to 2
- bias_out: bfloat16 [768], P('img'), may hold values from -2 to 2
- bias_up: bfloat16 [3072], P('img'), may hold values from -2 to 2
- bias_down: bfloat16 [768], P('img'), may hold values from -2 to 2
- gain_one: bfloat16 [768], P('img'), may hold values from 0.25 to 1.75
- shift_one: bfloat16 [768], P('img'), may hold values from -2 to 2
- gain_two: bfloat16 [768], P('img'), may hold values from 0.25 to 1.75
- shift_two: bfloat16 [768], P('img'), may hold values from -2 to 2
- cotangent: bfloat16 [8, 1024, 2, 768], P('img', 'band'), may hold values from -6 to 6
Outputs:
- out_tokens: bfloat16 [8, 1024, 2, 768], P('img', 'band')
- grad_tokens: bfloat16 [8, 1024, 2, 768], P('img', 'band')
- grad_w_qkv: float32 [768, 2304], P('band', 'img')
- grad_w_out: float32 [768, 768], P('band', 'img')
- grad_w_up: float32 [768, 3072], P('band', 'img')
- grad_w_down: float32 [3072, 768], P('band', 'img')
- grad_bias_qv: float32 [1536], P('img')
- grad_bias_out: float32 [768], P('img')
- grad_bias_up: float32 [3072], P('img')
- grad_bias_down: float32 [768], P('img')
- grad_gain_one: float32 [768], P('img')
- grad_shift_one: float32 [768], P('img')
- grad_gain_two: float32 [768], P('img')
- grad_shift_two: float32 [768], P('img')
Inputs may be any that keep to these rules, and one draw needn't show every extreme that they name: `slot_kind`: 0: an empty slot. 1: one image of 32 x 32 tokens. 2: four images of (16) x (16) tokens, as image_of gives them.
All inputs are finite; a program needn't handle non-finite values.
Results may differ from a plain program's by a relative error of at most 0.015.
Values may be sent and summed in bfloat16 or wider, within the bound.
A program may use at most 256 MiB of HBM per device.

v0:
```python
import math

import jax
import jax.numpy as jnp
from jax import lax
from jax.sharding import PartitionSpec as P

HEADS = 16
HEAD_DIM = 48


EPSILON = 1e-06
MASKED = -1e30


def layer_norm(values, gain_vec, shift_vec):
    average = jnp.mean(values, axis=-1, keepdims=True)
    centered = values - average
    variance = jnp.mean(centered * centered, axis=-1, keepdims=True)
    return centered * lax.rsqrt(variance + EPSILON) * gain_vec + shift_vec


def exact_gelu(values):
    return jax.nn.gelu(values, approximate=False)


def inner_rows(left_side, right_side):
    return lax.dot_general(
        left_side, right_side, (((0,), (0,)), ((), ())), preferred_element_type=jnp.float32
    )


def outer_cols(left_side, right_side):
    return lax.dot_general(
        left_side, right_side, (((1,), (1,)), ((), ())), preferred_element_type=jnp.float32
    )


def column_sum(values):
    return jnp.sum(values, axis=0, dtype=jnp.float32)


def image_ids(kind_values, positions, band_rows):
    small_id = 2 * (positions % band_rows // (band_rows // 2)) + positions // band_rows // 2
    return jnp.where(kind_values == 2, small_id, 0)


def fetch_img(
    w_qkv,
    w_out,
    w_up,
    w_down,
    bias_qv,
    bias_out,
    bias_up,
    bias_down,
    gain_one,
    shift_one,
    gain_two,
    shift_two,
):
    return (
        lax.all_gather(w_qkv, "img", axis=1, tiled=True),
        lax.all_gather(w_out, "img", axis=1, tiled=True),
        lax.all_gather(w_up, "img", axis=1, tiled=True),
        lax.all_gather(w_down, "img", axis=1, tiled=True),
        lax.all_gather(bias_qv, "img", axis=0, tiled=True),
        lax.all_gather(bias_out, "img", axis=0, tiled=True),
        lax.all_gather(bias_up, "img", axis=0, tiled=True),
        lax.all_gather(bias_down, "img", axis=0, tiled=True),
        lax.all_gather(gain_one, "img", axis=0, tiled=True),
        lax.all_gather(shift_one, "img", axis=0, tiled=True),
        lax.all_gather(gain_two, "img", axis=0, tiled=True),
        lax.all_gather(shift_two, "img", axis=0, tiled=True),
    )


def fetch_band(w_qkv, w_out, w_up, w_down):
    return (
        lax.all_gather(w_qkv, "band", axis=0, tiled=True),
        lax.all_gather(w_out, "band", axis=0, tiled=True),
        lax.all_gather(w_up, "band", axis=0, tiled=True),
        lax.all_gather(w_down, "band", axis=0, tiled=True),
    )


def reduce_img(
    g_qkv,
    g_out,
    g_up,
    g_down,
    g_bias_qv,
    g_bias_out,
    g_bias_up,
    g_bias_down,
    g_gain_one,
    g_shift_one,
    g_gain_two,
    g_shift_two,
):
    return (
        lax.psum_scatter(g_qkv, "img", scatter_dimension=1, tiled=True),
        lax.psum_scatter(g_out, "img", scatter_dimension=1, tiled=True),
        lax.psum_scatter(g_up, "img", scatter_dimension=1, tiled=True),
        lax.psum_scatter(g_down, "img", scatter_dimension=1, tiled=True),
        lax.psum_scatter(g_bias_qv, "img", scatter_dimension=0, tiled=True),
        lax.psum_scatter(g_bias_out, "img", scatter_dimension=0, tiled=True),
        lax.psum_scatter(g_bias_up, "img", scatter_dimension=0, tiled=True),
        lax.psum_scatter(g_bias_down, "img", scatter_dimension=0, tiled=True),
        lax.psum_scatter(g_gain_one, "img", scatter_dimension=0, tiled=True),
        lax.psum_scatter(g_shift_one, "img", scatter_dimension=0, tiled=True),
        lax.psum_scatter(g_gain_two, "img", scatter_dimension=0, tiled=True),
        lax.psum_scatter(g_shift_two, "img", scatter_dimension=0, tiled=True),
    )


def reduce_band(
    g_qkv,
    g_out,
    g_up,
    g_down,
    g_bias_qv,
    g_bias_out,
    g_bias_up,
    g_bias_down,
    g_gain_one,
    g_shift_one,
    g_gain_two,
    g_shift_two,
):
    matrices = (
        lax.psum_scatter(
            g_qkv.astype(jnp.bfloat16), "band", scatter_dimension=0, tiled=True
        ).astype(jnp.float32),
        lax.psum_scatter(
            g_out.astype(jnp.bfloat16), "band", scatter_dimension=0, tiled=True
        ).astype(jnp.float32),
        lax.psum_scatter(g_up.astype(jnp.bfloat16), "band", scatter_dimension=0, tiled=True).astype(
            jnp.float32
        ),
        lax.psum_scatter(
            g_down.astype(jnp.bfloat16), "band", scatter_dimension=0, tiled=True
        ).astype(jnp.float32),
    )
    smalls = (
        lax.psum(g_bias_qv.astype(jnp.bfloat16), "band").astype(jnp.float32),
        lax.psum(g_bias_out.astype(jnp.bfloat16), "band").astype(jnp.float32),
        lax.psum(g_bias_up.astype(jnp.bfloat16), "band").astype(jnp.float32),
        lax.psum(g_bias_down.astype(jnp.bfloat16), "band").astype(jnp.float32),
        lax.psum(g_gain_one.astype(jnp.bfloat16), "band").astype(jnp.float32),
        lax.psum(g_shift_one.astype(jnp.bfloat16), "band").astype(jnp.float32),
        lax.psum(g_gain_two.astype(jnp.bfloat16), "band").astype(jnp.float32),
        lax.psum(g_shift_two.astype(jnp.bfloat16), "band").astype(jnp.float32),
    )
    return tuple(matrices) + tuple(smalls)


def body(
    tokens,
    slot_kind,
    w_qkv,
    w_out,
    w_up,
    w_down,
    bias_qv,
    bias_out,
    bias_up,
    bias_down,
    gain_one,
    shift_one,
    gain_two,
    shift_two,
    cotangent,
):
    band_rows = tokens.shape[1]
    slot_count = tokens.shape[2]
    model_width = tokens.shape[3]
    token_count = band_rows * slot_count
    keys_count = band_rows * lax.axis_size("band")
    band_index = lax.axis_index("band")
    score_scale = 1.0 / math.sqrt(HEAD_DIM)
    banded = fetch_band(w_qkv, w_out, w_up, w_down)
    fetched = fetch_img(
        banded[0],
        banded[1],
        banded[2],
        banded[3],
        bias_qv,
        bias_out,
        bias_up,
        bias_down,
        gain_one,
        shift_one,
        gain_two,
        shift_two,
    )
    matrices = fetched[:4]
    smalls = fetched[4:]
    full_qkv, full_out, full_up, full_down = (matrices[0], matrices[1], matrices[2], matrices[3])
    (
        bias_qv_f,
        bias_out_f,
        bias_up_f,
        bias_down_f,
        gain_one_f,
        shift_one_f,
        gain_two_f,
        shift_two_f,
    ) = tuple((item_small.astype(jnp.float32) for item_small in smalls))
    slot_kinds = slot_kind[0]
    valid_rows = jnp.broadcast_to(
        (slot_kinds > 0).astype(jnp.float32)[None, :, None], (band_rows, slot_count, 1)
    ).reshape(token_count, 1)
    inputs = tokens[0].astype(jnp.float32).reshape(token_count, model_width)
    normed_one, norm_one_back = jax.vjp(layer_norm, inputs, gain_one_f, shift_one_f)
    normed_low = normed_one.astype(jnp.bfloat16)
    projected = jnp.dot(normed_low, full_qkv, preferred_element_type=jnp.float32)
    query_low = ((projected[:, :model_width] + bias_qv_f[:model_width]) * score_scale).astype(
        jnp.bfloat16
    )
    query_low = query_low.reshape(band_rows, slot_count, HEADS, HEAD_DIM)
    key_value = jnp.concatenate(
        [
            projected[:, model_width : 2 * model_width],
            projected[:, 2 * model_width :] + bias_qv_f[model_width:],
        ],
        axis=1,
    )
    key_value = key_value.astype(jnp.bfloat16).reshape(band_rows, slot_count, 2 * model_width)
    positions = jnp.arange(keys_count, dtype=jnp.int32)
    query_pos = band_index * band_rows + jnp.arange(band_rows, dtype=jnp.int32)

    def pair_scores(query_blk, keys_blk, kinds_blk):
        scores = jnp.einsum(
            "rshd,tshd->shrt", query_blk, keys_blk, preferred_element_type=jnp.float32
        )
        key_ids = image_ids(kinds_blk[:, None], positions[None, :], band_rows)
        query_ids = image_ids(kinds_blk[:, None], query_pos[None, :], band_rows)
        allowed = query_ids[:, None, :, None] == key_ids[:, None, None, :]
        return jnp.where(allowed, scores, MASKED)

    def split_kv(source, chosen):
        keys_blk = source[:, chosen, :model_width].reshape(keys_count, 2, HEADS, HEAD_DIM)
        values_blk = source[:, chosen, model_width:].reshape(keys_count, 2, HEADS, HEAD_DIM)
        return (keys_blk, values_blk)

    gathered_kv = lax.all_gather(key_value, "band", axis=0, tiled=True)
    first_slot = 0
    chosen = slice(first_slot, first_slot + 2)
    keys_blk, values_blk = split_kv(gathered_kv, chosen)
    scores = pair_scores(query_low, keys_blk, slot_kinds)
    maximum = jnp.max(scores, axis=-1, keepdims=True)
    exponent = jnp.exp(scores - maximum)
    totals = jnp.sum(exponent, axis=-1, keepdims=True)
    attention_p = (exponent / totals).astype(jnp.bfloat16)
    lse_parts = [maximum + jnp.log(totals)]
    attended_parts = jnp.einsum(
        "shrt,tshd->rshd", attention_p, values_blk, preferred_element_type=jnp.float32
    ).astype(jnp.bfloat16)
    attended = attended_parts.reshape(token_count, model_width)
    branch = jnp.dot(attended, full_out, preferred_element_type=jnp.float32) + bias_out_f
    middle = inputs + branch
    normed_two, norm_two_back = jax.vjp(layer_norm, middle, gain_two_f, shift_two_f)
    normed_two_low = normed_two.astype(jnp.bfloat16)
    hidden_pre = jnp.dot(normed_two_low, full_up, preferred_element_type=jnp.float32) + bias_up_f
    activated, gelu_back = jax.vjp(exact_gelu, hidden_pre)
    act_low = activated.astype(jnp.bfloat16)
    mlp_out = jnp.dot(act_low, full_down, preferred_element_type=jnp.float32) + bias_down_f
    result = (middle + mlp_out) * valid_rows
    out_tokens = result.astype(jnp.bfloat16).reshape(1, band_rows, slot_count, model_width)
    grad_out = cotangent[0].astype(jnp.float32).reshape(token_count, model_width) * valid_rows
    grad_mlp = grad_out.astype(jnp.bfloat16)
    g_down = inner_rows(act_low, grad_mlp)
    g_bias_down = column_sum(grad_mlp)
    grad_act = outer_cols(grad_mlp, full_down)
    grad_hidden = gelu_back(grad_act)[0].astype(jnp.bfloat16)
    g_up = inner_rows(normed_two_low, grad_hidden)
    g_bias_up = column_sum(grad_hidden)
    grad_second = outer_cols(grad_hidden, full_up)
    back_mid, g_gain_two, g_shift_two = norm_two_back(grad_second)
    grad_middle = grad_out + back_mid
    grad_branch = grad_middle.astype(jnp.bfloat16)
    g_out = inner_rows(attended, grad_branch)
    g_bias_out = column_sum(grad_branch)
    grad_att = outer_cols(grad_branch, full_out).astype(jnp.bfloat16)
    grad_att = grad_att.reshape(band_rows, slot_count, HEADS, HEAD_DIM)
    first_slot = 0
    chosen = slice(first_slot, first_slot + 2)
    keys_blk, values_blk = split_kv(gathered_kv, chosen)
    query_blk = query_low
    scores = pair_scores(query_blk, keys_blk, slot_kinds)
    attention_p = jnp.exp(scores - lse_parts[first_slot // 2])
    grad_p = jnp.einsum("rshd,tshd->shrt", grad_att, values_blk, preferred_element_type=jnp.float32)
    row_inner = jnp.sum(attention_p * grad_p, axis=-1, keepdims=True)
    grad_scores = (attention_p * (grad_p - row_inner)).astype(jnp.bfloat16)
    query_parts = jnp.einsum(
        "shrt,tshd->rshd", grad_scores, keys_blk, preferred_element_type=jnp.float32
    )
    grad_keys = jnp.einsum(
        "shrt,rshd->tshd", grad_scores, query_blk, preferred_element_type=jnp.float32
    )
    grad_values = jnp.einsum(
        "shrt,rshd->tshd",
        attention_p.astype(jnp.bfloat16),
        grad_att,
        preferred_element_type=jnp.float32,
    )
    kv_parts = jnp.concatenate(
        [
            grad_keys.reshape(keys_count, 2, model_width),
            grad_values.reshape(keys_count, 2, model_width),
        ],
        axis=2,
    )
    grad_query = (query_parts.reshape(token_count, model_width) * score_scale).astype(jnp.bfloat16)
    summed_kv = lax.psum_scatter(
        kv_parts.astype(jnp.bfloat16), "band", scatter_dimension=0, tiled=True
    )
    grad_kv = summed_kv.reshape(token_count, 2 * model_width)
    grad_qkv = jnp.concatenate([grad_query, grad_kv], axis=1)
    g_qkv = inner_rows(normed_low, grad_qkv)
    g_bias_qv = jnp.concatenate([column_sum(grad_query), column_sum(grad_kv[:, model_width:])])
    grad_first = outer_cols(grad_qkv, full_qkv)
    back_in, g_gain_one, g_shift_one = norm_one_back(grad_first)
    grad_tokens = (
        (grad_middle + back_in).astype(jnp.bfloat16).reshape(1, band_rows, slot_count, model_width)
    )
    banded_g = reduce_band(
        g_qkv,
        g_out,
        g_up,
        g_down,
        g_bias_qv,
        g_bias_out,
        g_bias_up,
        g_bias_down,
        g_gain_one,
        g_shift_one,
        g_gain_two,
        g_shift_two,
    )
    finals = reduce_img(
        banded_g[0],
        banded_g[1],
        banded_g[2],
        banded_g[3],
        banded_g[4],
        banded_g[5],
        banded_g[6],
        banded_g[7],
        banded_g[8],
        banded_g[9],
        banded_g[10],
        banded_g[11],
    )
    return (
        out_tokens,
        grad_tokens,
        finals[0],
        finals[1],
        finals[2],
        finals[3],
        finals[4],
        finals[5],
        finals[6],
        finals[7],
        finals[8],
        finals[9],
        finals[10],
        finals[11],
    )


def solution(mesh):
    return jax.shard_map(
        body,
        mesh=mesh,
        in_specs=(
            P("img", "band", None, None),
            P("img", None),
            P("band", "img"),
            P("band", "img"),
            P("band", "img"),
            P("band", "img"),
            P("img"),
            P("img"),
            P("img"),
            P("img"),
            P("img"),
            P("img"),
            P("img"),
            P("img"),
            P("img", "band", None, None),
        ),
        out_specs=(
            P("img", "band", None, None),
            P("img", "band", None, None),
            P("band", "img"),
            P("band", "img"),
            P("band", "img"),
            P("band", "img"),
            P("img"),
            P("img"),
            P("img"),
            P("img"),
            P("img"),
            P("img"),
            P("img"),
            P("img"),
        ),
        check_vma=False,
    )
```

profile of v0, /device:TPU:0, one launch (start us, length us, event | category | flops | bytes accessed | tf_op | source)
XLA Modules:
  0.0 1055.2 jit_solution(11750248751497532593)
XLA Ops:
  7.2 9.3 all_gather.53
  26.2 39.2 %all-reduce.17 = (bf16[1536]{0:T(1024)(128)(2,1)S(1)}, bf16[768]{0:T(1024)(128)(2,1)S(1)}, bf16[768]{0:T(1024)(128)(2,1)S(1)}, bf16[768]{0:T(1024)(128)(2,1)S(1)...) all-reduce(bf16[1536]{0:T(1024)(128)(2,1)S(1)} %dynamic-update-slic, ...), channel_id=1, replica_groups=mesh['img'=8,'band'=4] {'img'}, use_global_device_ids=true, to_apply=%add.2 | all-reduce | flops 6144 | bytes 24576
  65.4 2.2 reshape.522
  70.2 13.7 %all-gather.7.cloned.1.call-done = bf16[768,2304]{0,1:T(8,128)(2,1)} async-done(((bf16[768,288]{0,1:T(8,128)(2,1)}), bf16[768,2304]{0,1:T(8,128)(2,1)}) %all-gather.7.cloned.1.call-update) | async-done | bytes 3538960 | tf_op jit(solution)/shard_map/all_gather | solution.py:63
  83.8 4.1 fusion.50
  88.0 2.1 copy-done.15
  90.5 2.1 fusion.18
  93.9 3.7 pad_maximum_fusion.1
  97.7 5.7 all_gather.57
  104.3 11.5 %all_gather.62 = bf16[768,384]{1,0:T(8,128)(2,1)} all-gather(bf16[192,384]{1,0:T(8,128)(2,1)S(1)} %copy-done.18), channel_id=1, replica_groups=mesh['img'=8,'band'=4] {'band'}, dimensions={0}, use_global_device_ids=true | all-gather | bytes 737280 | tf_op jit(solution)/shard_map/all_gather | solution.py:82
  115.9 11.7 %all_gather.65 = bf16[3072,96]{0,1:T(8,128)(2,1)} all-gather(bf16[768,96]{0,1:T(8,128)(2,1)S(1)} %copy-done.19), channel_id=1, replica_groups=mesh['img'=8,'band'=4] {'band'}, dimensions={0}, use_global_device_ids=true | all-gather | bytes 737280 | tf_op jit(solution)/shard_map/all_gather | solution.py:83
  127.9 26.2 %all-gather = bf16[8,1,384]{2,1,0:T(2,128)(2,1)S(1)} all-gather(bf16[1,1,384]{2,1,0:T(2,128)(2,1)S(1)} %reshape.546), channel_id=1, replica_groups=mesh['img'=8,'band'=4] {'img'}, dimensions={0}, use_global_device_ids=true | all-gather | bytes 6912 | tf_op jit(solution)/shard_map/all_gather | solution.py:69
  156.9 2.5 reshape.513
  159.4 2.4 copy.63
  161.9 8.5 fusion.55
  170.3 7.0 copy.62
  177.3 8.9 copy.61
  186.2 15.1 %select_reduce_fusion = (f32[2,16,256]{2,1,0:T(8,128)S(1)}, f32[2,16,256,1024]{3,2,1,0:T(8,128)}) fusion(pred[2,256,1024]{2,1,0:T(8,128)(4,1)} %broadcast_compare_fusion, bf16[256,2,16,48]{0,3,2,1:T(8,128)(2,1)} %copy.63, bf16[1024,2,16,48]{0,3,2,1:T(8,128)(2,1)S(1)} %bitcast.56), kind=kOutput, calls=%fused_computation.6 | convolution fusion | flops 822075392 | bytes 38043648 | tf_op jit(solution)/shard_map/rshd,tshd->shrt/dot_general | solution.py:234
  201.3 14.9 %fusion = f32[2,16,256]{2,1,0:T(8,128)S(1)} fusion(f32[2,16,256,1024]{3,2,1,0:T(8,128)} %get-tuple-element.118, f32[2,16,256]{2,1,0:T(8,128)S(1)} %get-tuple-element.117, pred[2,256,1024]{2,1,0:T(8,128)(4,1)S(1)} %copy-done.2), kind=kLoop, calls=%fused_computation.5 | loop fusion | flops 25157632 | bytes 34144256 | tf_op jit(solution)/shard_map/reduce_sum | solution.py:254
  216.3 13.9 %fusion.21 = bf16[256,2,16,48]{0,3,2,1:T(8,128)(2,1)S(1)} fusion(bf16[1024,2,16,48]{0,3,2,1:T(8,128)(2,1)S(1)} %bitcast.59, f32[2,16,256,1024]{3,2,1,0:T(8,128)} %get-tuple-element.118, f32[2,16,256]{2,1,0:T(8,128)S(1)} %fusion, f32[2,16,256]{2,1,0:T(8,128)S(1)} %get-tuple-element.117, pred[2,256,1024]{2,1,0:T(8,128)(4,1)S(1)} %copy-done.2), kind=kOutput, calls=%fused_computation.63 | convolution fusion | flops 839254016 | bytes 38076416 | tf_op jit(solution)/shard_map/shrt,tshd->rshd/dot_general | solution.py:257
  230.2 3.0 copy.64
  233.2 3.6 reshape.515
  236.8 2.9 fusion.58
  240.1 33.5 %all-gather.13.cloned.1.call-done = bf16[768,3072]{1,0:T(8,128)(2,1)} async-done(((bf16[768,384]{1,0:T(8,128)(2,1)}), bf16[768,3072]{1,0:T(8,128)(2,1)}) %all-gather.13.cloned.1.call-update) | async-done | bytes 4718608 | tf_op jit(solution)/shard_map/all_gather | solution.py:65
  273.5 19.8 %multiply_convert_fusion.1 = (bf16[512,3072]{1,0:T(8,128)(2,1)}, f32[512,3072]{1,0:T(8,128)}, f32[512,3072]{1,0:T(8,128)}) fusion(f32[3072]{0:T(1024)S(1)} %bitcast.68, bf16[768,3072]{1,0:T(8,128)(2,1)} %all-gather.13.cloned.1.call-done, f32[512,768]{1,0:T(8,128)S(1)} %get-tuple-element.120, f32[768]{0:T(1024)S(1)} %convert_element_type.205, ...), kind=kOutput, calls=%fused_computation.17 | convolution fusion | flops 2521694208 | bytes 22042624 | tf_op jit(solution)/shard_map/dot_general | solution.py:265
  293.3 59.8 %all-gather.15.cloned.1.call-done = bf16[3072,768]{0,1:T(8,128)(2,1)} async-done(((bf16[3072,96]{0,1:T(8,128)(2,1)}), bf16[3072,768]{0,1:T(8,128)(2,1)}) %all-gather.15.cloned.1.call-update) | async-done | bytes 4718608 | tf_op jit(solution)/shard_map/all_gather | solution.py:66
  353.1 9.2 fusion.60
  362.3 3.0 multiply_reduce_fusion.1
  368.3 2.7 reshape.517
  371.0 1.7 copy.66
  372.8 15.7 %fusion.14 = bf16[2,16,48,1024]{3,2,1,0:T(8,128)(2,1)} fusion(bf16[256,2,16,48]{0,3,2,1:T(8,128)(2,1)S(1)} %copy.66, f32[2,16,256,1024]{3,2,1,0:T(8,128)} %get-tuple-element.118, f32[2,16,256]{2,1,0:T(8,128)S(1)} %log_add_fusion, pred[2,256,1024]{2,1,0:T(8,128)(4,1)S(1)} %copy-done.3), kind=kOutput, calls=%fused_computation.36 | convolution fusion | flops 832045056 | bytes 38043648 | tf_op jit(solution)/shard_map/shrt,rshd->tshd/dot_general | solution.py:302
  388.4 25.3 %multiply_reduce_fusion = (f32[2,16,256]{2,1,0:T(8,128)S(1)}, f32[2,16,256,1024]{3,2,1,0:T(8,128)}) fusion(f32[2,16,256,1024]{3,2,1,0:T(8,128)} %get-tuple-element.118, f32[2,16,256]{2,1,0:T(8,128)S(1)} %log_add_fusion, pred[2,256,1024]{2,1,0:T(8,128)(4,1)S(1)} %copy-done.3, bf16[256,2,16,48]{0,3,2,1:T(8,128)(2,1)S(1)} %copy.66, ...), kind=kOutput, calls=%fused_computation.1 | convolution fusion | flops 838852608 | bytes 71630848 | tf_op jit(solution)/shard_map/rshd,tshd->shrt/dot_general | solution.py:293
  413.8 8.7 copy.71
  422.5 27.8 %multiply_convert_fusion = bf16[2,16,256,1024]{3,2,1,0:T(8,128)(2,1)} fusion(f32[2,16,256,1024]{3,2,1,0:T(8,128)} %get-tuple-element.124, f32[2,16,256,1024]{3,2,1,0:T(8,128)} %get-tuple-element.118, f32[2,16,256]{2,1,0:T(8,128)S(1)} %get-tuple-element.123, f32[2,16,256]{2,1,0:T(8,128)S(1)} %log_add_fusion, pred[2,256,1024]{2,1,0:T(8,128)(4,1)S(1)} %copy-done.3), kind=kLoop, calls=%fused_computation | loop fusion | flops 41943040 | bytes 84475904 | tf_op jit(solution)/shard_map/convert_element_type | solution.py:295
  450.3 9.1 convolution_convert_fusion.3
  459.4 5.9 copy.70
  465.2 8.2 pad_maximum_fusion
  473.5 3.6 convolution_convert_fusion.4
  478.4 11.9 %fusion.59 = (bf16[16,48]{1,0:T(8,128)(2,1)S(1)}, bf16[2,16,48,256]{3,2,1,0:T(8,128)(2,1)}) fusion(bf16[1024,2,16,48]{0,3,2,1:T(8,128)(2,1)S(1)} %bitcast.57, bf16[2,16,256,1024]{3,2,1,0:T(8,128)(2,1)} %multiply_convert_fusion), kind=kOutput, calls=%fused_computation.146 | convolution fusion | flops 806485248 | bytes 20710912 | tf_op jit(solution)/shard_map/shrt,tshd->rshd/dot_general | solution.py:296
  490.4 4.3 copy.67
  494.6 2.5 convert_element_type.222
  498.1 93.5 %all-reduce.21.cloned.1.call-done = bf16[1024,2,1536]{2,1,0:T(2,128)(2,1)} async-done(((bf16[1024,2,1536]{2,1,0:T(2,128)(2,1)}), bf16[1024,2,1536]{2,1,0:T(2,128)(2,1)}) %all-reduce.21.cloned.1.call-update) | async-done | bytes 6291472
  591.5 3.6 constant_dynamic-slice_fusion
  595.2 3.8 reshape.520
  600.3 5.9 convolution_convert_fusion.2
  607.6 6.4 convolution_convert_fusion.1
  615.4 6.8 convolution_convert_fusion
  622.5 2.0 copy.75
  624.6 38.4 %reduce-scatter.15.cloned.1.call-done = bf16[192,2304]{1,0:T(8,128)(2,1)} async-done(((bf16[768,2304]{1,0:T(8,128)(2,1)}), bf16[192,2304]{1,0:T(8,128)(2,1)}) %reduce-scatter.15.cloned.1.call-update) | async-done | bytes 884752 | tf_op jit(solution)/shard_map/reduce_scatter | solution.py:132
  662.9 2.6 copy.73
  665.6 47.8 %reduce-scatter.19.cloned.1.call-done = bf16[192,3072]{1,0:T(8,128)(2,1)} async-done(((bf16[768,3072]{1,0:T(8,128)(2,1)}), bf16[192,3072]{1,0:T(8,128)(2,1)}) %reduce-scatter.19.cloned.1.call-update) | async-done | bytes 1179664 | tf_op jit(solution)/shard_map/reduce_scatter | solution.py:138
  713.5 2.9 convert_element_type.230
  716.5 47.3 %reduce-scatter.23.cloned.1.call-done = bf16[768,768]{1,0:T(8,128)(2,1)} async-done(((bf16[3072,768]{1,0:T(8,128)(2,1)}), bf16[768,768]{1,0:T(8,128)(2,1)}) %reduce-scatter.23.cloned.1.call-update) | async-done | bytes 1179664 | tf_op jit(solution)/shard_map/reduce_scatter | solution.py:141
  763.9 2.7 copy.77
  769.6 7.4 multiply_convert_fusion.4
  777.0 2.8 reshape.516
  780.0 5.0 multiply_reduce_fusion.2
  787.9 11.0 %all-reduce.18 = (bf16[1536]{0:T(1024)(128)(2,1)S(1)}, bf16[768]{0:T(1024)(128)(2,1)S(1)}, bf16[3072]{0:T(1024)(128)(2,1)S(1)}, bf16[768]{0:T(1024)(128)(2,1)S(1...) all-reduce(bf16[1536]{0:T(1024)(128)(2,1)S(1)} %pad_maximum_fusion., ...), channel_id=1, replica_groups=mesh['img'=8,'band'=4] {'band'}, use_global_device_ids=true, to_apply=%region_22.23 | all-reduce | flops 9216 | bytes 36864 | tf_op jit(solution)/shard_map/psum | solution.py:146
  799.0 37.3 %all-reduce.16 = (f32[1536]{0:T(1024)S(1)}, f32[768]{0:T(1024)S(1)}, f32[3072]{0:T(1024)S(1)}, f32[768]{0:T(1024)S(1)}, f32[768]{0:T(1024)S(1)}, /*index=5*/f32[...) all-reduce(bf16[1536]{0:T(1024)(128)(2,1)S(1)} %get-tuple-element.9, ...), channel_id=11, replica_groups=mesh['img'=8,'band'=4] {'img'}, use_global_device_ids=true, to_apply=%region_23.24.clone | all-reduce | flops 9216 | bytes 55296
  841.1 1.6 copy.76
  842.7 59.9 %reduce-scatter.25.cloned.1.call-done = f32[288,192]{1,0:T(8,128)} async-done(((f32[2304,192]{1,0:T(8,128)}), f32[288,192]{1,0:T(8,128)}) %reduce-scatter.25.cloned.1.call-update) | async-done | bytes 221200
  902.6 1.8 copy.74
  904.4 71.3 %reduce-scatter.21.cloned.1.call-done = f32[192,384]{1,0:T(8,128)} async-done(((f32[192,3072]{1,0:T(8,128)}), f32[192,384]{1,0:T(8,128)}) %reduce-scatter.21.cloned.1.call-update) | async-done | bytes 294928 | tf_op jit(solution)/shard_map/reduce_scatter | solution.py:104
  975.8 72.8 %reduce-scatter.29.cloned.1.call-done = f32[96,768]{1,0:T(8,128)} async-done(((f32[768,768]{1,0:T(8,128)}), f32[96,768]{1,0:T(8,128)}) %reduce-scatter.29.cloned.1.call-update) | async-done | bytes 294928
  (185 shorter events, 34.8 us)
Async XLA Ops:
  7.2 60.4 %copy-start.7 = (bf16[1,256,2,768]{3,2,1,0:T(2,128)(2,1)S(1)}, bf16[1,256,2,768]{3,2,1,0:T(2,128)(2,1)}, u32[]{:S(2)}) copy-start(bf16[1,256,2,768]{3,2,1,0:T(2,128)(2,1)} %param.15) | copy-start | bytes 2359300
  7.2 76.6 %all-gather.7.cloned.1.call-start = ((), (), s32[]{:S(2)}) async-start(), calls=%async_computation.8 | async-start | bytes 3981312 | tf_op jit(solution)/shard_map/all_gather | solution.py:63
  17.6 144.3 %all-gather.9.cloned.1.call-start = ((), (), s32[]{:S(2)}) async-start(), calls=%async_computation.9 | async-start | bytes 7864320 | tf_op jit(solution)/shard_map/all_gather | solution.py:247
  65.4 22.6 %copy-start.23 = (f32[768]{0:T(1024)}, f32[768]{0:T(1024)S(1)}, u32[]{:S(2)}) copy-start(f32[768]{0:T(1024)S(1)} %convert_element_type.195) | copy-start | bytes 9220
  65.4 22.6 %copy-start.29 = (f32[768]{0:T(1024)}, f32[768]{0:T(1024)S(1)}, u32[]{:S(2)}) copy-start(f32[768]{0:T(1024)S(1)} %convert_element_type.196) | copy-start | bytes 9220
  67.6 20.4 %copy-start.10 = (f32[512,768]{1,0:T(8,128)}, f32[512,768]{1,0:T(8,128)S(1)}, u32[]{:S(2)}) copy-start(f32[512,768]{1,0:T(8,128)S(1)} %reshape.522) | copy-start | bytes 4718596
  68.5 19.5 %copy-start.25 = (f32[512]{0:T(512)}, f32[512]{0:T(512)S(1)}, u32[]{:S(2)}) copy-start(f32[512]{0:T(512)S(1)} %div.115) | copy-start | bytes 6148
  70.1 13.7 %copy-start.21 = (f32[512]{0:T(512)}, f32[512]{0:T(512)S(1)}, u32[]{:S(2)}) copy-start(f32[512]{0:T(512)S(1)} %add.240) | copy-start | bytes 6148
  70.1 13.7 %copy-start.27 = (f32[512]{0:T(512)}, f32[512]{0:T(512)S(1)}, u32[]{:S(2)}) copy-start(f32[512]{0:T(512)S(1)} %rsqrt.20) | copy-start | bytes 6148
  88.0 2.1 copy-start.15
  92.7 5.0 copy-start.20
  92.7 11.6 %copy-start.18 = (bf16[192,384]{1,0:T(8,128)(2,1)S(1)}, bf16[192,384]{1,0:T(8,128)(2,1)}, u32[]{:S(2)}) copy-start(bf16[192,384]{1,0:T(8,128)(2,1)} %param.19) | copy-start | bytes 442372
  93.9 22.0 %copy-start.19 = (bf16[768,96]{0,1:T(8,128)(2,1)S(1)}, bf16[768,96]{0,1:T(8,128)(2,1)}, u32[]{:S(2)}) copy-start(bf16[768,96]{0,1:T(8,128)(2,1)} %param.20) | copy-start | bytes 442372
  97.6 30.1 %copy-start.37 = (s32[1,2]{1,0:T(1,128)S(1)}, s32[1,2]{1,0:T(1,128)}, u32[]{:S(2)}) copy-start(s32[1,2]{1,0:T(1,128)} %param.16) | copy-start | bytes 28
  97.6 30.1 %copy-start.34 = (bf16[384]{0:T(512)(128)(2,1)S(1)}, bf16[384]{0:T(512)(128)(2,1)}, u32[]{:S(2)}) copy-start(bf16[384]{0:T(512)(128)(2,1)} %param.23) | copy-start | bytes 2308
  97.6 56.7 %copy-start.16 = (bf16[1,256,2,768]{3,2,1,0:T(2,128)(2,1)S(1)}, bf16[1,256,2,768]{3,2,1,0:T(2,128)(2,1)}, u32[]{:S(2)}) copy-start(bf16[1,256,2,768]{3,2,1,0:T(2,128)(2,1)} %param.29) | copy-start | bytes 2359300
  97.6 139.2 %all-gather.11.cloned.1.call-start = ((), (), s32[]{:S(2)}) async-start(), calls=%async_computation.10 | async-start | bytes 1327104 | tf_op jit(solution)/shard_map/all_gather | solution.py:64
  104.2 169.3 %all-gather.13.cloned.1.call-start = ((), (), s32[]{:S(2)}) async-start(), calls=%async_computation.11 | async-start | bytes 5308416 | tf_op jit(solution)/shard_map/all_gather | solution.py:65
  115.8 237.3 %all-gather.15.cloned.1.call-start = ((), (), s32[]{:S(2)}) async-start(), calls=%async_computation.12 | async-start | bytes 5308416 | tf_op jit(solution)/shard_map/all_gather | solution.py:66
  127.6 463.9 %all-reduce.21.cloned.1.call-start = ((), (), s32[]{:S(2)}) async-start(), calls=%async_computation.21 | async-start | bytes 12582912
  127.7 34.1 %copy-start.32 = (f32[2]{0:T(128)}, f32[2]{0:T(128)S(1)}, u32[]{:S(2)}) copy-start(f32[2]{0:T(128)S(1)} %get-tuple-element.115) | copy-start | bytes 28
  177.3 8.9 copy-start
  186.2 15.1 %copy-start.2 = (pred[2,256,1024]{2,1,0:T(8,128)(4,1)S(1)}, pred[2,256,1024]{2,1,0:T(8,128)(4,1)}, u32[]{:S(2)}) copy-start(pred[2,256,1024]{2,1,0:T(8,128)(4,1)} %broadcast_compare_fusion) | copy-start | bytes 1572868
  201.3 14.9 %copy-start.4 = (bf16[1024,2,768]{0,2,1:T(8,128)(2,1)S(1)}, bf16[1024,2,768]{0,2,1:T(8,128)(2,1)}, u32[]{:S(2)}) copy-start(bf16[1024,2,768]{0,2,1:T(8,128)(2,1)} %copy.61) | copy-start | bytes 9437188
  239.7 125.6 %copy-start.13 = (f32[512,768]{1,0:T(8,128)}, f32[512,768]{1,0:T(8,128)S(1)}, u32[]{:S(2)}) copy-start(f32[512,768]{1,0:T(8,128)S(1)} %get-tuple-element.120) | copy-start | bytes 4718596
  273.5 79.6 %copy-start.8 = (f32[512,768]{1,0:T(8,128)S(1)}, f32[512,768]{1,0:T(8,128)}, u32[]{:S(2)}) copy-start(f32[512,768]{1,0:T(8,128)} %reshape.524) | copy-start | bytes 4718596
  353.1 9.2 copy-start.35
  362.3 3.0 copy-start.39
  366.0 1.6 copy-start.36
  366.3 1.2 copy-start.5
  368.3 4.4 copy-start.3
  473.4 3.7 copy-start.38
  473.5 5.0 copy-start.1
  473.5 149.0 %reduce-scatter.17.cloned.1.call-start = ((), (), s32[]{:S(2)}) async-start(), calls=%async_computation.14 | async-start | bytes 1474560 | tf_op jit(solution)/shard_map/reduce_scatter | solution.py:135
  477.1 185.8 %reduce-scatter.15.cloned.1.call-start = ((), (), s32[]{:S(2)}) async-start(), calls=%async_computation.13 | async-start | bytes 4423680 | tf_op jit(solution)/shard_map/reduce_scatter | solution.py:132
  595.2 5.1 copy-start.11
  595.2 5.1 copy-start.24
  595.2 5.1 copy-start.26
  595.2 5.1 copy-start.28
  595.2 5.1 copy-start.30
  606.2 1.4 copy-start.14
  606.2 107.3 %reduce-scatter.19.cloned.1.call-start = ((), (), s32[]{:S(2)}) async-start(), calls=%async_computation.15 | async-start | bytes 5898240 | tf_op jit(solution)/shard_map/reduce_scatter | solution.py:138
  614.0 1.4 copy-start.9
  614.1 149.8 %reduce-scatter.23.cloned.1.call-start = ((), (), s32[]{:S(2)}) async-start(), calls=%async_computation.17 | async-start | bytes 5898240 | tf_op jit(solution)/shard_map/reduce_scatter | solution.py:141
  622.2 218.8 %reduce-scatter.27.cloned.1.call-start = ((), (), s32[]{:S(2)}) async-start(), calls=%async_computation.19 | async-start | bytes 884736
  624.5 278.1 %reduce-scatter.25.cloned.1.call-start = ((), (), s32[]{:S(2)}) async-start(), calls=%async_computation.18 | async-start | bytes 2654208
  665.6 310.2 %reduce-scatter.21.cloned.1.call-start = ((), (), s32[]{:S(2)}) async-start(), calls=%async_computation.16 | async-start | bytes 2654208 | tf_op jit(solution)/shard_map/reduce_scatter | solution.py:104
  716.4 52.1 %copy-start.31 = (bf16[768]{0:T(1024)(128)(2,1)S(1)}, bf16[768]{0:T(1024)(128)(2,1)}, u32[]{:S(2)}) copy-start(bf16[768]{0:T(1024)(128)(2,1)} %get-tuple-element.90) | copy-start | bytes 4612
  716.5 52.1 %copy-start.17 = (bf16[1,256,2,768]{3,2,1,0:T(2,128)(2,1)S(1)}, bf16[1,256,2,768]{3,2,1,0:T(2,128)(2,1)}, u32[]{:S(2)}) copy-start(bf16[1,256,2,768]{3,2,1,0:T(2,128)(2,1)} %param.29) | copy-start | bytes 2359300
  716.5 52.1 %copy-start.33 = (f32[2]{0:T(128)S(1)}, f32[2]{0:T(128)}, u32[]{:S(2)}) copy-start(f32[2]{0:T(128)} %copy-done.32) | copy-start | bytes 28
  716.5 332.0 %reduce-scatter.29.cloned.1.call-start = ((), (), s32[]{:S(2)}) async-start(), calls=%async_computation.20 | async-start | bytes 2654208
  769.6 10.3 copy-start.12
  780.0 5.0 copy-start.22
  785.0 1.4 copy-start.6
Sparse Core Ops, SparseCore 0:
  17.7 66.0 all-gather.6
  97.7 51.4 all-gather.8
  152.0 40.1 all-gather.10
  194.1 79.3 all-gather.12
  275.6 77.4 all-gather.14
  473.6 117.9 all-reduce.20
  594.1 25.7 reduce-scatter.16
  622.5 40.3 reduce-scatter.14
  665.5 47.9 reduce-scatter.18
  715.9 47.9 reduce-scatter.22
  767.2 63.4 reduce-scatter.26
  834.0 68.5 reduce-scatter.24
  906.7 69.0 reduce-scatter.20
  979.7 68.8 reduce-scatter.28
where the time goes:
time: 1070 us; the launch traced here: 1060 us
  waiting for transfers between devices  538 us (50%)
  matrix products  166 us (16%)
  blocking collectives  152 us (14%)
  local copies, waits for them, and re-layouts  113 us (11%)
  other arithmetic  66.7 us (6%)
  between operations  18.8 us (2%)
    unnamed x18, waiting for transfers between devices  226 us
    unnamed x2, blocking collectives  76.5 us
    reduce_scatter x1, waiting for transfers between devices, reduce_img(): lax.psum_scatter(g_up, 'img', scatter_dimension=1, tiled=True)  71.3 us
    all_gather x1, waiting for transfers between devices, fetch_img(): lax.all_gather(w_down, 'img', axis=1, tiled=True)  59.8 us
    reduce_scatter x1, waiting for transfers between devices, reduce_band(): lax.psum_scatter(g_up.astype(jnp.bfloat16), 'band', scatter_dimension=0,...  47.8 us
    reduce_scatter x1, waiting for transfers between devices, reduce_band(): lax.psum_scatter(g_down.astype(jnp.bfloat16), 'band', scatter_dimension=0...  47.3 us
    reduce_scatter x1, waiting for transfers between devices, reduce_band(): lax.psum_scatter(g_qkv.astype(jnp.bfloat16), 'band', scatter_dimension=0,...  38.4 us
    unnamed x112, local copies, waits for them, and re-layouts  34.9 us
  transfers between devices with their start and end apart: 14, of which 10 were waited for; matrix products, arithmetic and copies ran while one was open for 20% of the time, Pallas kernels for 0%

commit v1 on v0

v1 whole, which is shorter than its diff:
```python
import functools
import math

import jax
import jax.numpy as jnp
from jax import lax
from jax.experimental import pallas as pl
from jax.experimental.pallas import tpu as pltpu
from jax.sharding import PartitionSpec as P

HEADS = 16
HEAD_DIM = 48
EPSILON = 1e-06
MASKED = -1e30
BF = jnp.bfloat16
F = jnp.float32
MESH = pl.DeviceIdType.MESH
VM = pl.BlockSpec(memory_space=pltpu.VMEM)
SM = pl.BlockSpec(memory_space=pltpu.SMEM)
ANY = pl.BlockSpec(memory_space=pl.ANY)
LIMIT = 67043328


def dg(left, right, left_dim, right_dim):
    return lax.dot_general(
        left, right, (((left_dim,), (right_dim,)), ((), ())), preferred_element_type=F
    )


def shape(dims, dtype):
    return jax.ShapeDtypeStruct(tuple(dims), dtype)


def row_sums(values):
    ones = jnp.ones((8, values.shape[1]), BF)
    if values.dtype == BF:
        return dg(ones, values, 1, 1)
    high = values.astype(BF)
    low = (values - high.astype(F)).astype(BF)
    return dg(ones, high, 1, 1) + dg(ones, low, 1, 1)


def normalize(values):
    average = jnp.mean(values, axis=0, keepdims=True)
    centered = values - average
    variance = jnp.mean(centered * centered, axis=0, keepdims=True)
    inverse = lax.rsqrt(variance + EPSILON)
    return centered * inverse, inverse


def norm_back(error, normed, inverse, gain):
    f = gain * error
    mean_f = jnp.mean(f, axis=0, keepdims=True)
    mean_fn = jnp.mean(f * normed, axis=0, keepdims=True)
    return (f - mean_f - normed * mean_fn) * inverse


def project_kernel(x_ref, w_ref, gain_ref, shift_ref, bias_ref, h_ref, qkv_ref):
    width = x_ref.shape[0]
    normed, _ = normalize(x_ref[...].astype(F))
    h_ref[...] = (normed * gain_ref[...] + shift_ref[...]).astype(BF)
    scale = 1.0 / math.sqrt(HEAD_DIM)
    step = 256

    @pl.loop(0, 3 * width // step)
    def _(j):
        rows = pl.ds(pl.multiple_of(j * step, step), step)
        out = dg(w_ref[rows, :], h_ref[...], 1, 0) + bias_ref[rows, :]
        qkv_ref[rows, :] = (out * jnp.where(j < width // step, scale, 1.0)).astype(BF)


def project(x, w, gain, shift, bias):
    width, tokens = x.shape
    return pl.pallas_call(
        project_kernel,
        name="project",
        out_shape=(shape((width, tokens), BF), shape((3 * width, tokens), BF)),
        in_specs=[VM] * 5,
        out_specs=(VM, VM),
        compiler_params=pltpu.CompilerParams(vmem_limit_bytes=LIMIT),
    )(x, w, gain, shift, bias)


def fill_bias(scalars_ref, bias_ref, rows):
    lane_half = lax.broadcasted_iota(jnp.int32, (1, rows), 1) // (rows // 2)
    for s in range(2):
        small = scalars_ref[s] == 2
        for other in range(2):
            for half in range(2):
                keep = jnp.logical_and(other == 0, lane_half == half)
                masked = jnp.where(small, MASKED, 0.0)
                bias_ref[pl.ds(4 * s + 2 * other + half, 1), :] = jnp.where(
                    keep, jnp.zeros((1, rows), F), jnp.full((1, rows), masked, F)
                )


def add_bias(scores, bias_ref, s, other):
    rows = scores.shape[0]
    at = 4 * s + 2 * other
    return jnp.concatenate(
        [
            scores[: rows // 2] + bias_ref[pl.ds(at, 1), :],
            scores[rows // 2 :] + bias_ref[pl.ds(at + 1, 1), :],
        ],
        axis=0,
    )


def head_slices(i, rows):
    s, h = i // HEADS, i % HEADS
    lanes = pl.ds(pl.multiple_of(s * rows, rows), rows)
    first = pl.ds(pl.multiple_of(h * HEAD_DIM, 16), HEAD_DIM)
    second = pl.ds(pl.multiple_of(HEADS * HEAD_DIM + h * HEAD_DIM, 16), HEAD_DIM)
    return s, lanes, first, second


def attend_step(i, chip_x, q_ref, kv_ref, bias_ref, out_ref, lse_ref):
    bands = kv_ref.shape[0]
    rows = q_ref.shape[1] // 2
    s, lanes, first, second = head_slices(i, rows)
    q = q_ref[first, lanes]
    scores = []
    maximum = None
    for b in range(bands):
        other = jnp.where(chip_x == b // 2, 0, 1)
        part = add_bias(dg(kv_ref[b, first, lanes], q, 0, 0), bias_ref, s, other)
        scores.append(part)
        top = jnp.max(part, axis=0, keepdims=True)
        maximum = top if maximum is None else jnp.maximum(maximum, top)
    total, acc = 0.0, 0.0
    for b in range(bands):
        weight = jnp.exp(scores[b] - maximum)
        total = total + jnp.sum(weight, axis=0, keepdims=True)
        acc = acc + dg(kv_ref[b, second, lanes], weight.astype(BF), 1, 0)
    out_ref[first, lanes] = acc / total
    lse_ref[pl.ds(i, 1), :] = maximum + jnp.log(total)


def attend_kernel(unroll, scalars_ref, q_ref, kv_ref, out_ref, lse_ref, bias_ref):
    fill_bias(scalars_ref, bias_ref, q_ref.shape[1] // 2)

    @pl.loop(0, 2 * HEADS // unroll)
    def _(j):
        for k in range(unroll):
            attend_step(
                j * unroll + k, scalars_ref[2], q_ref, kv_ref, bias_ref, out_ref, lse_ref
            )


def attend(scalars, q, kv):
    width, tokens = q.shape
    return pl.pallas_call(
        functools.partial(attend_kernel, 4),
        name="attend",
        out_shape=(shape((width, tokens), F), shape((2 * HEADS, tokens // 2), F)),
        in_specs=[SM, VM, VM],
        out_specs=(VM, VM),
        scratch_shapes=[pltpu.VMEM((8, tokens // 2), F)],
        compiler_params=pltpu.CompilerParams(vmem_limit_bytes=LIMIT),
    )(scalars, q, kv)


def attend_back_step(
    i, chip_x, q_ref, kv_ref, out_ref, lse_ref, dout_ref, bias_ref, dq_ref, dkv_ref
):
    bands = kv_ref.shape[0]
    rows = q_ref.shape[1] // 2
    s, lanes, first, second = head_slices(i, rows)
    q = q_ref[first, lanes]
    dout = dout_ref[first, lanes]
    delta = jnp.sum(out_ref[first, lanes] * dout.astype(F), axis=0, keepdims=True)
    lse = lse_ref[pl.ds(i, 1), :]
    dq = 0.0
    for b in range(bands):
        other = jnp.where(chip_x == b // 2, 0, 1)
        k, v = kv_ref[b, first, lanes], kv_ref[b, second, lanes]
        scores = add_bias(dg(k, q, 0, 0), bias_ref, s, other)
        dweight = dg(v, dout, 0, 0)
        weight = jnp.exp(scores - lse)
        dscores = (weight * (dweight - delta)).astype(BF)
        dq = dq + dg(k, dscores, 1, 0)
        dkv_ref[b, first, lanes] = dg(q, dscores, 1, 1).astype(BF)
        dkv_ref[b, second, lanes] = dg(dout, weight.astype(BF), 1, 1).astype(BF)
    dq_ref[first, lanes] = (dq * (1.0 / math.sqrt(HEAD_DIM))).astype(BF)


def attend_back_kernel(
    unroll, scalars_ref, q_ref, kv_ref, out_ref, lse_ref, dout_ref, dq_ref, dkv_ref, bias_ref
):
    fill_bias(scalars_ref, bias_ref, q_ref.shape[1] // 2)

    @pl.loop(0, 2 * HEADS // unroll)
    def _(j):
        for k in range(unroll):
            attend_back_step(
                j * unroll + k,
                scalars_ref[2],
                q_ref,
                kv_ref,
                out_ref,
                lse_ref,
                dout_ref,
                bias_ref,
                dq_ref,
                dkv_ref,
            )


def attend_back(scalars, q, kv, out, lse, dout):
    return pl.pallas_call(
        functools.partial(attend_back_kernel, 4),
        name="attend_back",
        out_shape=(shape(q.shape, BF), shape(kv.shape, BF)),
        in_specs=[SM] + [VM] * 5,
        out_specs=(VM, VM),
        scratch_shapes=[pltpu.VMEM((8, q.shape[1] // 2), F)],
        compiler_params=pltpu.CompilerParams(vmem_limit_bytes=LIMIT),
    )(scalars, q, kv, out, lse, dout)


def middle_kernel(
    x_ref,
    cot_ref,
    valid_ref,
    att_ref,
    w_out_ref,
    w_up_ref,
    w_down_ref,
    bias_out_ref,
    gain_ref,
    shift_ref,
    bias_up_ref,
    bias_down_ref,
    out_ref,
    dmid_ref,
    datt_ref,
    g_out_ref,
    g_up_ref,
    g_down_ref,
    sum_up_ref,
    sums_ref,
    mid_ref,
    norm_ref,
    h_ref,
    dmlp_ref,
    mlp_ref,
    err_ref,
    attb_ref,
    dbranch_ref,
):
    width, tokens = x_ref.shape
    hidden = w_up_ref.shape[0]
    step = 256
    attb_ref[...] = att_ref[...].astype(BF)

    @pl.loop(0, width // step)
    def _(j):
        rows = pl.ds(pl.multiple_of(j * step, step), step)
        mid_ref[rows, :] = (
            dg(w_out_ref[rows, :], attb_ref[...], 1, 0)
            + bias_out_ref[rows, :]
            + x_ref[rows, :].astype(F)
        )

    normed, inverse = normalize(mid_ref[...])
    norm_ref[...] = normed
    h_ref[...] = (normed * gain_ref[...] + shift_ref[...]).astype(BF)
    dmlp_ref[...] = (cot_ref[...].astype(F) * valid_ref[...]).astype(BF)
    mlp_ref[...] = jnp.zeros_like(mlp_ref)
    err_ref[...] = jnp.zeros_like(err_ref)

    @pl.loop(0, hidden // step)
    def _(j):
        rows = pl.ds(pl.multiple_of(j * step, step), step)
        pre = dg(w_up_ref[rows, :], h_ref[...], 1, 0) + bias_up_ref[rows, :]
        phi = 0.5 + 0.5 * lax.erf(pre * math.sqrt(0.5))
        act = (pre * phi).astype(BF)
        slope = phi + pre * jnp.exp(pre * pre * -0.5) * (1.0 / math.sqrt(2.0 * math.pi))
        mlp_ref[...] += dg(w_down_ref[:, rows], act, 1, 0)
        dact = dg(w_down_ref[:, rows], dmlp_ref[...], 0, 0)
        dhid = (slope * dact).astype(BF)
        g_down_ref[:, rows] = dg(dmlp_ref[...], act, 1, 1).astype(BF)
        g_up_ref[rows, :] = dg(dhid, h_ref[...], 1, 1).astype(BF)
        sum_up_ref[:, rows] = row_sums(dhid)
        err_ref[...] += dg(w_up_ref[rows, :], dhid, 0, 0)

    out_ref[...] = ((mid_ref[...] + mlp_ref[...] + bias_down_ref[...]) * valid_ref[...]).astype(BF)
    err = err_ref[...]
    sums_ref[0] = row_sums(dmlp_ref[...])
    sums_ref[1] = row_sums(err * norm_ref[...])
    sums_ref[2] = row_sums(err)
    dmid = cot_ref[...].astype(F) * valid_ref[...] + norm_back(
        err, norm_ref[...], inverse, gain_ref[...]
    )
    dmid_ref[...] = dmid
    dbranch_ref[...] = dmid.astype(BF)
    sums_ref[3] = row_sums(dbranch_ref[...])
    datt_ref[...] = dg(w_out_ref[...], dbranch_ref[...], 0, 0).astype(BF)

    @pl.loop(0, width // step)
    def _(j):
        rows = pl.ds(pl.multiple_of(j * step, step), step)
        g_out_ref[rows, :] = dg(dbranch_ref[rows, :], attb_ref[...], 1, 1).astype(BF)


def middle(x, cot, valid, att, w_out, w_up, w_down, bias_out, gain, shift, bias_up, bias_down):
    width, tokens = x.shape
    hidden = w_up.shape[0]
    full = (width, tokens)
    return pl.pallas_call(
        middle_kernel,
        name="middle",
        out_shape=(
            shape(full, BF),
            shape(full, F),
            shape(full, BF),
            shape(w_out.shape, BF),
            shape(w_up.shape, BF),
            shape(w_down.shape, BF),
            shape((8, hidden), F),
            shape((4, 8, width), F),
        ),
        in_specs=[VM] * 12,
        out_specs=tuple([VM] * 8),
        scratch_shapes=[
            pltpu.VMEM(full, F),
            pltpu.VMEM(full, F),
            pltpu.VMEM(full, BF),
            pltpu.VMEM(full, BF),
            pltpu.VMEM(full, F),
            pltpu.VMEM(full, F),
            pltpu.VMEM(full, BF),
            pltpu.VMEM(full, BF),
        ],
        compiler_params=pltpu.CompilerParams(vmem_limit_bytes=LIMIT),
    )(x, cot, valid, att, w_out, w_up, w_down, bias_out, gain, shift, bias_up, bias_down)


def finish_kernel(
    x_ref, h_ref, dq_ref, dkv_ref, w_ref, gain_ref, dmid_ref, gx_ref, g_ref, sums_ref, err_ref
):
    width, tokens = x_ref.shape
    step = 256
    blocks = width // step
    err_ref[...] = jnp.zeros_like(err_ref)
    for ref, count, base in ((dq_ref, blocks, 0), (dkv_ref, 2 * blocks, blocks)):

        @pl.loop(0, count)
        def _(j):
            rows = pl.ds(pl.multiple_of(j * step, step), step)
            to = pl.ds(pl.multiple_of((j + base) * step, step), step)
            g_ref[to, :] = dg(ref[rows, :], h_ref[...], 1, 1).astype(BF)
            err_ref[...] += dg(w_ref[to, :], ref[rows, :], 0, 0)

    normed, inverse = normalize(x_ref[...].astype(F))
    err = err_ref[...]
    sums_ref[0] = row_sums(dq_ref[...])
    sums_ref[1] = row_sums(dkv_ref[pl.ds(width, width), :])
    sums_ref[2] = row_sums(err * normed)
    sums_ref[3] = row_sums(err)
    gx_ref[...] = (dmid_ref[...] + norm_back(err, normed, inverse, gain_ref[...])).astype(BF)


def finish(x, h, dq, dkv, w, gain, dmid):
    width, tokens = x.shape
    return pl.pallas_call(
        finish_kernel,
        name="finish",
        out_shape=(shape(x.shape, BF), shape(w.shape, BF), shape((4, 8, width), F)),
        in_specs=[VM] * 7,
        out_specs=(VM, VM, VM),
        scratch_shapes=[pltpu.VMEM(x.shape, F)],
        compiler_params=pltpu.CompilerParams(vmem_limit_bytes=LIMIT),
    )(x, h, dq, dkv, w, gain, dmid)


class Place:
    def __init__(self, images):
        self.images = images
        self.depth = images // 2
        self.img = lax.axis_index("img")
        self.band = lax.axis_index("band")
        self.z, self.y = self.img // 2, self.img % 2
        self.x, self.c = self.band // 2, self.band % 2
        self.partner = (self.img, self.band + 1 - 2 * self.c)
        self.across_x = (self.img, self.band + 2 - 4 * self.x)
        self.across_y = (self.img + 1 - 2 * self.y, self.band)

    def along_z(self, k):
        z = lax.rem(self.z + k, self.depth)
        return (2 * z + self.y, self.band), z


def greet(peers):
    barrier = pltpu.get_barrier_semaphore()
    for peer in peers:
        pl.semaphore_signal(barrier, inc=1, device_id=peer, device_id_type=MESH)
    pl.semaphore_wait(barrier, len(peers))


def send(src, dst, send_sem, recv_sem, peer):
    copy = pltpu.make_async_remote_copy(
        src_ref=src,
        dst_ref=dst,
        send_sem=send_sem,
        recv_sem=recv_sem,
        device_id=peer,
        device_id_type=MESH,
    )
    copy.start()
    return copy


def comm_params(collective_id):
    return pltpu.CompilerParams(
        collective_id=collective_id, has_side_effects=True, vmem_limit_bytes=LIMIT
    )


def split_rows(shards, parts):
    return jnp.concatenate(
        [item.reshape(parts, item.shape[0] // parts, item.shape[1]) for item in shards], axis=1
    )


def gather_kernel(
    images, narrow_ref, wide_ref, small_ref, qkv_ref, out_ref, up_ref, down_ref, smalls_ref,
    theirs_ref, mine_ref, mine_wide_ref, local_sem, send_sem, recv_sem, small_send, small_recv,
):
    at = Place(images)
    depth, near = at.depth, at.depth // 2
    peers = [at.partner, at.across_x, at.across_y]
    peers += [at.along_z(k)[0] for k in range(1, depth)]
    others = [(lax.rem(at.img + k, images), at.band) for k in range(1, images)]
    others = peers[:2] + others
    greet(others)
    c = at.c

    first = [
        send(narrow_ref.at[1 - c], theirs_ref, send_sem.at[16], recv_sem.at[16], at.partner)
    ]
    half = wide_ref.shape[0] // 2
    wide = wide_ref.shape[1]
    lanes = pl.ds(pl.multiple_of(c * wide, 128), wide)
    own = pltpu.make_async_copy(
        wide_ref.at[pl.ds(pl.multiple_of(c * half, 8), half), :],
        mine_wide_ref.at[:, lanes],
        local_sem.at[0],
    )
    own.start()
    first.append(
        send(
            wide_ref.at[pl.ds(pl.multiple_of((1 - c) * half, 8), half), :],
            mine_wide_ref.at[:, lanes],
            send_sem.at[17],
            recv_sem.at[17],
            at.partner,
        )
    )
    small_copies = []
    keep = pltpu.make_async_copy(small_ref, smalls_ref.at[at.img], local_sem.at[1])
    keep.start()
    for k in range(1, images):
        small_copies.append(
            send(
                small_ref,
                smalls_ref.at[at.img],
                small_send.at[k - 1],
                small_recv.at[k - 1],
                others[k + 1],
            )
        )
    first[0].wait_recv()
    mine, theirs = narrow_ref[c], theirs_ref[...]
    width = mine.shape[1]
    mine_ref[:, pl.ds(0, width)] = jnp.where(c == 0, mine, theirs)
    mine_ref[:, pl.ds(width, width)] = jnp.where(c == 0, theirs, mine)
    own.wait()
    first[1].wait_recv()

    refs = (qkv_ref, out_ref, up_ref, down_ref)
    views, sources = [], []
    row = 0
    for ref in refs[:3]:
        rows = ref.shape[2] // 2
        sources.append(mine_ref.at[pl.ds(row, rows), :])
        row += rows
    sources.append(mine_wide_ref)

    sends = list(first) + small_copies
    stage = [[None] * 4 for _ in refs]
    locals_ = [keep]

    def rows_of(m):
        rows = refs[m].shape[2] // 2
        return pl.ds(pl.multiple_of(c * rows, 8), rows)

    def lanes_of(m):
        half_lanes = refs[m].shape[3] // 2
        return pl.ds(pl.multiple_of(at.x * half_lanes, 128), half_lanes)

    for m, ref in enumerate(refs):
        piece = ref.at[at.z, at.y, rows_of(m), lanes_of(m)]
        copy = pltpu.make_async_copy(sources[m], piece, local_sem.at[2 + m])
        copy.start()
        stage[m][0] = [copy]
        for k in range(1, depth):
            index = 18 + m * (depth - 1) + k - 1
            stage[m][0].append(
                send(sources[m], piece, send_sem.at[index], recv_sem.at[index], at.along_z(k)[0])
            )

    def second(m):
        stage[m][0][0].wait()
        for copy in stage[m][0][1:]:
            copy.wait_recv()
        region = (pl.ds(0, near), at.y, rows_of(m), lanes_of(m))
        to_x = refs[m].at[region]
        region = (pl.ds(near, depth - near), at.y, rows_of(m), lanes_of(m))
        to_y = refs[m].at[region]
        stage[m][1] = [
            send(to_x, to_x, send_sem.at[4 * m], recv_sem.at[4 * m], at.across_x),
            send(to_y, to_y, send_sem.at[4 * m + 1], recv_sem.at[4 * m + 1], at.across_y),
        ]

    def third(m):
        for copy in stage[m][1]:
            copy.wait_recv()
        to_y = refs[m].at[pl.ds(0, near), at.y, rows_of(m), :]
        to_x = refs[m].at[pl.ds(near, depth - near), :, rows_of(m), lanes_of(m)]
        stage[m][2] = [
            send(to_y, to_y, send_sem.at[4 * m + 2], recv_sem.at[4 * m + 2], at.across_y),
            send(to_x, to_x, send_sem.at[4 * m + 3], recv_sem.at[4 * m + 3], at.across_x),
        ]

    last = 18 + 4 * (depth - 1)

    def fourth(m):
        for copy in stage[m][2]:
            copy.wait_recv()
        part = refs[m].at[:, :, rows_of(m), :]
        stage[m][3] = [
            send(part, part, send_sem.at[last + m], recv_sem.at[last + m], at.partner)
        ]

    second(0)
    second(1)
    third(0)
    second(2)
    third(1)
    fourth(0)
    second(3)
    third(2)
    fourth(1)
    third(3)
    fourth(2)
    fourth(3)
    for m in range(4):
        stage[m][3][0].wait_recv()
        for copy in stage[m][0][1:] + stage[m][1] + stage[m][2] + stage[m][3]:
            copy.wait_send()
    for copy in first:
        copy.wait_send()
    for copy in small_copies:
        copy.wait()
    keep.wait()


def gather(images, narrow, wide, small, widths):
    depth = images // 2
    full = 4 * narrow.shape[2]
    outs = [shape((depth, 2, w, full), BF) for w in widths]
    outs.append(shape((depth, 2, wide.shape[0], 4 * wide.shape[1]), BF))
    outs.append(shape((images,) + small.shape, F))
    count = 18 + 4 * (depth - 1) + 4
    return pl.pallas_call(
        functools.partial(gather_kernel, images),
        name="gather",
        out_shape=tuple(outs),
        in_specs=[VM, VM, VM],
        out_specs=(ANY, ANY, ANY, ANY, VM),
        scratch_shapes=[
            pltpu.VMEM(narrow.shape[1:], BF),
            pltpu.VMEM((narrow.shape[1], 2 * narrow.shape[2]), BF),
            pltpu.VMEM((wide.shape[0] // 2, 2 * wide.shape[1]), BF),
            pltpu.SemaphoreType.DMA((6,)),
            pltpu.SemaphoreType.DMA((count,)),
            pltpu.SemaphoreType.DMA((count,)),
            pltpu.SemaphoreType.DMA((images - 1,)),
            pltpu.SemaphoreType.DMA((images - 1,)),
        ],
        compiler_params=comm_params(0),
    )(narrow, wide, small)


def share_kernel(images, kv_ref, all_ref, local_sem, send_sem, recv_sem):
    at = Place(images)
    greet([at.partner, at.across_x])
    rows = kv_ref.shape[1] // 2
    mine = pltpu.make_async_copy(kv_ref, all_ref.at[at.band], local_sem)
    mine.start()
    copies = []
    for s in range(2):
        lanes = pl.ds(s * rows, rows)
        copies.append(
            send(
                kv_ref.at[:, lanes],
                all_ref.at[at.band, :, lanes],
                send_sem.at[s],
                recv_sem.at[s],
                at.across_x,
            )
        )
    near = send(kv_ref, all_ref.at[at.band], send_sem.at[2], recv_sem.at[2], at.partner)
    passed = []
    for s in range(2):
        copies[s].wait_recv()
        part = all_ref.at[at.across_x[1], :, pl.ds(s * rows, rows)]
        passed.append(send(part, part, send_sem.at[3 + s], recv_sem.at[3 + s], at.partner))
    for copy in passed + [near]:
        copy.wait()
    for copy in copies:
        copy.wait_send()
    mine.wait()


def share(images, bands, kv):
    return pl.pallas_call(
        functools.partial(share_kernel, images),
        name="share",
        out_shape=shape((bands,) + kv.shape, BF),
        in_specs=[VM],
        out_specs=ANY,
        scratch_shapes=[
            pltpu.SemaphoreType.DMA,
            pltpu.SemaphoreType.DMA((5,)),
            pltpu.SemaphoreType.DMA((5,)),
        ],
        compiler_params=comm_params(1),
    )(kv)


def add_rows(total_ref, other_ref, step):
    @pl.loop(0, total_ref.shape[0] // step)
    def _(j):
        rows = pl.ds(pl.multiple_of(j * step, step), step)
        total_ref[rows, :] = (
            total_ref[rows, :].astype(F) + other_ref[rows, :].astype(F)
        ).astype(total_ref.dtype)


def unshare_kernel(images, dkv_ref, sum_ref, near_ref, far_ref, send_sem, recv_sem):
    at = Place(images)
    greet([at.partner, at.across_x])
    mate, far = at.partner[1], at.across_x[1]
    far_mate = at.band + 2 - 4 * at.x + 1 - 2 * at.c
    one = send(dkv_ref.at[far_mate], near_ref.at[0], send_sem.at[0], recv_sem.at[0], at.partner)
    two = send(dkv_ref.at[mate], near_ref.at[1], send_sem.at[1], recv_sem.at[1], at.partner)
    one.wait_recv()
    add_rows(near_ref.at[0], dkv_ref.at[far], 64)
    three = send(near_ref.at[0], far_ref, send_sem.at[2], recv_sem.at[2], at.across_x)
    two.wait_recv()
    add_rows(near_ref.at[1], dkv_ref.at[at.band], 64)
    three.wait_recv()
    sum_ref[...] = near_ref[1]
    add_rows(sum_ref, far_ref, 64)
    for copy in (one, two, three):
        copy.wait_send()


def unshare(images, dkv):
    block = dkv.shape[1:]
    return pl.pallas_call(
        functools.partial(unshare_kernel, images),
        name="unshare",
        out_shape=shape(block, BF),
        in_specs=[VM],
        out_specs=VM,
        scratch_shapes=[
            pltpu.VMEM((2,) + block, BF),
            pltpu.VMEM(block, BF),
            pltpu.SemaphoreType.DMA((3,)),
            pltpu.SemaphoreType.DMA((3,)),
        ],
        compiler_params=comm_params(2),
    )(dkv)


def scatter_kernel(
    images, bands, qkv_ref, out_ref, up_ref, down_ref, small_ref,
    narrow_ref, wide_ref, small_out_ref, *rest,
):
    at = Place(images)
    depth, near = at.depth, at.depth // 2
    c = at.c
    refs = (down_ref, up_ref, out_ref, qkv_ref)
    count = len(refs)
    one, two_x, two_y, three, four = (rest[count * k : count * k + count] for k in range(5))
    away_ref, away_wide_ref, small_in, small_band = rest[5 * count : 5 * count + 4]
    send_sem, recv_sem, small_send, small_recv = rest[5 * count + 4 :]
    others = [(lax.rem(at.img + k, images), at.band) for k in range(1, images)]
    mates = [(at.img, lax.rem(at.band + k, bands)) for k in range(1, bands)]
    greet(others + mates)

    small_copies = []
    for k in range(1, images):
        small_copies.append(
            send(
                small_ref.at[others[k - 1][0]],
                small_in.at[k - 1],
                small_send.at[k - 1],
                small_recv.at[k - 1],
                others[k - 1],
            )
        )

    def rows_of(m, core):
        rows = refs[m].shape[2] // 2
        return pl.ds(pl.multiple_of(core * rows, 8), rows)

    def lanes_of(m, x):
        half_lanes = refs[m].shape[3] // 2
        return pl.ds(pl.multiple_of(x * half_lanes, 128), half_lanes)

    stage = [[] for _ in refs]
    per = 6 + depth - 1
    for m, ref in enumerate(refs):
        stage[m].append(
            [
                send(
                    ref.at[:, :, rows_of(m, 1 - c), :],
                    one[m],
                    send_sem.at[per * m],
                    recv_sem.at[per * m],
                    at.partner,
                )
            ]
        )

    def add(total, other):
        total[...] = (total[...].astype(F) + other[...].astype(F)).astype(BF)

    def first(m):
        stage[m][0][0].wait_recv()

        @pl.loop(0, images)
        def _(j):
            add(one[m].at[j // 2, j % 2], refs[m].at[j // 2, j % 2, rows_of(m, c), :])

        stage[m].append(
            [
                send(
                    one[m].at[pl.ds(0, near), :, :, lanes_of(m, 1 - at.x)],
                    two_x[m],
                    send_sem.at[per * m + 1],
                    recv_sem.at[per * m + 1],
                    at.across_x,
                ),
                send(
                    one[m].at[pl.ds(near, depth - near), 1 - at.y],
                    two_y[m],
                    send_sem.at[per * m + 2],
                    recv_sem.at[per * m + 2],
                    at.across_y,
                ),
            ]
        )

    def second(m):
        stage[m][1][0].wait_recv()

        @pl.loop(0, 2 * near)
        def _(j):
            add(two_x[m].at[j // 2, j % 2], one[m].at[j // 2, j % 2, :, lanes_of(m, at.x)])

        copies = [
            send(
                two_x[m].at[:, 1 - at.y],
                three[m].at[pl.ds(0, near)],
                send_sem.at[per * m + 3],
                recv_sem.at[per * m + 3],
                at.across_y,
            )
        ]
        stage[m][1][1].wait_recv()

        @pl.loop(0, depth - near)
        def _(j):
            add(two_y[m].at[j], one[m].at[near + j, at.y])

        copies.append(
            send(
                two_y[m].at[:, :, lanes_of(m, 1 - at.x)],
                three[m].at[pl.ds(near, depth - near)],
                send_sem.at[per * m + 4],
                recv_sem.at[per * m + 4],
                at.across_x,
            )
        )
        stage[m].append(copies)

    def third(m):
        for copy in stage[m][2]:
            copy.wait_recv()

        @pl.loop(0, near)
        def _(j):
            add(three[m].at[j], two_x[m].at[j, at.y])

        @pl.loop(0, depth - near)
        def _(j):
            add(three[m].at[near + j], two_y[m].at[j, :, lanes_of(m, at.x)])

        copies = []
        for k in range(1, depth):
            peer, z = at.along_z(k)
            copies.append(
                send(
                    three[m].at[z],
                    four[m].at[k - 1],
                    send_sem.at[per * m + 5 + k],
                    recv_sem.at[per * m + 5 + k],
                    peer,
                )
            )
        stage[m].append(copies)

    width = narrow_ref.shape[2]
    starts = {}
    row = 0
    for m in (3, 2, 1):
        starts[m] = row
        row += refs[m].shape[2] // 2

    def fourth(m):
        for copy in stage[m][3]:
            copy.wait_recv()
        total = three[m][at.z].astype(F)
        for k in range(1, depth):
            total = total + four[m][k - 1].astype(F)
        if m == 0:
            lanes = wide_ref.shape[2]
            low, high = total[:, :lanes], total[:, lanes:]
            wide_ref[c] = jnp.where(c == 0, low, high)
            away_wide_ref[...] = jnp.where(c == 0, high, low)
            source, target = away_wide_ref, wide_ref.at[c]
        else:
            rows = pl.ds(starts[m], total.shape[0])
            low, high = total[:, :width], total[:, width:]
            narrow_ref[c, rows, :] = jnp.where(c == 0, low, high)
            away_ref[rows, :] = jnp.where(c == 0, high, low)
            source, target = away_ref.at[rows, :], narrow_ref.at[c, rows, :]
        stage[m].append(
            [send(source, target, send_sem.at[per * m + 5], recv_sem.at[per * m + 5], at.partner)]
        )

    def small_one():
        for copy in small_copies:
            copy.wait_recv()
        total = small_ref[at.img]
        for k in range(1, images):
            total = total + small_in[k - 1]
        small_band[at.band] = total
        copies = []
        for k in range(1, bands):
            slot = images - 2 + k
            copies.append(
                send(
                    small_band.at[at.band],
                    small_band.at[at.band],
                    small_send.at[slot],
                    small_recv.at[slot],
                    mates[k - 1],
                )
            )
        return copies

    first(0)
    first(1)
    second(0)
    first(2)
    second(1)
    third(0)
    first(3)
    second(2)
    third(1)
    fourth(0)
    small_mates = small_one()
    second(3)
    third(2)
    fourth(1)
    third(3)
    fourth(2)
    fourth(3)
    for copy in small_mates:
        copy.wait_recv()
    total = small_band[0]
    for k in range(1, bands):
        total = total + small_band[k]
    small_out_ref[...] = total
    for m in range(count):
        stage[m][4][0].wait_recv()
        for copies in stage[m]:
            for copy in copies:
                copy.wait_send()
    for copy in small_copies + small_mates:
        copy.wait_send()


def scatter(images, bands, qkv, out, up, down, small):
    depth = images // 2
    near = depth // 2
    refs = (down, up, out, qkv)
    full = qkv.shape[3]
    one, two_x, two_y, three, four = [], [], [], [], []
    for ref in refs:
        rows, lanes = ref.shape[2] // 2, ref.shape[3]
        one.append(pltpu.VMEM((depth, 2, rows, lanes), BF))
        two_x.append(pltpu.VMEM((near, 2, rows, lanes // 2), BF))
        two_y.append(pltpu.VMEM((depth - near, rows, lanes), BF))
        three.append(pltpu.VMEM((depth, rows, lanes // 2), BF))
        four.append(pltpu.VMEM((depth - 1, rows, lanes // 2), BF))
    rows = sum(ref.shape[2] // 2 for ref in refs[1:])
    wide_rows, wide = down.shape[2] // 2, down.shape[3] // 4
    count = len(refs) * (6 + depth)
    smalls = images + bands - 2
    return pl.pallas_call(
        functools.partial(scatter_kernel, images, bands),
        name="scatter",
        out_shape=(
            shape((2, rows, full // 4), F),
            shape((2, wide_rows, wide), F),
            shape(small.shape[1:], F),
        ),
        in_specs=[VM] * 5,
        out_specs=(VM, VM, VM),
        scratch_shapes=one
        + two_x
        + two_y
        + three
        + four
        + [
            pltpu.VMEM((rows, full // 4), F),
            pltpu.VMEM((wide_rows, wide), F),
            pltpu.VMEM((images - 1,) + small.shape[1:], F),
            pltpu.VMEM((bands,) + small.shape[1:], F),
            pltpu.SemaphoreType.DMA((count,)),
            pltpu.SemaphoreType.DMA((count,)),
            pltpu.SemaphoreType.DMA((smalls,)),
            pltpu.SemaphoreType.DMA((smalls,)),
        ],
        compiler_params=comm_params(3),
    )(qkv, out, up, down, small)


def pack_small(parts):
    flat = jnp.concatenate([p.reshape(p.shape[0], -1).astype(F) for p in parts], axis=1)
    size = flat.shape[1]
    lines = -(-size // 1024) * 8
    flat = jnp.pad(flat, ((0, 0), (0, lines * 128 - size)))
    return flat.reshape(flat.shape[0], lines, 128)


def unpack_small(packed, sizes):
    flat = packed.reshape(packed.shape[0], -1)
    pieces, start = [], 0
    for size in sizes:
        pieces.append(flat[:, start : start + size].reshape(-1))
        start += size
    return pieces


def body(
    tokens,
    slot_kind,
    w_qkv,
    w_out,
    w_up,
    w_down,
    bias_qv,
    bias_out,
    bias_up,
    bias_down,
    gain_one,
    shift_one,
    gain_two,
    shift_two,
    cotangent,
):
    rows, slots, width = tokens.shape[1:]
    count = rows * slots
    images, bands = lax.axis_size("img"), lax.axis_size("band")
    band = lax.axis_index("band")
    smalls = (bias_qv, bias_out, bias_up, bias_down, gain_one, shift_one, gain_two, shift_two)
    sizes = [item.shape[0] for item in smalls]
    own = (w_qkv, w_out, w_up)
    widths = [item.shape[1] for item in own]
    direct = images % 4 == 0 and all(w % 16 == 0 for w in widths + [w_down.shape[1]])

    def turn(values):
        return values[0].transpose(2, 1, 0).reshape(width, count)

    def turn_back(values):
        return values.reshape(width, slots, rows).transpose(2, 1, 0)[None]

    x, cot = turn(tokens), turn(cotangent)
    kinds = slot_kind[0].astype(jnp.int32)
    valid = jnp.repeat((kinds > 0).astype(F), rows)[None, :]
    scalars = jnp.concatenate([kinds, (band // 2).astype(jnp.int32)[None]])

    small = pack_small([item[None] for item in smalls])[0]
    if direct:
        narrow = split_rows([item.T for item in own], 2)
        *full, small_all = gather(images, narrow, w_down.T, small, widths)
        full = [item.reshape(-1, item.shape[3]) for item in full]
    else:
        full = [
            lax.all_gather(lax.all_gather(item, "band", axis=0, tiled=True).T, "img", tiled=True)
            for item in (*own, w_down)
        ]
        small_all = lax.all_gather(small, "img")
    full_qkv, full_out, full_up, full_down = full
    columns = [item[:, None] for item in unpack_small(small_all, sizes)]
    c_qv, c_out, c_up, c_down, c_gain_one, c_shift_one, c_gain_two, c_shift_two = columns
    bias = jnp.concatenate([c_qv[:width], jnp.zeros((width, 1), F), c_qv[width:]])

    h, qkv = project(x, full_qkv, c_gain_one, c_shift_one, bias)
    q, kv = qkv[:width], qkv[width:]
    all_kv = share(images, bands, kv)
    att, lse = attend(scalars, q, all_kv)
    out, dmid, datt, g_out, g_up, g_down, sum_up, sums_two = middle(
        x, cot, valid, att, full_out, full_up, full_down,
        c_out, c_gain_two, c_shift_two, c_up, c_down,
    )
    dq, dkv = attend_back(scalars, q, all_kv, att, lse, datt)
    dkv = unshare(images, dkv)
    gx, g_qkv, sums_one = finish(x, h, dq, dkv, full_qkv, c_gain_one, dmid)

    small_sums = [
        jnp.concatenate([sums_one[0, 0], sums_one[1, 0]]),
        sums_two[3, 0],
        sum_up[0],
        sums_two[0, 0],
        sums_one[2, 0],
        sums_one[3, 0],
        sums_two[1, 0],
        sums_two[2, 0],
    ]
    packed = pack_small([item.reshape(images, -1) for item in small_sums])
    grads = (g_qkv, g_out, g_up, g_down)
    if direct:
        grads = [item.reshape(images // 2, 2, -1, item.shape[1]) for item in grads]
        narrow, wide, small = scatter(images, bands, *grads, packed)
        matrices, start = [], 0
        for w in widths:
            part = narrow[:, start : start + w // 2].reshape(w, -1)
            matrices.append(part.T)
            start += w // 2
        matrices.append(wide.reshape(-1, wide.shape[2]).T)
    else:
        matrices = [
            lax.psum_scatter(
                lax.psum_scatter(item, "img", scatter_dimension=0, tiled=True),
                "band",
                scatter_dimension=1,
                tiled=True,
            )
            .astype(F)
            .T
            for item in grads
        ]
        small = lax.psum(lax.psum_scatter(packed, "img", scatter_dimension=0), "band")
    return (
        turn_back(out),
        turn_back(gx),
        *matrices,
        *unpack_small(small[None], sizes),
    )


def solution(mesh):
    data, weight, vector = P("img", "band", None, None), P("band", "img"), P("img")
    return jax.shard_map(
        body,
        mesh=mesh,
        in_specs=(data, P("img", None)) + (weight,) * 4 + (vector,) * 8 + (data,),
        out_specs=(data, data) + (weight,) * 4 + (vector,) * 8,
        check_vma=False,
    )
```

time: 1070 us -> 450 us (0.42); the launches traced: 1060 us -> 448 us
  waiting for transfers between devices: 538 us -> 0 us
  Pallas kernels: 0 us -> 389 us
  matrix products: 166 us -> 0 us
  blocking collectives: 152 us -> 0 us
  other arithmetic: 66.7 us -> 4.04 us
  local copies, waits for them, and re-layouts: 113 us -> 54 us
  between operations: 18.8 us -> 0.89 us
    pallas_call x0 -> x9, Pallas kernels: none -> 389 us  [the longest x1 90.7 us: scatter(): pl.pallas_call(functools.partial(scatter_kernel, images, bands), name='sc...]
    unnamed x18 -> x0, waiting for transfers between devices: 226 us -> none
    reduce_scatter x5 -> x0, waiting for transfers between devices: 205 us -> none  [the longest x1 71.3 us: reduce_img(): lax.psum_scatter(g_up, 'img', scatter_dimension=1, tiled=True)]
    dot_general x18 -> x0, matrix products: 166 us -> none  [the longest x1 25.3 us: body(): jnp.einsum('rshd,tshd->shrt', grad_att, values_blk, preferred_element_typ...]
    all_gather x5 -> x0, waiting for transfers between devices: 107 us -> none  [the longest x1 59.8 us: fetch_img(): lax.all_gather(w_down, 'img', axis=1, tiled=True)]
    unnamed x2 -> x0, blocking collectives: 76.5 us -> none
    all_gather x5 -> x0, blocking collectives: 64.5 us -> none  [the longest x1 26.2 us: fetch_img(): lax.all_gather(bias_up, 'img', axis=0, tiled=True)]
    convert_element_type x12 -> x1, other arithmetic: 33.1 us -> 0.66 us  [body(): valid = jnp.repeat((kinds > 0).astype(F), rows)[None, :]]
  transfers between devices with their start and end apart: 14 -> 0, of which waited for: 10 -> 0; matrix products, arithmetic and copies ran while one was open for 20% -> 0% of each run, Pallas kernels for 0% -> 0%
where the time goes in v1:
time: 450 us; the launch traced here: 448 us
  Pallas kernels  389 us (86%)
  local copies, waits for them, and re-layouts  54 us (12%)
    pallas_call x1, Pallas kernels, scatter(): pl.pallas_call(functools.partial(scatter_kernel, images, bands), name='sc...  90.7 us
    pallas_call x1, Pallas kernels, gather(): pl.pallas_call(functools.partial(gather_kernel, images), name='gather', o...  89 us
    pallas_call x1, Pallas kernels, unshare(): pl.pallas_call(functools.partial(unshare_kernel, images), name='unshare',...  45 us
    pallas_call x1, Pallas kernels, attend_back(): pl.pallas_call(functools.partial(attend_back_kernel, 4), name='attend_bac...  42.9 us
    pallas_call x1, Pallas kernels, share(): pl.pallas_call(functools.partial(share_kernel, images), name='share', out...  40.6 us
    pallas_call x1, Pallas kernels, middle(): pl.pallas_call(middle_kernel, name='middle', out_shape=(shape(full, BF),...  38.2 us
    pallas_call x1, Pallas kernels, attend(): pl.pallas_call(functools.partial(attend_kernel, 4), name='attend', out_sh...  22.5 us
    pallas_call x1, Pallas kernels, finish(): pl.pallas_call(finish_kernel, name='finish', out_shape=(shape(x.shape, BF...  12.3 us

profile of v1, /device:TPU:0, one launch (start us, length us, event | category | flops | bytes accessed | tf_op | source)
XLA Modules:
  0.0 448.4 jit_solution(9814219047928416778)
XLA Ops:
  0.7 1.2 pad_add_fusion.scalars_ref
  1.9 0.7 compare_convert_fusion
  2.6 0.7 convert_element_type.40
  3.3 0.6 copy.80
  3.9 0.7 convert_element_type.42
  4.5 0.8 concatenate.26
  5.4 0.6 pad_convert_fusion
  6.0 0.6 pad.14.clone
  6.6 0.9 copy.62
  7.5 1.0 copy.61
  8.5 1.0 copy.63
  9.6 0.8 pad_maximum_fusion.narrow_ref
  10.4 2.8 copy.59
  13.2 1.1 copy.78
  14.2 1.3 copy.60
  15.6 1.1 copy.79
  16.6 89.0 %gather.1 = (bf16[4,2,288,768]{3,2,1,0:T(8,128)(2,1)}, bf16[4,2,96,768]{3,2,1,0:T(8,128)(2,1)}, bf16[4,2,384,768]{3,2,1,0:T(8,128)(2,1)}, bf16[4,2,96,3072]{3,2,1,0:T(8,128)(2,1)}, f32[8,16,128]{2,1,0:T(8,128)}) custom-call(bf16[2,384,192]{2,1,0:T(8,128)(2,1)} %pad_maximum_fusion.narrow_ref, bf16[96,768]{1,0:T(8,128)(2,1)} %bitcast.117, f32[16,128]{1,0:T(8,128)} %bitcast.122), custom_call_target="tpu_custom_call" | custom-call | tf_op jit(solution)/shard_map/gather/pallas_call | solution.py:576
  105.6 0.9 copy.88
  106.5 0.1 slice.105
  106.6 0.1 slice.107
  106.7 0.7 fusion
  107.6 1.0 broadcast_in_dim_reshape.39.bias_down_ref
  108.6 1.0 broadcast_in_dim_reshape.33.gain_ref
  109.6 1.0 broadcast_in_dim_reshape.37.shift_ref
  110.6 1.1 broadcast_in_dim_reshape.36.gain_ref
  111.7 1.0 broadcast_in_dim_reshape.35.bias_out_ref
  112.7 1.0 broadcast_in_dim_reshape.34.shift_ref
  113.7 1.4 copy.66.bias_ref
  115.1 1.6 copy.83
  116.8 8.2 %project.1 = (bf16[768,512]{1,0:T(8,128)(2,1)}, bf16[2304,512]{1,0:T(8,128)(2,1)}) custom-call(bf16[768,512]{1,0:T(8,128)(2,1)} %bitcast.84, bf16[2304,768]{1,0:T(8,128)(2,1)} %bitcast.82, f32[768,1]{1,0:T(8,128)} %broadcast_in_dim_reshape.33.gain_ref, f32[768,1]{1,0:T(8,128)} %broadcast_in_dim_reshape.34.shift_ref, f32[2304,1]{1,0:T(8,128)} %copy.66.bias_ref), custom_call_target="tpu_custom_call" | custom-call | tf_op jit(solution)/shard_map/project/pallas_call | solution.py:74
  125.0 2.1 slice.108.q_ref
  127.1 2.7 slice.109.kv_ref
  129.8 40.6 %share.1.kv_ref = bf16[4,1536,512]{2,1,0:T(8,128)(2,1)} custom-call(bf16[1536,512]{1,0:T(8,128)(2,1)} %slice.109.kv_ref), custom_call_target="tpu_custom_call" | custom-call | tf_op jit(solution)/shard_map/share/pallas_call | solution.py:628
  170.3 22.5 %attend.1 = (f32[768,512]{1,0:T(8,128)}, f32[32,256]{1,0:T(8,128)}) custom-call(s32[3]{0:T(128)} %pad_add_fusion.scalars_ref, bf16[768,512]{1,0:T(8,128)(2,1)} %slice.108.q_ref, bf16[4,1536,512]{2,1,0:T(8,128)(2,1)} %share.1.kv_ref), custom_call_target="tpu_custom_call" | custom-call | tf_op jit(solution)/shard_map/attend/pallas_call | solution.py:152
  192.9 38.2 %middle.1 = (bf16[768,512]{1,0:T(8,128)(2,1)}, f32[768,512]{1,0:T(8,128)}, bf16[768,512]{1,0:T(8,128)(2,1)}, bf16[768,768]{1,0:T(8,128)(2,1)}, bf16[3072,768]{1,...) custom-call(bf16[768,512]{1,0:T(8,128)(2,1)} %bitcast.85, ...), custom_call_target="tpu_custom_call" | custom-call | tf_op jit(solution)/shard_map/middle/pallas_call | solution.py:310
  231.1 42.9 %attend_back.1 = (bf16[768,512]{1,0:T(8,128)(2,1)}, bf16[4,1536,512]{2,1,0:T(8,128)(2,1)}) custom-call(s32[3]{0:T(128)} %pad_add_fusion.scalars_ref, bf16[768,512]{1,0:T(8,128)(2,1)} %slice.108.q_ref, bf16[4,1536,512]{2,1,0:T(8,128)(2,1)} %share.1.kv_ref, f32[768,512]{1,0:T(8,128)} %get-tuple-element.42.att_ref.out_ref, ...), custom_call_target="tpu_custom_call" | custom-call | tf_op jit(solution)/shard_map/attend_back/pallas_call | solution.py:210
  273.9 2.2 reshape.148
  276.2 2.3 copy.72
  278.5 0.9 slice_reduce_fusion
  279.4 0.6 reshape_squeeze.22
  280.0 0.8 slice_reduce_fusion.1
  280.8 0.7 reshape_squeeze.27
  281.5 0.7 reshape_squeeze.26
  282.2 0.7 reshape_squeeze.23
  282.8 0.7 reshape_squeeze.21
  283.5 45.0 %unshare.1.dkv_ref = bf16[1536,512]{1,0:T(8,128)(2,1)} custom-call(bf16[4,1536,512]{2,1,0:T(8,128)(2,1)} %get-tuple-element.51.dkv_ref), custom_call_target="tpu_custom_call" | custom-call | tf_op jit(solution)/shard_map/unshare/pallas_call | solution.py:673
  328.5 12.3 %finish.1 = (bf16[768,512]{1,0:T(8,128)(2,1)}, bf16[2304,768]{1,0:T(8,128)(2,1)}, f32[4,8,768]{2,1,0:T(8,128)}) custom-call(bf16[768,512]{1,0:T(8,128)(2,1)} %bitcast.86, bf16[768,512]{1,0:T(8,128)(2,1)} %get-tuple-element.47.h_ref, bf16[768,512]{1,0:T(8,128)(2,1)} %get-tuple-element.50.dq_ref, bf16[1536,512]{1,0:T(8,128)(2,1)} %unshare.1.dkv_ref, ...), custom_call_target="tpu_custom_call" | custom-call | tf_op jit(solution)/shard_map/finish/pallas_call | solution.py:366
  340.9 2.4 reshape.149
  343.3 2.3 copy.74
  345.7 0.8 slice_reduce_fusion.3
  346.6 0.1 concatenate.29
  346.8 0.1 concatenate.31
  346.9 0.6 copy.87
  347.6 90.7 %scatter.1 = (f32[2,384,192]{2,1,0:T(8,128)}, f32[2,48,768]{2,1,0:T(8,128)}, f32[16,128]{1,0:T(8,128)}) custom-call(bf16[4,2,288,768]{3,2,1,0:T(8,128)(2,1)} %bitcast.92, bf16[4,2,96,768]{3,2,1,0:T(8,128)(2,1)} %bitcast.97, bf16[4,2,384,768]{3,2,1,0:T(8,128)(2,1)} %bitcast.88, bf16[4,2,96,3072]{3,2,1,0:T(8,128)(2,1)} %bitcast.89, f32[8,16,128]{2,1,0:T(8,128)} %bitcast.110), custom_call_target="tpu_custom_call" | custom-call | tf_op jit(solution)/shard_map/scatter/pallas_call | solution.py:927
  438.3 1.3 slice.144
  439.6 1.3 slice_reduce_fusion.9
  440.9 1.4 slice_bitcast_fusion.1
  442.3 0.9 slice.125
  443.2 0.7 copy.76
  443.9 1.0 slice.124
  444.9 1.0 slice.126
  445.9 0.9 copy.77
  446.8 0.9 copy.75
  447.7 0.7 copy.90
  (25 shorter events, 0.5 us)
Async XLA Ops:
  5.4 8.8 %copy-start = (bf16[1,256,2,768]{3,2,1,0:T(2,128)(2,1)S(1)}, bf16[1,256,2,768]{3,2,1,0:T(2,128)(2,1)}, u32[]{:S(2)}) copy-start(bf16[1,256,2,768]{3,2,1,0:T(2,128)(2,1)} %param.29) | copy-start | bytes 2359300
  340.8 6.0 %copy-start.2 = (f32[8,384]{1,0:T(8,128)S(1)}, f32[8,384]{1,0:T(8,128)}, u32[]{:S(2)}) copy-start(f32[8,384]{1,0:T(8,128)} %reshape_squeeze.22) | copy-start | bytes 36868
  340.8 6.0 %copy-start.3 = (f32[8,96]{1,0:T(8,128)S(1)}, f32[8,96]{1,0:T(8,128)}, u32[]{:S(2)}) copy-start(f32[8,96]{1,0:T(8,128)} %reshape_squeeze.27) | copy-start | bytes 9220
  340.8 6.0 %copy-start.4 = (f32[8,96]{1,0:T(8,128)S(1)}, f32[8,96]{1,0:T(8,128)}, u32[]{:S(2)}) copy-start(f32[8,96]{1,0:T(8,128)} %reshape_squeeze.26) | copy-start | bytes 9220
  340.9 6.0 %copy-start.5 = (f32[8,96]{1,0:T(8,128)S(1)}, f32[8,96]{1,0:T(8,128)}, u32[]{:S(2)}) copy-start(f32[8,96]{1,0:T(8,128)} %reshape_squeeze.23) | copy-start | bytes 9220
  340.9 6.0 %copy-start.6 = (f32[8,96]{1,0:T(8,128)S(1)}, f32[8,96]{1,0:T(8,128)}, u32[]{:S(2)}) copy-start(f32[8,96]{1,0:T(8,128)} %reshape_squeeze.21) | copy-start | bytes 9220
  438.3 9.4 %copy-start.1 = (f32[2,48,768]{2,1,0:T(8,128)S(1)}, f32[2,48,768]{2,1,0:T(8,128)}, u32[]{:S(2)}) copy-start(f32[2,48,768]{2,1,0:T(8,128)} %get-tuple-element.62) | copy-start | bytes 884740

commit v2 on v1

--- a/solution.py
+++ b/solution.py
@@ -19,6 +19,7 @@
 SM = pl.BlockSpec(memory_space=pltpu.SMEM)
 ANY = pl.BlockSpec(memory_space=pl.ANY)
 LIMIT = 67043328
+SUM_ROWS, UP_ROW = 16, 8
 
 
 def dg(left, right, left_dim, right_dim):
@@ -161,7 +162,7 @@
 
 
 def attend_back_step(
-    i, chip_x, q_ref, kv_ref, out_ref, lse_ref, dout_ref, bias_ref, dq_ref, dkv_ref
+    i, chip_x, q_ref, kv_ref, out_ref, lse_ref, dout_ref, bias_ref, dq_ref, put_key, put_value
 ):
     bands = kv_ref.shape[0]
     rows = q_ref.shape[1] // 2
@@ -179,8 +180,8 @@
         weight = jnp.exp(scores - lse)
         dscores = (weight * (dweight - delta)).astype(BF)
         dq = dq + dg(k, dscores, 1, 0)
-        dkv_ref[b, first, lanes] = dg(q, dscores, 1, 1).astype(BF)
-        dkv_ref[b, second, lanes] = dg(dout, weight.astype(BF), 1, 1).astype(BF)
+        put_key(b, dg(q, dscores, 1, 1).astype(BF))
+        put_value(b, dg(dout, weight.astype(BF), 1, 1).astype(BF))
     dq_ref[first, lanes] = (dq * (1.0 / math.sqrt(HEAD_DIM))).astype(BF)
 
 
@@ -192,17 +193,18 @@
     @pl.loop(0, 2 * HEADS // unroll)
     def _(j):
         for k in range(unroll):
+            i = j * unroll + k
+            _, lanes, first, second = head_slices(i, q_ref.shape[1] // 2)
+
+            def put_key(b, values):
+                dkv_ref[b, first, lanes] = values
+
+            def put_value(b, values):
+                dkv_ref[b, second, lanes] = values
+
             attend_back_step(
-                j * unroll + k,
-                scalars_ref[2],
-                q_ref,
-                kv_ref,
-                out_ref,
-                lse_ref,
-                dout_ref,
-                bias_ref,
-                dq_ref,
-                dkv_ref,
+                i, scalars_ref[2], q_ref, kv_ref, out_ref, lse_ref, dout_ref, bias_ref, dq_ref,
+                put_key, put_value,
             )
 
 
@@ -237,7 +239,6 @@
     g_out_ref,
     g_up_ref,
     g_down_ref,
-    sum_up_ref,
     sums_ref,
     mid_ref,
     norm_ref,
@@ -252,6 +253,7 @@
     hidden = w_up_ref.shape[0]
     step = 256
     attb_ref[...] = att_ref[...].astype(BF)
+    sums_ref[...] = jnp.zeros_like(sums_ref)
 
     @pl.loop(0, width // step)
     def _(j):
@@ -281,20 +283,22 @@
         dhid = (slope * dact).astype(BF)
         g_down_ref[:, rows] = dg(dmlp_ref[...], act, 1, 1).astype(BF)
         g_up_ref[rows, :] = dg(dhid, h_ref[...], 1, 1).astype(BF)
-        sum_up_ref[:, rows] = row_sums(dhid)
+        per = width // step
+        lanes = pl.ds(pl.multiple_of(j % per * step, step), step)
+        sums_ref[pl.ds(UP_ROW + j // per, 1), lanes] = row_sums(dhid)[:1]
         err_ref[...] += dg(w_up_ref[rows, :], dhid, 0, 0)
 
     out_ref[...] = ((mid_ref[...] + mlp_ref[...] + bias_down_ref[...]) * valid_ref[...]).astype(BF)
     err = err_ref[...]
-    sums_ref[0] = row_sums(dmlp_ref[...])
-    sums_ref[1] = row_sums(err * norm_ref[...])
-    sums_ref[2] = row_sums(err)
+    sums_ref[3:4] = row_sums(dmlp_ref[...])[:1]
+    sums_ref[6:7] = row_sums(err * norm_ref[...])[:1]
+    sums_ref[7:8] = row_sums(err)[:1]
     dmid = cot_ref[...].astype(F) * valid_ref[...] + norm_back(
         err, norm_ref[...], inverse, gain_ref[...]
     )
     dmid_ref[...] = dmid
     dbranch_ref[...] = dmid.astype(BF)
-    sums_ref[3] = row_sums(dbranch_ref[...])
+    sums_ref[2:3] = row_sums(dbranch_ref[...])[:1]
     datt_ref[...] = dg(w_out_ref[...], dbranch_ref[...], 0, 0).astype(BF)
 
     @pl.loop(0, width // step)
@@ -317,11 +321,10 @@
             shape(w_out.shape, BF),
             shape(w_up.shape, BF),
             shape(w_down.shape, BF),
-            shape((8, hidden), F),
-            shape((4, 8, width), F),
+            shape((SUM_ROWS, width), F),
         ),
         in_specs=[VM] * 12,
-        out_specs=tuple([VM] * 8),
+        out_specs=tuple([VM] * 7),
         scratch_shapes=[
             pltpu.VMEM(full, F),
             pltpu.VMEM(full, F),
@@ -354,10 +357,11 @@
 
     normed, inverse = normalize(x_ref[...].astype(F))
     err = err_ref[...]
-    sums_ref[0] = row_sums(dq_ref[...])
-    sums_ref[1] = row_sums(dkv_ref[pl.ds(width, width), :])
-    sums_ref[2] = row_sums(err * normed)
-    sums_ref[3] = row_sums(err)
+    sums_ref[...] = jnp.zeros_like(sums_ref)
+    sums_ref[0:1] = row_sums(dq_ref[...])[:1]
+    sums_ref[1:2] = row_sums(dkv_ref[pl.ds(width, width), :])[:1]
+    sums_ref[4:5] = row_sums(err * normed)[:1]
+    sums_ref[5:6] = row_sums(err)[:1]
     gx_ref[...] = (dmid_ref[...] + norm_back(err, normed, inverse, gain_ref[...])).astype(BF)
 
 
@@ -366,7 +370,7 @@
     return pl.pallas_call(
         finish_kernel,
         name="finish",
-        out_shape=(shape(x.shape, BF), shape(w.shape, BF), shape((4, 8, width), F)),
+        out_shape=(shape(x.shape, BF), shape(w.shape, BF), shape((SUM_ROWS, width), F)),
         in_specs=[VM] * 7,
         out_specs=(VM, VM, VM),
         scratch_shapes=[pltpu.VMEM(x.shape, F)],
@@ -385,6 +389,7 @@
         self.partner = (self.img, self.band + 1 - 2 * self.c)
         self.across_x = (self.img, self.band + 2 - 4 * self.x)
         self.across_y = (self.img + 1 - 2 * self.y, self.band)
+        self.z_peers = [self.along_z(k) for k in range(1, self.depth)]
 
     def along_z(self, k):
         z = lax.rem(self.z + k, self.depth)
@@ -686,271 +691,340 @@
     )(dkv)
 
 
-def scatter_kernel(
-    images, bands, qkv_ref, out_ref, up_ref, down_ref, small_ref,
-    narrow_ref, wide_ref, small_out_ref, *rest,
+def accumulate(total, other):
+    total[...] = (total[...].astype(F) + other[...].astype(F)).astype(total.dtype)
+
+
+class Reduction:
+    def __init__(self, at, make, ref, bufs, target, away):
+        one, two_x, two_y, three, four = bufs
+        self.at, self.ref, self.one, self.two_x, self.two_y = at, ref, one, two_x, two_y
+        self.three, self.four, self.target, self.away = three, four, target, away
+        depth, near, c = at.depth, at.depth // 2, at.c
+        self.near = near
+        rows, half = ref.shape[2] // 2, ref.shape[3] // 2
+
+        def lanes_of(x):
+            return pl.ds(pl.multiple_of(x * half, 128), half)
+
+        self.rows = pl.ds(pl.multiple_of(c * rows, 16), rows)
+        self.lanes = lanes_of(at.x)
+        far_rows = pl.ds(pl.multiple_of((1 - c) * rows, 16), rows)
+        far_lanes = lanes_of(1 - at.x)
+        upper = depth - near
+        self.zero = make(ref.at[:, :, far_rows, :], one, at.partner)
+        self.first = [
+            make(one.at[pl.ds(0, near), :, :, far_lanes], two_x, at.across_x),
+            make(one.at[pl.ds(near, upper), 1 - at.y], two_y, at.across_y),
+        ]
+        self.second = [
+            make(two_x.at[:, 1 - at.y], three.at[pl.ds(0, near)], at.across_y),
+            make(two_y.at[:, :, far_lanes], three.at[pl.ds(near, upper)], at.across_x),
+        ]
+        self.third = [
+            make(three.at[z], four.at[k], peer) for k, (peer, z) in enumerate(at.z_peers)
+        ]
+        self.last = make(away, target.at[c], at.partner)
+
+    def start(self):
+        self.zero.start()
+
+    def step_one(self):
+        self.zero.wait_recv()
+
+        @pl.loop(0, self.ref.shape[0] * 2)
+        def _(j):
+            accumulate(
+                self.one.at[j // 2, j % 2], self.ref.at[j // 2, j % 2, self.rows, :]
+            )
+
+        for copy in self.first:
+            copy.start()
+
+    def step_two(self):
+        self.first[0].wait_recv()
+
+        @pl.loop(0, 2 * self.near)
+        def _(j):
+            accumulate(
+                self.two_x.at[j // 2, j % 2], self.one.at[j // 2, j % 2, :, self.lanes]
+            )
+
+        self.second[0].start()
+        self.first[1].wait_recv()
+
+        @pl.loop(0, self.at.depth - self.near)
+        def _(j):
+            accumulate(self.two_y.at[j], self.one.at[self.near + j, self.at.y])
+
+        self.second[1].start()
+
+    def step_three(self):
+        for copy in self.second:
+            copy.wait_recv()
+
+        @pl.loop(0, self.near)
+        def _(j):
+            accumulate(self.three.at[j], self.two_x.at[j, self.at.y])
+
+        @pl.loop(0, self.at.depth - self.near)
+        def _(j):
+            accumulate(self.three.at[self.near + j], self.two_y.at[j, :, self.lanes])
+
+        for copy in self.third:
+            copy.start()
+
+    def step_four(self):
+        for copy in self.third:
+            copy.wait_recv()
+        c = self.at.c
+        total = self.three[self.at.z].astype(F)
+        for k in range(len(self.third)):
+            total = total + self.four[k].astype(F)
+        size = total.shape[1] // 2
+        low, high = total[:, :size], total[:, size:]
+        self.target[c] = jnp.where(c == 0, low, high)
+        self.away[...] = jnp.where(c == 0, high, low)
+        self.last.start()
+
+    def end(self):
+        self.last.wait()
+        for copy in [self.zero] + self.first + self.second + self.third:
+            copy.wait_send()
+
+
+def back_kernel(
+    images, bands, scalars_ref, q_ref, kv_ref, att_ref, lse_ref, datt_ref, x_ref, h_ref, dmid_ref,
+    w_ref, gain_ref, g_out_ref, g_up_ref, g_down_ref, sums_ref,
+    gx_ref, p_qkv_ref, p_out_ref, p_up_ref, p_down_ref, total_ref,
+    bias_ref, dqkv_ref, dkv_ref, near_ref, far_ref, g_qkv_ref, err_ref,
+    small_ref, small_in_ref, small_z_ref, *rest,
 ):
     at = Place(images)
-    depth, near = at.depth, at.depth // 2
-    c = at.c
-    refs = (down_ref, up_ref, out_ref, qkv_ref)
-    count = len(refs)
-    one, two_x, two_y, three, four = (rest[count * k : count * k + count] for k in range(5))
-    away_ref, away_wide_ref, small_in, small_band = rest[5 * count : 5 * count + 4]
-    send_sem, recv_sem, small_send, small_recv = rest[5 * count + 4 :]
-    others = [(lax.rem(at.img + k, images), at.band) for k in range(1, images)]
-    mates = [(at.img, lax.rem(at.band + k, bands)) for k in range(1, bands)]
-    greet(others + mates)
-
-    small_copies = []
-    for k in range(1, images):
-        small_copies.append(
-            send(
-                small_ref.at[others[k - 1][0]],
-                small_in.at[k - 1],
-                small_send.at[k - 1],
-                small_recv.at[k - 1],
-                others[k - 1],
+    depth = at.depth
+    send_sem, recv_sem = rest[-2:]
+    used = [0]
+
+    def make(src, dst, peer):
+        k = used[0]
+        used[0] += 1
+        return pltpu.make_async_remote_copy(
+            src_ref=src,
+            dst_ref=dst,
+            send_sem=send_sem.at[k],
+            recv_sem=recv_sem.at[k],
+            device_id=peer,
+            device_id_type=MESH,
+        )
+
+    width, tokens = x_ref.shape
+    rows = tokens // 2
+    unroll = 4
+    groups = HEADS // unroll
+    part = width // groups
+
+    def four_d(ref):
+        return ref.reshape(depth, 2, ref.shape[0] // images, ref.shape[1])
+
+    sources = (four_d(g_down_ref), four_d(g_up_ref), four_d(g_out_ref), g_qkv_ref)
+    targets = (p_down_ref, p_up_ref, p_out_ref, p_qkv_ref)
+    moves = []
+    for m in range(4):
+        moves.append(
+            Reduction(at, make, sources[m], rest[6 * m : 6 * m + 5], targets[m], rest[6 * m + 5])
+        )
+    down, up, out, qkv = moves
+    mate, far = at.partner[1], at.across_x[1]
+    far_mate = at.across_x[1] + 1 - 2 * at.c
+    one = [make(dkv_ref.at[far_mate, g], near_ref.at[0, g], at.partner) for g in range(groups)]
+    two = [make(dkv_ref.at[mate, g], near_ref.at[1, g], at.partner) for g in range(groups)]
+    three = [make(near_ref.at[0, g], far_ref.at[g], at.across_x) for g in range(groups)]
+    small_steps = [
+        make(small_ref.at[k], small_in_ref.at[k], peer)
+        for k, peer in enumerate((at.partner, at.across_x, at.across_y))
+    ]
+    small_last = [
+        make(small_z_ref.at[at.z], small_z_ref.at[at.z], peer) for peer, _ in at.z_peers
+    ]
+
+    greet([at.partner, at.across_x, at.across_y] + [peer for peer, _ in at.z_peers])
+    for move in (down, up, out):
+        move.start()
+    fill_bias(scalars_ref, bias_ref, rows)
+
+    def share_one(g):
+        one[g].start()
+        two[g].start()
+
+    def share_two(g):
+        one[g].wait_recv()
+        add_rows(near_ref.at[0, g], dkv_ref.at[far, g], part)
+        three[g].start()
+
+    def share_three(g):
+        two[g].wait_recv()
+        three[g].wait_recv()
+        for half in range(2):
+            block = pl.ds(half * part, part)
+            to = pl.ds((1 + half) * width + g * part, part)
+            dqkv_ref[to, :] = (
+                near_ref[1, g, block, :].astype(F)
+                + dkv_ref[at.band, g, block, :].astype(F)
+                + far_ref[g, block, :].astype(F)
+            ).astype(BF)
+
+    events = {}
+
+    def when(j, *actions):
+        events.setdefault(j, []).extend(actions)
+
+    when(0, down.step_one)
+    when(1, lambda: share_one(0), up.step_one)
+    when(2, lambda: share_two(0))
+    when(3, lambda: share_one(1), down.step_two, out.step_one)
+    when(4, lambda: share_two(1))
+    when(5, lambda: share_one(2), down.step_three)
+    when(6, lambda: share_two(2), up.step_two)
+
+    @pl.loop(0, 2 * groups)
+    def _(j):
+        g, s = j // 2, j % 2
+        lanes = pl.ds(pl.multiple_of(s * rows, rows), rows)
+        for k in range(unroll):
+
+            def put_key(b, values):
+                dkv_ref[b, g, pl.ds(k * HEAD_DIM, HEAD_DIM), lanes] = values
+
+            def put_value(b, values):
+                dkv_ref[b, g, pl.ds(part + k * HEAD_DIM, HEAD_DIM), lanes] = values
+
+            attend_back_step(
+                s * HEADS + g * unroll + k,
+                at.x, q_ref, kv_ref, att_ref, lse_ref, datt_ref, bias_ref, dqkv_ref,
+                put_key, put_value,
             )
-        )
-
-    def rows_of(m, core):
-        rows = refs[m].shape[2] // 2
-        return pl.ds(pl.multiple_of(core * rows, 8), rows)
-
-    def lanes_of(m, x):
-        half_lanes = refs[m].shape[3] // 2
-        return pl.ds(pl.multiple_of(x * half_lanes, 128), half_lanes)
-
-    stage = [[] for _ in refs]
-    per = 6 + depth - 1
-    for m, ref in enumerate(refs):
-        stage[m].append(
-            [
-                send(
-                    ref.at[:, :, rows_of(m, 1 - c), :],
-                    one[m],
-                    send_sem.at[per * m],
-                    recv_sem.at[per * m],
-                    at.partner,
-                )
-            ]
-        )
-
-    def add(total, other):
-        total[...] = (total[...].astype(F) + other[...].astype(F)).astype(BF)
-
-    def first(m):
-        stage[m][0][0].wait_recv()
-
-        @pl.loop(0, images)
-        def _(j):
-            add(one[m].at[j // 2, j % 2], refs[m].at[j // 2, j % 2, rows_of(m, c), :])
-
-        stage[m].append(
-            [
-                send(
-                    one[m].at[pl.ds(0, near), :, :, lanes_of(m, 1 - at.x)],
-                    two_x[m],
-                    send_sem.at[per * m + 1],
-                    recv_sem.at[per * m + 1],
-                    at.across_x,
-                ),
-                send(
-                    one[m].at[pl.ds(near, depth - near), 1 - at.y],
-                    two_y[m],
-                    send_sem.at[per * m + 2],
-                    recv_sem.at[per * m + 2],
-                    at.across_y,
-                ),
-            ]
-        )
-
-    def second(m):
-        stage[m][1][0].wait_recv()
-
-        @pl.loop(0, 2 * near)
-        def _(j):
-            add(two_x[m].at[j // 2, j % 2], one[m].at[j // 2, j % 2, :, lanes_of(m, at.x)])
-
-        copies = [
-            send(
-                two_x[m].at[:, 1 - at.y],
-                three[m].at[pl.ds(0, near)],
-                send_sem.at[per * m + 3],
-                recv_sem.at[per * m + 3],
-                at.across_y,
-            )
-        ]
-        stage[m][1][1].wait_recv()
-
-        @pl.loop(0, depth - near)
-        def _(j):
-            add(two_y[m].at[j], one[m].at[near + j, at.y])
-
-        copies.append(
-            send(
-                two_y[m].at[:, :, lanes_of(m, 1 - at.x)],
-                three[m].at[pl.ds(near, depth - near)],
-                send_sem.at[per * m + 4],
-                recv_sem.at[per * m + 4],
-                at.across_x,
-            )
-        )
-        stage[m].append(copies)
-
-    def third(m):
-        for copy in stage[m][2]:
-            copy.wait_recv()
-
-        @pl.loop(0, near)
-        def _(j):
-            add(three[m].at[j], two_x[m].at[j, at.y])
-
-        @pl.loop(0, depth - near)
-        def _(j):
-            add(three[m].at[near + j], two_y[m].at[j, :, lanes_of(m, at.x)])
-
-        copies = []
-        for k in range(1, depth):
-            peer, z = at.along_z(k)
-            copies.append(
-                send(
-                    three[m].at[z],
-                    four[m].at[k - 1],
-                    send_sem.at[per * m + 5 + k],
-                    recv_sem.at[per * m + 5 + k],
-                    peer,
-                )
-            )
-        stage[m].append(copies)
-
-    width = narrow_ref.shape[2]
-    starts = {}
-    row = 0
-    for m in (3, 2, 1):
-        starts[m] = row
-        row += refs[m].shape[2] // 2
-
-    def fourth(m):
-        for copy in stage[m][3]:
-            copy.wait_recv()
-        total = three[m][at.z].astype(F)
-        for k in range(1, depth):
-            total = total + four[m][k - 1].astype(F)
-        if m == 0:
-            lanes = wide_ref.shape[2]
-            low, high = total[:, :lanes], total[:, lanes:]
-            wide_ref[c] = jnp.where(c == 0, low, high)
-            away_wide_ref[...] = jnp.where(c == 0, high, low)
-            source, target = away_wide_ref, wide_ref.at[c]
-        else:
-            rows = pl.ds(starts[m], total.shape[0])
-            low, high = total[:, :width], total[:, width:]
-            narrow_ref[c, rows, :] = jnp.where(c == 0, low, high)
-            away_ref[rows, :] = jnp.where(c == 0, high, low)
-            source, target = away_ref.at[rows, :], narrow_ref.at[c, rows, :]
-        stage[m].append(
-            [send(source, target, send_sem.at[per * m + 5], recv_sem.at[per * m + 5], at.partner)]
-        )
-
-    def small_one():
-        for copy in small_copies:
-            copy.wait_recv()
-        total = small_ref[at.img]
-        for k in range(1, images):
-            total = total + small_in[k - 1]
-        small_band[at.band] = total
-        copies = []
-        for k in range(1, bands):
-            slot = images - 2 + k
-            copies.append(
-                send(
-                    small_band.at[at.band],
-                    small_band.at[at.band],
-                    small_send.at[slot],
-                    small_recv.at[slot],
-                    mates[k - 1],
-                )
-            )
-        return copies
-
-    first(0)
-    first(1)
-    second(0)
-    first(2)
-    second(1)
-    third(0)
-    first(3)
-    second(2)
-    third(1)
-    fourth(0)
-    small_mates = small_one()
-    second(3)
-    third(2)
-    fourth(1)
-    third(3)
-    fourth(2)
-    fourth(3)
-    for copy in small_mates:
+        for when_j, actions in events.items():
+
+            @pl.when(j == when_j)
+            def _():
+                for action in actions:
+                    action()
+
+    share_one(groups - 1)
+    block = w_ref.shape[0] // images
+
+    def weight_grad(j):
+        piece = dqkv_ref[pl.ds(pl.multiple_of(j * block, 16), block), :]
+        g_qkv_ref[j // 2, j % 2] = dg(piece, h_ref[...], 1, 1).astype(BF)
+
+    early = width // block
+
+    @pl.loop(0, early)
+    def _(j):
+        weight_grad(j)
+
+    share_two(groups - 1)
+    out.step_two()
+    down.step_four()
+    for g in range(groups - 1):
+        share_three(g)
+    up.step_three()
+    share_three(groups - 1)
+
+    @pl.loop(early, images)
+    def _(j):
+        weight_grad(j)
+
+    qkv.start()
+    err_ref[...] = jnp.zeros_like(err_ref)
+
+    @pl.loop(0, images)
+    def _(j):
+        piece = pl.ds(pl.multiple_of(j * block, 16), block)
+        err_ref[...] += dg(w_ref[piece, :], dqkv_ref[piece, :], 0, 0)
+
+    out.step_three()
+    qkv.step_one()
+    normed, inverse = normalize(x_ref[...].astype(F))
+    err = err_ref[...]
+    small_ref[0] = sums_ref[...]
+    small_ref[0, 0:1] = row_sums(dqkv_ref[pl.ds(0, width), :])[:1]
+    small_ref[0, 1:2] = row_sums(dqkv_ref[pl.ds(2 * width, width), :])[:1]
+    small_ref[0, 4:5] = row_sums(err * normed)[:1]
+    small_ref[0, 5:6] = row_sums(err)[:1]
+    small_steps[0].start()
+    gx_ref[...] = (dmid_ref[...] + norm_back(err, normed, inverse, gain_ref[...])).astype(BF)
+    up.step_four()
+    small_steps[0].wait_recv()
+    small_ref[1] = small_ref[0] + small_in_ref[0]
+    small_steps[1].start()
+    qkv.step_two()
+    small_steps[1].wait_recv()
+    small_ref[2] = small_ref[1] + small_in_ref[1]
+    small_steps[2].start()
+    out.step_four()
+    small_steps[2].wait_recv()
+    small_z_ref[at.z] = small_ref[2] + small_in_ref[2]
+    for copy in small_last:
+        copy.start()
+    qkv.step_three()
+    for copy in small_last:
         copy.wait_recv()
-    total = small_band[0]
-    for k in range(1, bands):
-        total = total + small_band[k]
-    small_out_ref[...] = total
-    for m in range(count):
-        stage[m][4][0].wait_recv()
-        for copies in stage[m]:
-            for copy in copies:
-                copy.wait_send()
-    for copy in small_copies + small_mates:
+    total = small_z_ref[0]
+    for k in range(1, depth):
+        total = total + small_z_ref[k]
+    total_ref[...] = total
+    qkv.step_four()
+    for move in moves:
+        move.end()
+    for copy in one + two + three + small_steps + small_last:
         copy.wait_send()
 
 
-def scatter(images, bands, qkv, out, up, down, small):
+def back(images, bands, scalars, q, kv, att, lse, datt, x, h, dmid, w, gain, grads, sums):
     depth = images // 2
     near = depth // 2
-    refs = (down, up, out, qkv)
-    full = qkv.shape[3]
-    one, two_x, two_y, three, four = [], [], [], [], []
-    for ref in refs:
-        rows, lanes = ref.shape[2] // 2, ref.shape[3]
-        one.append(pltpu.VMEM((depth, 2, rows, lanes), BF))
-        two_x.append(pltpu.VMEM((near, 2, rows, lanes // 2), BF))
-        two_y.append(pltpu.VMEM((depth - near, rows, lanes), BF))
-        three.append(pltpu.VMEM((depth, rows, lanes // 2), BF))
-        four.append(pltpu.VMEM((depth - 1, rows, lanes // 2), BF))
-    rows = sum(ref.shape[2] // 2 for ref in refs[1:])
-    wide_rows, wide = down.shape[2] // 2, down.shape[3] // 4
-    count = len(refs) * (6 + depth)
-    smalls = images + bands - 2
+    width, tokens = x.shape
+    g_out, g_up, g_down = grads
+    groups = HEADS // 4
+    results, buffers = [], []
+    count = 0
+    for item in (g_down, g_up, g_out, w):
+        block, lanes = item.shape[0] // images // 2, item.shape[1]
+        results.append(shape((2, block, lanes // 4), F))
+        buffers += [
+            pltpu.VMEM((depth, 2, block, lanes), BF),
+            pltpu.VMEM((near, 2, block, lanes // 2), BF),
+            pltpu.VMEM((depth - near, block, lanes), BF),
+            pltpu.VMEM((depth, block, lanes // 2), BF),
+            pltpu.VMEM((depth - 1, block, lanes // 2), BF),
+            pltpu.VMEM((block, lanes // 4), F),
+        ]
+        count += 6 + depth - 1
+    count += 3 * groups + 3 + depth - 1
+    small = (SUM_ROWS, width)
     return pl.pallas_call(
-        functools.partial(scatter_kernel, images, bands),
-        name="scatter",
-        out_shape=(
-            shape((2, rows, full // 4), F),
-            shape((2, wide_rows, wide), F),
-            shape(small.shape[1:], F),
-        ),
-        in_specs=[VM] * 5,
-        out_specs=(VM, VM, VM),
-        scratch_shapes=one
-        + two_x
-        + two_y
-        + three
-        + four
-        + [
-            pltpu.VMEM((rows, full // 4), F),
-            pltpu.VMEM((wide_rows, wide), F),
-            pltpu.VMEM((images - 1,) + small.shape[1:], F),
-            pltpu.VMEM((bands,) + small.shape[1:], F),
-            pltpu.SemaphoreType.DMA((count,)),
-            pltpu.SemaphoreType.DMA((count,)),
-            pltpu.SemaphoreType.DMA((smalls,)),
-            pltpu.SemaphoreType.DMA((smalls,)),
-        ],
+        functools.partial(back_kernel, images, bands),
+        name="back",
+        out_shape=(shape(x.shape, BF), results[3], results[2], results[1], results[0], shape(small, F)),
+        in_specs=[SM] + [VM] * 14,
+        out_specs=(VM,) * 6,
+        scratch_shapes=[
+            pltpu.VMEM((8, tokens // 2), F),
+            pltpu.VMEM((3 * width, tokens), BF),
+            pltpu.VMEM((bands, groups, 2 * width // groups, tokens), BF),
+            pltpu.VMEM((2, groups, 2 * width // groups, tokens), BF),
+            pltpu.VMEM((groups, 2 * width // groups, tokens), BF),
+            pltpu.VMEM((depth, 2, w.shape[0] // images, width), BF),
+            pltpu.VMEM((width, tokens), F),
+            pltpu.VMEM((3,) + small, F),
+            pltpu.VMEM((3,) + small, F),
+            pltpu.VMEM((depth,) + small, F),
+        ]
+        + buffers
+        + [pltpu.SemaphoreType.DMA((count,)), pltpu.SemaphoreType.DMA((count,))],
         compiler_params=comm_params(3),
-    )(qkv, out, up, down, small)
+    )(scalars, q, kv, att, lse, datt, x, h, dmid, w, gain, g_out, g_up, g_down, sums)
 
 
 def pack_small(parts):
@@ -1028,36 +1102,20 @@
     q, kv = qkv[:width], qkv[width:]
     all_kv = share(images, bands, kv)
     att, lse = attend(scalars, q, all_kv)
-    out, dmid, datt, g_out, g_up, g_down, sum_up, sums_two = middle(
+    out, dmid, datt, g_out, g_up, g_down, sums = middle(
         x, cot, valid, att, full_out, full_up, full_down,
         c_out, c_gain_two, c_shift_two, c_up, c_down,
     )
-    dq, dkv = attend_back(scalars, q, all_kv, att, lse, datt)
-    dkv = unshare(images, dkv)
-    gx, g_qkv, sums_one = finish(x, h, dq, dkv, full_qkv, c_gain_one, dmid)
-
-    small_sums = [
-        jnp.concatenate([sums_one[0, 0], sums_one[1, 0]]),
-        sums_two[3, 0],
-        sum_up[0],
-        sums_two[0, 0],
-        sums_one[2, 0],
-        sums_one[3, 0],
-        sums_two[1, 0],
-        sums_two[2, 0],
-    ]
-    packed = pack_small([item.reshape(images, -1) for item in small_sums])
-    grads = (g_qkv, g_out, g_up, g_down)
     if direct:
-        grads = [item.reshape(images // 2, 2, -1, item.shape[1]) for item in grads]
-        narrow, wide, small = scatter(images, bands, *grads, packed)
-        matrices, start = [], 0
-        for w in widths:
-            part = narrow[:, start : start + w // 2].reshape(w, -1)
-            matrices.append(part.T)
-            start += w // 2
-        matrices.append(wide.reshape(-1, wide.shape[2]).T)
+        gx, *pieces, total = back(
+            images, bands, scalars, q, all_kv, att, lse, datt, x, h, dmid,
+            full_qkv, c_gain_one, (g_out, g_up, g_down), sums,
+        )
+        matrices = [item.reshape(-1, item.shape[2]).T for item in pieces]
     else:
+        dq, dkv = attend_back(scalars, q, all_kv, att, lse, datt)
+        dkv = unshare(images, dkv)
+        gx, g_qkv, sums_one = finish(x, h, dq, dkv, full_qkv, c_gain_one, dmid)
         matrices = [
             lax.psum_scatter(
                 lax.psum_scatter(item, "img", scatter_dimension=0, tiled=True),
@@ -1067,15 +1125,17 @@
             )
             .astype(F)
             .T
-            for item in grads
+            for item in (g_qkv, g_out, g_up, g_down)
         ]
-        small = lax.psum(lax.psum_scatter(packed, "img", scatter_dimension=0), "band")
-    return (
-        turn_back(out),
-        turn_back(gx),
-        *matrices,
-        *unpack_small(small[None], sizes),
-    )
+        total = lax.psum(sums + sums_one, ("img", "band"))
+    own_small = lax.axis_index("img")
+    flat = total.reshape(-1)
+    starts = [0, 2, UP_ROW, 3, 4, 5, 6, 7]
+    small = [
+        lax.dynamic_slice(flat, (start * width + own_small * size,), (size,))
+        for start, size in zip(starts, sizes)
+    ]
+    return (turn_back(out), turn_back(gx), *matrices, *small)
 
 
 def solution(mesh):

time: 450 us -> 381 us (0.85)
  Pallas kernels: 389 us -> 335 us
  local copies, waits for them, and re-layouts: 54 us -> 42.2 us
    pallas_call x4 -> x1, Pallas kernels: 191 us -> 136 us  [back(): pl.pallas_call(functools.partial(back_kernel, images, bands), name='back'...]
    slice x6 -> x0, local copies, waits for them, and re-layouts: 5.48 us -> none  [the longest x3 2.91 us: body(): part = narrow[:, start:start + w // 2].reshape(w, -1)]
where the time goes in v2:
time: 381 us; the launch traced here: 380 us
  Pallas kernels  335 us (88%)
  local copies, waits for them, and re-layouts  42.2 us (11%)
    pallas_call x1, Pallas kernels, back(): pl.pallas_call(functools.partial(back_kernel, images, bands), name='back'...  136 us
    pallas_call x1, Pallas kernels, gather(): pl.pallas_call(functools.partial(gather_kernel, images), name='gather', o...  89 us
    pallas_call x1, Pallas kernels, share(): pl.pallas_call(functools.partial(share_kernel, images), name='share', out...  40.6 us
    pallas_call x1, Pallas kernels, middle(): pl.pallas_call(middle_kernel, name='middle', out_shape=(shape(full, BF),...  37.8 us
    pallas_call x1, Pallas kernels, attend(): pl.pallas_call(functools.partial(attend_kernel, 4), name='attend', out_sh...  22.6 us
    another operation x6, local copies, waits for them, and re-layouts, body(): columns = [item[:, None] for item in unpack_small(small_all, sizes)]  8.89 us
    pallas_call x1, Pallas kernels, project(): pl.pallas_call(project_kernel, name='project', out_shape=(shape((width, t...  8.23 us

profile of v2, /device:TPU:0, one launch (start us, length us, event | category | flops | bytes accessed | tf_op | source)
XLA Modules:
  0.0 380.5 jit_solution(17789774608374026490)
XLA Ops:
  0.7 1.2 pad_add_fusion.scalars_ref
  1.9 1.0 copy.63
  2.9 1.0 copy.61
  4.0 0.9 copy.62
  4.9 0.8 pad_maximum_fusion.narrow_ref
  5.7 0.7 convert_element_type.40
  6.4 0.7 convert_element_type.38
  7.0 0.8 concatenate.15
  7.8 0.6 pad_convert_fusion
  8.5 89.0 %gather.1 = (bf16[4,2,288,768]{3,2,1,0:T(8,128)(2,1)}, bf16[4,2,96,768]{3,2,1,0:T(8,128)(2,1)}, bf16[4,2,384,768]{3,2,1,0:T(8,128)(2,1)}, bf16[4,2,96,3072]{3,2,1,0:T(8,128)(2,1)}, f32[8,16,128]{2,1,0:T(8,128)}) custom-call(bf16[2,384,192]{2,1,0:T(8,128)(2,1)} %pad_maximum_fusion.narrow_ref, bf16[96,768]{1,0:T(8,128)(2,1)} %bitcast.88, f32[16,128]{1,0:T(8,128)} %bitcast.94), custom_call_target="tpu_custom_call" | custom-call | tf_op jit(solution)/shard_map/gather/pallas_call | solution.py:581
  97.5 0.0 copy-start
  97.5 0.9 copy.85
  98.4 0.0 copy-start.6
  98.4 0.1 slice.45
  98.5 0.1 slice.47
  98.6 1.5 copy.66.bias_ref
  100.1 0.7 fusion.1
  100.8 1.0 broadcast_in_dim_reshape.33.gain_ref
  101.8 1.0 broadcast_in_dim_reshape.34.shift_ref
  102.8 0.0 copy-done.6
  102.8 0.0 copy-done
  102.8 1.3 copy.59
  104.2 1.1 copy.78
  105.2 8.2 %project.1 = (bf16[768,512]{1,0:T(8,128)(2,1)}, bf16[2304,512]{1,0:T(8,128)(2,1)}) custom-call(bf16[768,512]{1,0:T(8,128)(2,1)} %bitcast.61, bf16[2304,768]{1,0:T(8,128)(2,1)} %bitcast.59, f32[768,1]{1,0:T(8,128)} %broadcast_in_dim_reshape.33.gain_ref, f32[768,1]{1,0:T(8,128)} %broadcast_in_dim_reshape.34.shift_ref, f32[2304,1]{1,0:T(8,128)} %copy.66.bias_ref), custom_call_target="tpu_custom_call" | custom-call | tf_op jit(solution)/shard_map/project/pallas_call | solution.py:75
  113.4 2.7 slice.49.kv_ref
  116.1 40.6 %share.1.kv_ref = bf16[4,1536,512]{2,1,0:T(8,128)(2,1)} custom-call(bf16[1536,512]{1,0:T(8,128)(2,1)} %slice.49.kv_ref), custom_call_target="tpu_custom_call" | custom-call | tf_op jit(solution)/shard_map/share/pallas_call | solution.py:633
  156.7 2.1 slice.48.q_ref
  158.8 22.6 %attend.1 = (f32[768,512]{1,0:T(8,128)}, f32[32,256]{1,0:T(8,128)}) custom-call(s32[3]{0:T(128)} %pad_add_fusion.scalars_ref, bf16[768,512]{1,0:T(8,128)(2,1)} %slice.48.q_ref, bf16[4,1536,512]{2,1,0:T(8,128)(2,1)} %share.1.kv_ref), custom_call_target="tpu_custom_call" | custom-call | tf_op jit(solution)/shard_map/attend/pallas_call | solution.py:153
  181.4 1.7 broadcast_in_dim_reshape.35.bias_out_ref
  183.1 1.7 broadcast_in_dim_reshape.36.gain_ref
  184.9 1.7 broadcast_in_dim_reshape.37.shift_ref
  186.6 1.7 broadcast_in_dim_reshape.39.bias_down_ref
  188.3 0.8 slice_bitcast_fusion
  189.1 0.0 copy-start.9
  189.1 1.6 copy.83
  190.7 0.0 copy-done.1
  190.7 1.3 copy.60
  192.1 1.1 copy.79
  193.1 0.0 copy-done.9
  193.1 0.1 broadcast_bitcast_fusion
  193.2 0.6 copy.80
  193.8 37.8 %middle.1 = (bf16[768,512]{1,0:T(8,128)(2,1)}, f32[768,512]{1,0:T(8,128)}, bf16[768,512]{1,0:T(8,128)(2,1)}, bf16[768,768]{1,0:T(8,128)(2,1)}, bf16[3072,768]{1,...) custom-call(bf16[768,512]{1,0:T(8,128)(2,1)} %bitcast.62, bf16[768,512]{1,0:T(8,128)(2,1)} %bitcast.67, ...), custom_call_target="tpu_custom_call" | custom-call | tf_op jit(solution)/shard_map/middle/pallas_call | solution.py:314
  231.6 136.5 %back.1 = (bf16[768,512]{1,0:T(8,128)(2,1)}, f32[2,144,192]{2,1,0:T(8,128)}, f32[2,48,192]{2,1,0:T(8,128)}, f32[2,192,192]{2,1,0:T(8,128)}, f32[2,48,768]{2,1,0:T(8,128)}, /*index=5*/f32[16,768]{1,0:T(8,128)}) custom-call(s32[3]{0:T(128)} %pad_add_fusion.scalars_ref, bf16[768,512]{1,0:T(8,128)(2,1)} %slice.48.q_ref, bf16[4,1536,512]{2,1,0:T(8,128)(2,1)} %share.1.kv_ref, ...), custom_call_target="tpu_custom_call" | custom-call | tf_op jit(solution)/shard_map/back/pallas_call | solution.py:1006
  368.1 0.0 copy-start.5
  368.1 0.0 copy-start.3
  368.1 0.0 copy-start.8
  368.2 0.0 copy-start.7
  368.2 0.0 copy-start.2
  368.2 2.3 reshape.108
  370.5 2.3 copy.74
  372.8 0.0 copy-done.5
  372.8 0.9 copy.75
  373.7 0.0 copy-done.3
  373.7 0.9 copy.77
  374.6 0.0 copy-done.8
  374.6 0.6 fusion.3
  375.2 0.0 copy-done.7
  375.2 0.7 copy.76
  375.9 0.7 dynamic_slice.26
  376.6 0.6 dynamic_slice.24
  377.2 0.0 copy-done.2
  377.2 0.2 reshape.107
  377.4 2.3 copy.72
  379.7 0.7 copy.87
  (10 shorter events, 0.1 us)
Async XLA Ops:
  97.5 5.4 %copy-start = (bf16[1,256,2,768]{3,2,1,0:T(2,128)(2,1)S(1)}, bf16[1,256,2,768]{3,2,1,0:T(2,128)(2,1)}, u32[]{:S(2)}) copy-start(bf16[1,256,2,768]{3,2,1,0:T(2,128)(2,1)} %param.15) | copy-start | bytes 2359300
  98.4 4.4 %copy-start.6 = (f32[1,8,16,128]{3,1,2,0:T(8,128)}, f32[1,8,16,128]{3,1,2,0:T(8,128)S(1)}, u32[]{:S(2)}) copy-start(f32[1,8,16,128]{3,1,2,0:T(8,128)S(1)} %copy.85) | copy-start | bytes 196612
  181.4 9.3 %copy-start.1 = (bf16[1,256,2,768]{3,2,1,0:T(2,128)(2,1)S(1)}, bf16[1,256,2,768]{3,2,1,0:T(2,128)(2,1)}, u32[]{:S(2)}) copy-start(bf16[1,256,2,768]{3,2,1,0:T(2,128)(2,1)} %param.29) | copy-start | bytes 2359300
  189.1 4.1 %copy-start.9 = (s32[1,2]{1,0:T(1,128)S(1)}, s32[1,2]{1,0:T(1,128)}, u32[]{:S(2)}) copy-start(s32[1,2]{1,0:T(1,128)} %param.16) | copy-start | bytes 28
  368.1 4.7 %copy-start.5 = (f32[2,144,192]{2,1,0:T(8,128)S(1)}, f32[2,144,192]{2,1,0:T(8,128)}, u32[]{:S(2)}) copy-start(f32[2,144,192]{2,1,0:T(8,128)} %get-tuple-element.53) | copy-start | bytes 663556
  368.1 5.6 %copy-start.3 = (f32[2,192,192]{2,1,0:T(8,128)S(1)}, f32[2,192,192]{2,1,0:T(8,128)}, u32[]{:S(2)}) copy-start(f32[2,192,192]{2,1,0:T(8,128)} %get-tuple-element.55) | copy-start | bytes 884740
  368.1 6.4 %copy-start.8 = (f32[16,768]{1,0:T(8,128)S(1)}, f32[16,768]{1,0:T(8,128)}, u32[]{:S(2)}) copy-start(f32[16,768]{1,0:T(8,128)} %get-tuple-element.57) | copy-start | bytes 147460
  368.2 7.0 %copy-start.7 = (f32[2,48,192]{2,1,0:T(8,128)S(1)}, f32[2,48,192]{2,1,0:T(8,128)}, u32[]{:S(2)}) copy-start(f32[2,48,192]{2,1,0:T(8,128)} %get-tuple-element.54) | copy-start | bytes 221188
  368.2 9.1 %copy-start.2 = (bf16[768,512]{1,0:T(8,128)(2,1)S(1)}, bf16[768,512]{1,0:T(8,128)(2,1)}, u32[]{:S(2)}) copy-start(bf16[768,512]{1,0:T(8,128)(2,1)} %get-tuple-element.43) | copy-start | bytes 2359300
  372.8 6.9 %copy-start.4 = (f32[2,48,768]{2,1,0:T(8,128)S(1)}, f32[2,48,768]{2,1,0:T(8,128)}, u32[]{:S(2)}) copy-start(f32[2,48,768]{2,1,0:T(8,128)} %get-tuple-element.56) | copy-start | bytes 884740

commit v3 on v2

--- a/solution.py
+++ b/solution.py
@@ -20,6 +20,9 @@
 ANY = pl.BlockSpec(memory_space=pl.ANY)
 LIMIT = 67043328
 SUM_ROWS, UP_ROW = 16, 8
+COLUMNS = 10
+BIAS_OUT, BIAS_DOWN, GAIN_ONE, SHIFT_ONE, GAIN_TWO, SHIFT_TWO = (slice(k, k + 1) for k in range(6))
+GROUPS_OF_HEADS = 4
 
 
 def dg(left, right, left_dim, right_dim):
@@ -56,10 +59,10 @@
     return (f - mean_f - normed * mean_fn) * inverse
 
 
-def project_kernel(x_ref, w_ref, gain_ref, shift_ref, bias_ref, h_ref, qkv_ref):
+def project_kernel(x_ref, w_ref, cols_ref, bias_ref, h_ref, qkv_ref):
     width = x_ref.shape[0]
     normed, _ = normalize(x_ref[...].astype(F))
-    h_ref[...] = (normed * gain_ref[...] + shift_ref[...]).astype(BF)
+    h_ref[...] = (normed * cols_ref[:, GAIN_ONE] + cols_ref[:, SHIFT_ONE]).astype(BF)
     scale = 1.0 / math.sqrt(HEAD_DIM)
     step = 256
 
@@ -70,16 +73,16 @@
         qkv_ref[rows, :] = (out * jnp.where(j < width // step, scale, 1.0)).astype(BF)
 
 
-def project(x, w, gain, shift, bias):
+def project(x, w, cols, bias):
     width, tokens = x.shape
     return pl.pallas_call(
         project_kernel,
         name="project",
         out_shape=(shape((width, tokens), BF), shape((3 * width, tokens), BF)),
-        in_specs=[VM] * 5,
+        in_specs=[VM] * 4,
         out_specs=(VM, VM),
         compiler_params=pltpu.CompilerParams(vmem_limit_bytes=LIMIT),
-    )(x, w, gain, shift, bias)
+    )(x, w, cols, bias)
 
 
 def fill_bias(scalars_ref, bias_ref, rows):
@@ -124,7 +127,8 @@
     maximum = None
     for b in range(bands):
         other = jnp.where(chip_x == b // 2, 0, 1)
-        part = add_bias(dg(kv_ref[b, first, lanes], q, 0, 0), bias_ref, s, other)
+        keys, _ = kv_rows(kv_ref, b, i % HEADS)
+        part = add_bias(dg(keys[:, lanes], q, 0, 0), bias_ref, s, other)
         scores.append(part)
         top = jnp.max(part, axis=0, keepdims=True)
         maximum = top if maximum is None else jnp.maximum(maximum, top)
@@ -132,7 +136,8 @@
     for b in range(bands):
         weight = jnp.exp(scores[b] - maximum)
         total = total + jnp.sum(weight, axis=0, keepdims=True)
-        acc = acc + dg(kv_ref[b, second, lanes], weight.astype(BF), 1, 0)
+        _, values = kv_rows(kv_ref, b, i % HEADS)
+        acc = acc + dg(values[:, lanes], weight.astype(BF), 1, 0)
     out_ref[first, lanes] = acc / total
     lse_ref[pl.ds(i, 1), :] = maximum + jnp.log(total)
 
@@ -174,7 +179,7 @@
     dq = 0.0
     for b in range(bands):
         other = jnp.where(chip_x == b // 2, 0, 1)
-        k, v = kv_ref[b, first, lanes], kv_ref[b, second, lanes]
+        k, v = (ref[:, lanes] for ref in kv_rows(kv_ref, b, i % HEADS))
         scores = add_bias(dg(k, q, 0, 0), bias_ref, s, other)
         dweight = dg(v, dout, 0, 0)
         weight = jnp.exp(scores - lse)
@@ -212,7 +217,7 @@
     return pl.pallas_call(
         functools.partial(attend_back_kernel, 4),
         name="attend_back",
-        out_shape=(shape(q.shape, BF), shape(kv.shape, BF)),
+        out_shape=(shape(q.shape, BF), shape((kv.shape[0], 2 * q.shape[0], q.shape[1]), BF)),
         in_specs=[SM] + [VM] * 5,
         out_specs=(VM, VM),
         scratch_shapes=[pltpu.VMEM((8, q.shape[1] // 2), F)],
@@ -223,16 +228,13 @@
 def middle_kernel(
     x_ref,
     cot_ref,
-    valid_ref,
+    scalars_ref,
     att_ref,
     w_out_ref,
     w_up_ref,
     w_down_ref,
-    bias_out_ref,
-    gain_ref,
-    shift_ref,
+    cols_ref,
     bias_up_ref,
-    bias_down_ref,
     out_ref,
     dmid_ref,
     datt_ref,
@@ -252,6 +254,12 @@
     width, tokens = x_ref.shape
     hidden = w_up_ref.shape[0]
     step = 256
+    first_slot = lax.broadcasted_iota(jnp.int32, (1, tokens), 1) < tokens // 2
+    valid = jnp.where(
+        first_slot,
+        jnp.where(scalars_ref[0] > 0, 1.0, 0.0),
+        jnp.where(scalars_ref[1] > 0, 1.0, 0.0),
+    )
     attb_ref[...] = att_ref[...].astype(BF)
     sums_ref[...] = jnp.zeros_like(sums_ref)
 
@@ -260,14 +268,14 @@
         rows = pl.ds(pl.multiple_of(j * step, step), step)
         mid_ref[rows, :] = (
             dg(w_out_ref[rows, :], attb_ref[...], 1, 0)
-            + bias_out_ref[rows, :]
+            + cols_ref[rows, BIAS_OUT]
             + x_ref[rows, :].astype(F)
         )
 
     normed, inverse = normalize(mid_ref[...])
     norm_ref[...] = normed
-    h_ref[...] = (normed * gain_ref[...] + shift_ref[...]).astype(BF)
-    dmlp_ref[...] = (cot_ref[...].astype(F) * valid_ref[...]).astype(BF)
+    h_ref[...] = (normed * cols_ref[:, GAIN_TWO] + cols_ref[:, SHIFT_TWO]).astype(BF)
+    dmlp_ref[...] = (cot_ref[...].astype(F) * valid).astype(BF)
     mlp_ref[...] = jnp.zeros_like(mlp_ref)
     err_ref[...] = jnp.zeros_like(err_ref)
 
@@ -288,13 +296,13 @@
         sums_ref[pl.ds(UP_ROW + j // per, 1), lanes] = row_sums(dhid)[:1]
         err_ref[...] += dg(w_up_ref[rows, :], dhid, 0, 0)
 
-    out_ref[...] = ((mid_ref[...] + mlp_ref[...] + bias_down_ref[...]) * valid_ref[...]).astype(BF)
+    out_ref[...] = ((mid_ref[...] + mlp_ref[...] + cols_ref[:, BIAS_DOWN]) * valid).astype(BF)
     err = err_ref[...]
     sums_ref[3:4] = row_sums(dmlp_ref[...])[:1]
     sums_ref[6:7] = row_sums(err * norm_ref[...])[:1]
     sums_ref[7:8] = row_sums(err)[:1]
-    dmid = cot_ref[...].astype(F) * valid_ref[...] + norm_back(
-        err, norm_ref[...], inverse, gain_ref[...]
+    dmid = cot_ref[...].astype(F) * valid + norm_back(
+        err, norm_ref[...], inverse, cols_ref[:, GAIN_TWO]
     )
     dmid_ref[...] = dmid
     dbranch_ref[...] = dmid.astype(BF)
@@ -307,7 +315,7 @@
         g_out_ref[rows, :] = dg(dbranch_ref[rows, :], attb_ref[...], 1, 1).astype(BF)
 
 
-def middle(x, cot, valid, att, w_out, w_up, w_down, bias_out, gain, shift, bias_up, bias_down):
+def middle(x, cot, scalars, att, w_out, w_up, w_down, cols, bias_up):
     width, tokens = x.shape
     hidden = w_up.shape[0]
     full = (width, tokens)
@@ -323,7 +331,7 @@
             shape(w_down.shape, BF),
             shape((SUM_ROWS, width), F),
         ),
-        in_specs=[VM] * 12,
+        in_specs=[VM, VM, SM] + [VM] * 6,
         out_specs=tuple([VM] * 7),
         scratch_shapes=[
             pltpu.VMEM(full, F),
@@ -336,11 +344,11 @@
             pltpu.VMEM(full, BF),
         ],
         compiler_params=pltpu.CompilerParams(vmem_limit_bytes=LIMIT),
-    )(x, cot, valid, att, w_out, w_up, w_down, bias_out, gain, shift, bias_up, bias_down)
+    )(x, cot, scalars, att, w_out, w_up, w_down, cols, bias_up)
 
 
 def finish_kernel(
-    x_ref, h_ref, dq_ref, dkv_ref, w_ref, gain_ref, dmid_ref, gx_ref, g_ref, sums_ref, err_ref
+    x_ref, h_ref, dq_ref, dkv_ref, w_ref, cols_ref, dmid_ref, gx_ref, g_ref, sums_ref, err_ref
 ):
     width, tokens = x_ref.shape
     step = 256
@@ -362,10 +370,10 @@
     sums_ref[1:2] = row_sums(dkv_ref[pl.ds(width, width), :])[:1]
     sums_ref[4:5] = row_sums(err * normed)[:1]
     sums_ref[5:6] = row_sums(err)[:1]
-    gx_ref[...] = (dmid_ref[...] + norm_back(err, normed, inverse, gain_ref[...])).astype(BF)
-
-
-def finish(x, h, dq, dkv, w, gain, dmid):
+    gx_ref[...] = (dmid_ref[...] + norm_back(err, normed, inverse, cols_ref[:, GAIN_ONE])).astype(BF)
+
+
+def finish(x, h, dq, dkv, w, cols, dmid):
     width, tokens = x.shape
     return pl.pallas_call(
         finish_kernel,
@@ -375,7 +383,7 @@
         out_specs=(VM, VM, VM),
         scratch_shapes=[pltpu.VMEM(x.shape, F)],
         compiler_params=pltpu.CompilerParams(vmem_limit_bytes=LIMIT),
-    )(x, h, dq, dkv, w, gain, dmid)
+    )(x, h, dq, dkv, w, cols, dmid)
 
 
 class Place:
@@ -428,174 +436,287 @@
     )
 
 
-def gather_kernel(
-    images, narrow_ref, wide_ref, small_ref, qkv_ref, out_ref, up_ref, down_ref, smalls_ref,
-    theirs_ref, mine_ref, mine_wide_ref, local_sem, send_sem, recv_sem, small_send, small_recv,
+class Spread:
+    def __init__(self, at, make, order, source, ref, local_sem):
+        depth, near, c = at.depth, at.depth // 2, at.c
+        rows, half = ref.shape[2] // 2, ref.shape[3] // 2
+        rows = pl.ds(pl.multiple_of(c * rows, 16), rows)
+        lanes = pl.ds(pl.multiple_of(at.x * half, 128), half)
+        low, high = pl.ds(0, near), pl.ds(near, depth - near)
+
+        def same(part, peer):
+            return make(part, part, peer)
+
+        piece = ref.at[at.z, at.y, rows, lanes]
+        self.keep = pltpu.make_async_copy(source, piece, local_sem)
+        if order == "mixed":
+            self.stages = [
+                [make(source, piece, peer) for peer, _ in at.z_peers],
+                [
+                    same(ref.at[low, at.y, rows, lanes], at.across_x),
+                    same(ref.at[high, at.y, rows, lanes], at.across_y),
+                ],
+                [
+                    same(ref.at[low, at.y, rows, :], at.across_y),
+                    same(ref.at[high, :, rows, lanes], at.across_x),
+                ],
+            ]
+        elif order == "zxy":
+            self.stages = [
+                [make(source, piece, peer) for peer, _ in at.z_peers],
+                [same(ref.at[:, at.y, rows, lanes], at.across_x)],
+                [same(ref.at[:, at.y, rows, :], at.across_y)],
+            ]
+        else:
+            self.stages = [
+                [make(source, piece, at.across_x)],
+                [same(ref.at[at.z, at.y, rows, :], at.across_y)],
+                [same(ref.at[at.z, :, rows, :], peer) for peer, _ in at.z_peers],
+            ]
+        self.stages.append([same(ref.at[:, :, rows, :], at.partner)])
+
+    def start(self):
+        self.keep.start()
+        for copy in self.stages[0]:
+            copy.start()
+
+    def step(self, k):
+        if k == 1:
+            self.keep.wait()
+        for copy in self.stages[k - 1]:
+            copy.wait_recv()
+        for copy in self.stages[k]:
+            copy.start()
+
+    def wait(self):
+        for copy in self.stages[-1]:
+            copy.wait_recv()
+
+    def end(self):
+        for stage in self.stages:
+            for copy in stage:
+                copy.wait_send()
+
+
+def kv_rows(ref, b, h):
+    part = ref.shape[2] // 2
+    heads = part // HEAD_DIM
+    first = pl.multiple_of(h % heads * HEAD_DIM, 16)
+    second = pl.multiple_of(part + h % heads * HEAD_DIM, 16)
+    at = ref.at[b, h // heads]
+    return at.at[pl.ds(first, HEAD_DIM)], at.at[pl.ds(second, HEAD_DIM)]
+
+
+def front_kernel(
+    images, bands, scalars_ref, narrow_ref, wide_ref, small_ref, x_ref,
+    qkv_w_ref, out_w_ref, up_w_ref, down_w_ref, h_ref, q_ref, kv_ref, att_ref, lse_ref,
+    cols_ref, up_col_ref,
+    theirs_ref, mine_ref, mine_wide_ref, smalls_ref, qv_col_ref, bias_ref,
+    local_sem, send_sem, recv_sem,
 ):
     at = Place(images)
-    depth, near = at.depth, at.depth // 2
-    peers = [at.partner, at.across_x, at.across_y]
-    peers += [at.along_z(k)[0] for k in range(1, depth)]
+    width, tokens = x_ref.shape
+    rows = tokens // 2
+    unit = width // images
+    groups = kv_ref.shape[1]
+    part = width // groups
+    c = at.c
+    used = [0]
+
+    def make(src, dst, peer):
+        k = used[0]
+        used[0] += 1
+        return pltpu.make_async_remote_copy(
+            src_ref=src,
+            dst_ref=dst,
+            send_sem=send_sem.at[k],
+            recv_sem=recv_sem.at[k],
+            device_id=peer,
+            device_id_type=MESH,
+        )
+
     others = [(lax.rem(at.img + k, images), at.band) for k in range(1, images)]
-    others = peers[:2] + others
-    greet(others)
-    c = at.c
-
-    first = [
-        send(narrow_ref.at[1 - c], theirs_ref, send_sem.at[16], recv_sem.at[16], at.partner)
-    ]
     half = wide_ref.shape[0] // 2
     wide = wide_ref.shape[1]
-    lanes = pl.ds(pl.multiple_of(c * wide, 128), wide)
-    own = pltpu.make_async_copy(
+    own_lanes = pl.ds(pl.multiple_of(c * wide, 128), wide)
+    own_wide = pltpu.make_async_copy(
         wide_ref.at[pl.ds(pl.multiple_of(c * half, 8), half), :],
-        mine_wide_ref.at[:, lanes],
+        mine_wide_ref.at[:, own_lanes],
         local_sem.at[0],
     )
-    own.start()
-    first.append(
-        send(
-            wide_ref.at[pl.ds(pl.multiple_of((1 - c) * half, 8), half), :],
-            mine_wide_ref.at[:, lanes],
-            send_sem.at[17],
-            recv_sem.at[17],
-            at.partner,
-        )
+    swap = make(narrow_ref.at[1 - c], theirs_ref, at.partner)
+    swap_wide = make(
+        wide_ref.at[pl.ds(pl.multiple_of((1 - c) * half, 8), half), :],
+        mine_wide_ref.at[:, own_lanes],
+        at.partner,
     )
-    small_copies = []
-    keep = pltpu.make_async_copy(small_ref, smalls_ref.at[at.img], local_sem.at[1])
-    keep.start()
-    for k in range(1, images):
-        small_copies.append(
-            send(
-                small_ref,
-                smalls_ref.at[at.img],
-                small_send.at[k - 1],
-                small_recv.at[k - 1],
-                others[k + 1],
+    lines = pl.ds(pl.multiple_of(at.img * 16, 16), 16)
+    keep_small = pltpu.make_async_copy(small_ref, smalls_ref.at[lines, :], local_sem.at[1])
+    small_copies = [make(small_ref, smalls_ref.at[lines, :], peer) for peer in others]
+    refs = (qkv_w_ref, out_w_ref, up_w_ref, down_w_ref)
+    sources, row = [], 0
+    for ref in refs[:3]:
+        count = ref.shape[2] // 2
+        sources.append(mine_ref.at[pl.ds(row, count), :])
+        row += count
+    sources.append(mine_wide_ref)
+    orders = ("mixed", "zxy", "zxy", "xyz")
+    spreads = [
+        Spread(at, make, orders[m], sources[m], refs[m], local_sem.at[2 + m]) for m in range(4)
+    ]
+    s_qkv, s_out, s_up, s_down = spreads
+    mate = kv_ref.at[at.band]
+    far = kv_ref.at[at.across_x[1]]
+    to_x = [make(mate.at[g], mate.at[g], at.across_x) for g in range(groups)]
+    to_mate = [make(mate.at[g], mate.at[g], at.partner) for g in range(groups)]
+    passed = [make(far.at[g], far.at[g], at.partner) for g in range(groups)]
+
+    greet([at.partner, at.across_x] + others)
+    swap.start()
+    own_wide.start()
+    swap_wide.start()
+    keep_small.start()
+    for copy in small_copies:
+        copy.start()
+    fill_bias(scalars_ref, bias_ref, rows)
+    swap.wait_recv()
+    mine, theirs = narrow_ref[c], theirs_ref[...]
+    lane_count = mine.shape[1]
+    mine_ref[:, pl.ds(0, lane_count)] = jnp.where(c == 0, mine, theirs)
+    mine_ref[:, pl.ds(lane_count, lane_count)] = jnp.where(c == 0, theirs, mine)
+    s_qkv.start()
+    own_wide.wait()
+    swap_wide.wait_recv()
+    s_down.start()
+    s_up.start()
+    s_out.start()
+
+    keep_small.wait()
+    for copy in small_copies:
+        copy.wait_recv()
+    turned = smalls_ref[...].T
+    qv_units, up_units = 2, up_w_ref.shape[2] // unit
+    singles = 16 - qv_units - up_units
+    for j in range(images):
+        block = turned[:unit, 16 * j : 16 * j + 16]
+        cols_ref[pl.ds(unit * j, unit), :] = block[:, :singles]
+        for u in range(qv_units):
+            lane = singles + u
+            qv_col_ref[pl.ds(unit * (qv_units * j + u), unit), :] = block[:, lane : lane + 1]
+        for u in range(up_units):
+            lane = singles + qv_units + u
+            up_col_ref[pl.ds(unit * (up_units * j + u), unit), :] = block[:, lane : lane + 1]
+
+    s_down.step(1)
+    normed, _ = normalize(x_ref[...].astype(F))
+    h_ref[...] = (normed * cols_ref[:, GAIN_ONE] + cols_ref[:, SHIFT_ONE]).astype(BF)
+    s_qkv.step(1)
+    s_down.step(2)
+    s_qkv.step(2)
+    s_qkv.step(3)
+    s_qkv.wait()
+
+    weights = qkv_w_ref.reshape(3 * width, width)
+
+    def project(row):
+        return dg(weights[pl.ds(row, part), :], h_ref[...], 1, 0)
+
+    for g in range(groups):
+        kv_ref[at.band, g, pl.ds(0, part), :] = project(width + g * part).astype(BF)
+        value = project(2 * width + g * part) + qv_col_ref[pl.ds(width + g * part, part), :]
+        kv_ref[at.band, g, pl.ds(part, part), :] = value.astype(BF)
+        to_x[g].start()
+        to_mate[g].start()
+        if g == 0:
+            s_up.step(1)
+            s_out.step(1)
+    scale = 1.0 / math.sqrt(HEAD_DIM)
+    for g in range(groups):
+        block = pl.ds(g * part, part)
+        q_ref[block, :] = ((project(g * part) + qv_col_ref[block, :]) * scale).astype(BF)
+
+    def forward(g):
+        to_x[g].wait_recv()
+        passed[g].start()
+
+    def arrive(g):
+        to_mate[g].wait_recv()
+        passed[g].wait_recv()
+
+    events = {}
+
+    def when(j, *actions):
+        events.setdefault(j, []).extend(actions)
+
+    for g in range(1, groups):
+        when(2 * g - 2, functools.partial(forward, g))
+        when(2 * g - 1, functools.partial(arrive, g))
+    when(1, functools.partial(s_up.step, 2))
+    when(2, functools.partial(s_out.step, 2))
+    when(4, functools.partial(s_out.step, 3))
+    when(6, functools.partial(s_up.step, 3))
+    forward(0)
+    arrive(0)
+    unroll = HEADS // groups
+
+    @pl.loop(0, 2 * groups)
+    def _(j):
+        g, s = j // 2, j % 2
+        for k in range(unroll):
+            attend_step(
+                s * HEADS + g * unroll + k, at.x, q_ref, kv_ref, bias_ref, att_ref, lse_ref
             )
-        )
-    first[0].wait_recv()
-    mine, theirs = narrow_ref[c], theirs_ref[...]
-    width = mine.shape[1]
-    mine_ref[:, pl.ds(0, width)] = jnp.where(c == 0, mine, theirs)
-    mine_ref[:, pl.ds(width, width)] = jnp.where(c == 0, theirs, mine)
-    own.wait()
-    first[1].wait_recv()
-
-    refs = (qkv_ref, out_ref, up_ref, down_ref)
-    views, sources = [], []
-    row = 0
-    for ref in refs[:3]:
-        rows = ref.shape[2] // 2
-        sources.append(mine_ref.at[pl.ds(row, rows), :])
-        row += rows
-    sources.append(mine_wide_ref)
-
-    sends = list(first) + small_copies
-    stage = [[None] * 4 for _ in refs]
-    locals_ = [keep]
-
-    def rows_of(m):
-        rows = refs[m].shape[2] // 2
-        return pl.ds(pl.multiple_of(c * rows, 8), rows)
-
-    def lanes_of(m):
-        half_lanes = refs[m].shape[3] // 2
-        return pl.ds(pl.multiple_of(at.x * half_lanes, 128), half_lanes)
-
-    for m, ref in enumerate(refs):
-        piece = ref.at[at.z, at.y, rows_of(m), lanes_of(m)]
-        copy = pltpu.make_async_copy(sources[m], piece, local_sem.at[2 + m])
-        copy.start()
-        stage[m][0] = [copy]
-        for k in range(1, depth):
-            index = 18 + m * (depth - 1) + k - 1
-            stage[m][0].append(
-                send(sources[m], piece, send_sem.at[index], recv_sem.at[index], at.along_z(k)[0])
-            )
-
-    def second(m):
-        stage[m][0][0].wait()
-        for copy in stage[m][0][1:]:
-            copy.wait_recv()
-        region = (pl.ds(0, near), at.y, rows_of(m), lanes_of(m))
-        to_x = refs[m].at[region]
-        region = (pl.ds(near, depth - near), at.y, rows_of(m), lanes_of(m))
-        to_y = refs[m].at[region]
-        stage[m][1] = [
-            send(to_x, to_x, send_sem.at[4 * m], recv_sem.at[4 * m], at.across_x),
-            send(to_y, to_y, send_sem.at[4 * m + 1], recv_sem.at[4 * m + 1], at.across_y),
-        ]
-
-    def third(m):
-        for copy in stage[m][1]:
-            copy.wait_recv()
-        to_y = refs[m].at[pl.ds(0, near), at.y, rows_of(m), :]
-        to_x = refs[m].at[pl.ds(near, depth - near), :, rows_of(m), lanes_of(m)]
-        stage[m][2] = [
-            send(to_y, to_y, send_sem.at[4 * m + 2], recv_sem.at[4 * m + 2], at.across_y),
-            send(to_x, to_x, send_sem.at[4 * m + 3], recv_sem.at[4 * m + 3], at.across_x),
-        ]
-
-    last = 18 + 4 * (depth - 1)
-
-    def fourth(m):
-        for copy in stage[m][2]:
-            copy.wait_recv()
-        part = refs[m].at[:, :, rows_of(m), :]
-        stage[m][3] = [
-            send(part, part, send_sem.at[last + m], recv_sem.at[last + m], at.partner)
-        ]
-
-    second(0)
-    second(1)
-    third(0)
-    second(2)
-    third(1)
-    fourth(0)
-    second(3)
-    third(2)
-    fourth(1)
-    third(3)
-    fourth(2)
-    fourth(3)
-    for m in range(4):
-        stage[m][3][0].wait_recv()
-        for copy in stage[m][0][1:] + stage[m][1] + stage[m][2] + stage[m][3]:
-            copy.wait_send()
-    for copy in first:
+        for when_j, actions in events.items():
+
+            @pl.when(j == when_j)
+            def _():
+                for action in actions:
+                    action()
+
+    s_down.step(3)
+    for item in spreads[1:]:
+        item.wait()
+    for item in spreads:
+        item.end()
+    for copy in [swap, swap_wide] + small_copies + to_x + to_mate + passed:
         copy.wait_send()
-    for copy in small_copies:
-        copy.wait()
-    keep.wait()
-
-
-def gather(images, narrow, wide, small, widths):
+
+
+def front(images, bands, scalars, narrow, wide, small, x, widths):
     depth = images // 2
-    full = 4 * narrow.shape[2]
-    outs = [shape((depth, 2, w, full), BF) for w in widths]
-    outs.append(shape((depth, 2, wide.shape[0], 4 * wide.shape[1]), BF))
-    outs.append(shape((images,) + small.shape, F))
-    count = 18 + 4 * (depth - 1) + 4
+    width, tokens = x.shape
+    groups = GROUPS_OF_HEADS
+    hidden = images * widths[2]
+    count = 2 + images - 1 + 2 * (depth + 5) + 2 * (depth + 2) + 3 * groups
     return pl.pallas_call(
-        functools.partial(gather_kernel, images),
-        name="gather",
-        out_shape=tuple(outs),
-        in_specs=[VM, VM, VM],
-        out_specs=(ANY, ANY, ANY, ANY, VM),
+        functools.partial(front_kernel, images, bands),
+        name="front",
+        out_shape=tuple(shape((depth, 2, w, width), BF) for w in widths)
+        + (
+            shape((depth, 2, wide.shape[0], 4 * wide.shape[1]), BF),
+            shape((width, tokens), BF),
+            shape((width, tokens), BF),
+            shape((bands, groups, 2 * width // groups, tokens), BF),
+            shape((width, tokens), F),
+            shape((2 * HEADS, tokens // 2), F),
+            shape((width, COLUMNS), F),
+            shape((hidden, 1), F),
+        ),
+        in_specs=[SM] + [VM] * 4,
+        out_specs=(VM, ANY, ANY, ANY) + (VM,) * 7,
         scratch_shapes=[
             pltpu.VMEM(narrow.shape[1:], BF),
             pltpu.VMEM((narrow.shape[1], 2 * narrow.shape[2]), BF),
             pltpu.VMEM((wide.shape[0] // 2, 2 * wide.shape[1]), BF),
+            pltpu.VMEM((16 * images, 128), F),
+            pltpu.VMEM((2 * width, 1), F),
+            pltpu.VMEM((8, tokens // 2), F),
             pltpu.SemaphoreType.DMA((6,)),
             pltpu.SemaphoreType.DMA((count,)),
             pltpu.SemaphoreType.DMA((count,)),
-            pltpu.SemaphoreType.DMA((images - 1,)),
-            pltpu.SemaphoreType.DMA((images - 1,)),
         ],
         compiler_params=comm_params(0),
-    )(narrow, wide, small)
+    )(scalars, narrow, wide, small, x)
 
 
 def share_kernel(images, kv_ref, all_ref, local_sem, send_sem, recv_sem):
@@ -795,7 +916,7 @@
 
 def back_kernel(
     images, bands, scalars_ref, q_ref, kv_ref, att_ref, lse_ref, datt_ref, x_ref, h_ref, dmid_ref,
-    w_ref, gain_ref, g_out_ref, g_up_ref, g_down_ref, sums_ref,
+    w_ref, cols_ref, g_out_ref, g_up_ref, g_down_ref, sums_ref,
     gx_ref, p_qkv_ref, p_out_ref, p_up_ref, p_down_ref, total_ref,
     bias_ref, dqkv_ref, dkv_ref, near_ref, far_ref, g_qkv_ref, err_ref,
     small_ref, small_in_ref, small_z_ref, *rest,
@@ -953,7 +1074,7 @@
     small_ref[0, 4:5] = row_sums(err * normed)[:1]
     small_ref[0, 5:6] = row_sums(err)[:1]
     small_steps[0].start()
-    gx_ref[...] = (dmid_ref[...] + norm_back(err, normed, inverse, gain_ref[...])).astype(BF)
+    gx_ref[...] = (dmid_ref[...] + norm_back(err, normed, inverse, cols_ref[:, GAIN_ONE])).astype(BF)
     up.step_four()
     small_steps[0].wait_recv()
     small_ref[1] = small_ref[0] + small_in_ref[0]
@@ -981,7 +1102,7 @@
         copy.wait_send()
 
 
-def back(images, bands, scalars, q, kv, att, lse, datt, x, h, dmid, w, gain, grads, sums):
+def back(images, bands, scalars, q, kv, att, lse, datt, x, h, dmid, w, cols, grads, sums):
     depth = images // 2
     near = depth // 2
     width, tokens = x.shape
@@ -1024,24 +1145,7 @@
         + buffers
         + [pltpu.SemaphoreType.DMA((count,)), pltpu.SemaphoreType.DMA((count,))],
         compiler_params=comm_params(3),
-    )(scalars, q, kv, att, lse, datt, x, h, dmid, w, gain, g_out, g_up, g_down, sums)
-
-
-def pack_small(parts):
-    flat = jnp.concatenate([p.reshape(p.shape[0], -1).astype(F) for p in parts], axis=1)
-    size = flat.shape[1]
-    lines = -(-size // 1024) * 8
-    flat = jnp.pad(flat, ((0, 0), (0, lines * 128 - size)))
-    return flat.reshape(flat.shape[0], lines, 128)
-
-
-def unpack_small(packed, sizes):
-    flat = packed.reshape(packed.shape[0], -1)
-    pieces, start = [], 0
-    for size in sizes:
-        pieces.append(flat[:, start : start + size].reshape(-1))
-        start += size
-    return pieces
+    )(scalars, q, kv, att, lse, datt, x, h, dmid, w, cols, g_out, g_up, g_down, sums)
 
 
 def body(
@@ -1069,7 +1173,9 @@
     sizes = [item.shape[0] for item in smalls]
     own = (w_qkv, w_out, w_up)
     widths = [item.shape[1] for item in own]
-    direct = images % 4 == 0 and all(w % 16 == 0 for w in widths + [w_down.shape[1]])
+    direct = images % 4 == 0 and all(w % 32 == 0 for w in widths + [w_down.shape[1]])
+    direct = direct and bias_qv.shape[0] == 2 * (width // images) <= 256
+    direct = direct and bias_up.shape[0] == 4 * (width // images)
 
     def turn(values):
         return values[0].transpose(2, 1, 0).reshape(width, count)
@@ -1079,43 +1185,47 @@
 
     x, cot = turn(tokens), turn(cotangent)
     kinds = slot_kind[0].astype(jnp.int32)
-    valid = jnp.repeat((kinds > 0).astype(F), rows)[None, :]
     scalars = jnp.concatenate([kinds, (band // 2).astype(jnp.int32)[None]])
-
-    small = pack_small([item[None] for item in smalls])[0]
+    single = (bias_out, bias_down, gain_one, shift_one, gain_two, shift_two)
     if direct:
         narrow = split_rows([item.T for item in own], 2)
-        *full, small_all = gather(images, narrow, w_down.T, small, widths)
-        full = [item.reshape(-1, item.shape[3]) for item in full]
+        unit = width // images
+        units = [jnp.stack(single), jnp.zeros((4, unit), BF)]
+        units += [bias_qv.reshape(2, unit), bias_up.reshape(4, unit)]
+        small = jnp.pad(jnp.concatenate(units), ((0, 0), (0, 128 - unit))).astype(F)
+        *full, h, q, all_kv, att, lse, cols, c_up = front(
+            images, bands, scalars, narrow, w_down.T, small, x, widths
+        )
+        full_qkv, full_out, full_up, full_down = (item.reshape(-1, item.shape[3]) for item in full)
     else:
-        full = [
+        full_qkv, full_out, full_up, full_down = (
             lax.all_gather(lax.all_gather(item, "band", axis=0, tiled=True).T, "img", tiled=True)
             for item in (*own, w_down)
-        ]
-        small_all = lax.all_gather(small, "img")
-    full_qkv, full_out, full_up, full_down = full
-    columns = [item[:, None] for item in unpack_small(small_all, sizes)]
-    c_qv, c_out, c_up, c_down, c_gain_one, c_shift_one, c_gain_two, c_shift_two = columns
-    bias = jnp.concatenate([c_qv[:width], jnp.zeros((width, 1), F), c_qv[width:]])
-
-    h, qkv = project(x, full_qkv, c_gain_one, c_shift_one, bias)
-    q, kv = qkv[:width], qkv[width:]
-    all_kv = share(images, bands, kv)
-    att, lse = attend(scalars, q, all_kv)
+        )
+        whole = [lax.all_gather(item, "img", tiled=True).astype(F) for item in single]
+        cols = jnp.stack(whole + [whole[0]] * (COLUMNS - len(whole)), axis=1)
+        c_qv = lax.all_gather(bias_qv, "img", tiled=True).astype(F)[:, None]
+        c_up = lax.all_gather(bias_up, "img", tiled=True).astype(F)[:, None]
+        bias = jnp.concatenate([c_qv[:width], jnp.zeros((width, 1), F), c_qv[width:]])
+        h, qkv = project(x, full_qkv, cols, bias)
+        q = qkv[:width]
+        all_kv = share(images, bands, qkv[width:])
+        all_kv = all_kv.reshape(bands, 2, GROUPS_OF_HEADS, -1, count).transpose(0, 2, 1, 3, 4)
+        all_kv = all_kv.reshape(bands, GROUPS_OF_HEADS, -1, count)
+        att, lse = attend(scalars, q, all_kv)
     out, dmid, datt, g_out, g_up, g_down, sums = middle(
-        x, cot, valid, att, full_out, full_up, full_down,
-        c_out, c_gain_two, c_shift_two, c_up, c_down,
+        x, cot, scalars, att, full_out, full_up, full_down, cols, c_up
     )
     if direct:
         gx, *pieces, total = back(
             images, bands, scalars, q, all_kv, att, lse, datt, x, h, dmid,
-            full_qkv, c_gain_one, (g_out, g_up, g_down), sums,
+            full_qkv, cols, (g_out, g_up, g_down), sums,
         )
         matrices = [item.reshape(-1, item.shape[2]).T for item in pieces]
     else:
         dq, dkv = attend_back(scalars, q, all_kv, att, lse, datt)
         dkv = unshare(images, dkv)
-        gx, g_qkv, sums_one = finish(x, h, dq, dkv, full_qkv, c_gain_one, dmid)
+        gx, g_qkv, sums_one = finish(x, h, dq, dkv, full_qkv, cols, dmid)
         matrices = [
             lax.psum_scatter(
                 lax.psum_scatter(item, "img", scatter_dimension=0, tiled=True),

time: 381 us -> 337 us (0.88)
  Pallas kernels: 335 us -> 311 us
  local copies, waits for them, and re-layouts: 42.2 us -> 22.5 us
    pallas_call x4 -> x1, Pallas kernels: 160 us -> 137 us  [front(): pl.pallas_call(functools.partial(front_kernel, images, bands), name='fron...]
    another operation x6 -> x0, local copies, waits for them, and re-layouts: 8.89 us -> none  [body(): columns = [item[:, None] for item in unpack_small(small_all, sizes)]]
    slice x6 -> x0, local copies, waits for them, and re-layouts: 5.62 us -> none  [the longest x2 4.77 us: body(): q, kv = (qkv[:width], qkv[width:])]
    unnamed x29 -> x33, local copies, waits for them, and re-layouts: 6.9 us -> 2.88 us
where the time goes in v3:
time: 337 us
  Pallas kernels  311 us (92%)
  local copies, waits for them, and re-layouts  22.5 us (7%)
    pallas_call x1, Pallas kernels, front(): pl.pallas_call(functools.partial(front_kernel, images, bands), name='fron...  137 us
    pallas_call x1, Pallas kernels, back(): pl.pallas_call(functools.partial(back_kernel, images, bands), name='back'...  136 us
    pallas_call x1, Pallas kernels, middle(): pl.pallas_call(middle_kernel, name='middle', out_shape=(shape(full, BF),...  37.3 us
    reshape x4, local copies, waits for them, and re-layouts, turn_back(): return values.reshape(width, slots, rows).transpose(2, 1, 0)[None]  7.15 us

profile of v3, /device:TPU:0, one launch (start us, length us, event | category | flops | bytes accessed | tf_op | source)
XLA Modules:
  0.0 337.1 jit_solution(3213412215011531951)
XLA Ops:
  0.7 0.0 copy-start.3
  0.7 0.0 copy-start.5
  0.7 0.0 copy-start.7
  0.7 0.0 copy-start.14
  0.7 0.0 copy-start.8
  0.7 0.0 copy-start.9
  0.7 0.0 copy-start.10
  0.7 0.0 copy-start.11
  0.7 0.0 copy-start.12
  0.7 0.0 copy-start.13
  0.8 1.3 pad_add_fusion.scalars_ref
  2.1 2.8 copy.29
  4.9 1.1 copy.39
  5.9 1.0 copy.33
  7.0 0.0 copy-done.3
  7.0 0.1 copy.31
  7.1 0.0 copy-done.5
  7.1 0.1 copy.32
  7.2 0.8 pad_maximum_fusion.narrow_ref
  8.0 0.0 copy-done.7
  8.0 0.1 reshape.88
  8.1 0.0 copy-done.14
  8.1 0.1 reshape.87
  8.2 0.0 copy-done.8
  8.2 0.0 copy-done.9
  8.2 0.0 copy-done.10
  8.2 0.0 copy-done.11
  8.3 0.0 copy-done.12
  8.3 0.0 copy-done.13
  8.3 0.1 concatenate.11
  8.4 0.6 pad_convert_fusion.small_ref
  9.0 137.3 %front.1 = (bf16[4,2,288,768]{3,2,1,0:T(8,128)(2,1)}, bf16[4,2,96,768]{3,2,1,0:T(8,128)(2,1)}, bf16[4,2,384,768]{3,2,1,0:T(8,128)(2,1)}, bf16[4,2,96,3072]{3,2,1...) custom-call(s32[3]{0:T(128)} %pad_add_fusion.scalars_ref, ...), custom_call_target="tpu_custom_call" | custom-call | tf_op jit(solution)/shard_map/front/pallas_call | solution.py:691
  146.3 2.8 copy.30
  149.1 1.1 copy.40
  150.2 37.3 %middle.1 = (bf16[768,512]{1,0:T(8,128)(2,1)}, f32[768,512]{1,0:T(8,128)}, bf16[768,512]{1,0:T(8,128)(2,1)}, bf16[768,768]{1,0:T(8,128)(2,1)}, bf16[3072,768]{1,...) custom-call(bf16[768,512]{1,0:T(8,128)(2,1)} %bitcast.45, bf16[768,512]{1,0:T(8,128)(2,1)} %bitcast.50, ...), custom_call_target="tpu_custom_call" | custom-call | tf_op jit(solution)/shard_map/middle/pallas_call | solution.py:322
  187.5 136.3 %back.1 = (bf16[768,512]{1,0:T(8,128)(2,1)}, f32[2,144,192]{2,1,0:T(8,128)}, f32[2,48,192]{2,1,0:T(8,128)}, f32[2,192,192]{2,1,0:T(8,128)}, f32[2,48,768]{2,1,0:T(8,128)}, /*index=5*/f32[16,768]{1,0:T(8,128)}) custom-call(s32[3]{0:T(128)} %pad_add_fusion.scalars_ref, bf16[768,512]{1,0:T(8,128)(2,1)} %get-tuple-element.45.q_ref, ...), custom_call_target="tpu_custom_call" | custom-call | tf_op jit(solution)/shard_map/back/pallas_call | solution.py:1127
  323.8 0.0 copy-start.1
  323.8 0.0 copy-start.6
  323.8 0.0 copy-start.4
  323.8 0.0 copy-start
  323.9 2.3 reshape.94
  326.2 0.0 copy-start.2
  326.2 2.3 copy.35
  328.5 1.8 copy.36
  330.3 0.0 copy-done.1
  330.3 0.9 copy.38
  331.2 0.0 copy-done.6
  331.2 0.6 fusion
  331.8 0.0 copy-done.4
  331.8 0.7 copy.37
  332.6 0.7 dynamic_slice.26
  333.2 0.6 dynamic_slice.24
  333.8 0.0 copy-done
  333.9 0.2 reshape.92
  334.0 2.3 copy.34
  336.4 0.0 copy-done.2
  336.4 0.7 copy.42
  (2 shorter events, 0.0 us)
Async XLA Ops:
  0.7 6.3 %copy-start.3 = (bf16[192,288]{1,0:T(8,128)(2,1)S(1)}, bf16[192,288]{1,0:T(8,128)(2,1)}, u32[]{:S(2)}) copy-start(bf16[192,288]{1,0:T(8,128)(2,1)} %param.17) | copy-start | bytes 331780
  0.7 6.5 %copy-start.5 = (bf16[192,96]{1,0:T(8,128)(2,1)S(1)}, bf16[192,96]{1,0:T(8,128)(2,1)}, u32[]{:S(2)}) copy-start(bf16[192,96]{1,0:T(8,128)(2,1)} %param.18) | copy-start | bytes 110596
  0.7 7.4 %copy-start.7 = (bf16[384]{0:T(512)(128)(2,1)S(1)}, bf16[384]{0:T(512)(128)(2,1)}, u32[]{:S(2)}) copy-start(bf16[384]{0:T(512)(128)(2,1)} %param.23) | copy-start | bytes 2308
  0.7 7.5 %copy-start.14 = (bf16[192]{0:T(256)(128)(2,1)S(1)}, bf16[192]{0:T(256)(128)(2,1)}, u32[]{:S(2)}) copy-start(bf16[192]{0:T(256)(128)(2,1)} %param.21) | copy-start | bytes 1156
  0.7 7.5 %copy-start.8 = (bf16[96]{0:T(256)(128)(2,1)S(1)}, bf16[96]{0:T(256)(128)(2,1)}, u32[]{:S(2)}) copy-start(bf16[96]{0:T(256)(128)(2,1)} %param.22) | copy-start | bytes 580
  0.7 7.5 %copy-start.9 = (bf16[96]{0:T(256)(128)(2,1)S(1)}, bf16[96]{0:T(256)(128)(2,1)}, u32[]{:S(2)}) copy-start(bf16[96]{0:T(256)(128)(2,1)} %param.24) | copy-start | bytes 580
  0.7 7.5 %copy-start.10 = (bf16[96]{0:T(256)(128)(2,1)S(1)}, bf16[96]{0:T(256)(128)(2,1)}, u32[]{:S(2)}) copy-start(bf16[96]{0:T(256)(128)(2,1)} %param.25) | copy-start | bytes 580
  0.7 7.5 %copy-start.11 = (bf16[96]{0:T(256)(128)(2,1)S(1)}, bf16[96]{0:T(256)(128)(2,1)}, u32[]{:S(2)}) copy-start(bf16[96]{0:T(256)(128)(2,1)} %param.26) | copy-start | bytes 580
  0.7 7.5 %copy-start.12 = (bf16[96]{0:T(256)(128)(2,1)S(1)}, bf16[96]{0:T(256)(128)(2,1)}, u32[]{:S(2)}) copy-start(bf16[96]{0:T(256)(128)(2,1)} %param.27) | copy-start | bytes 580
  0.7 7.5 %copy-start.13 = (bf16[96]{0:T(256)(128)(2,1)S(1)}, bf16[96]{0:T(256)(128)(2,1)}, u32[]{:S(2)}) copy-start(bf16[96]{0:T(256)(128)(2,1)} %param.28) | copy-start | bytes 580
  323.8 6.5 %copy-start.1 = (f32[2,192,192]{2,1,0:T(8,128)S(1)}, f32[2,192,192]{2,1,0:T(8,128)}, u32[]{:S(2)}) copy-start(f32[2,192,192]{2,1,0:T(8,128)} %get-tuple-element.59) | copy-start | bytes 884740
  323.8 7.4 %copy-start.6 = (f32[16,768]{1,0:T(8,128)S(1)}, f32[16,768]{1,0:T(8,128)}, u32[]{:S(2)}) copy-start(f32[16,768]{1,0:T(8,128)} %get-tuple-element.61) | copy-start | bytes 147460
  323.8 8.0 %copy-start.4 = (f32[2,48,192]{2,1,0:T(8,128)S(1)}, f32[2,48,192]{2,1,0:T(8,128)}, u32[]{:S(2)}) copy-start(f32[2,48,192]{2,1,0:T(8,128)} %get-tuple-element.58) | copy-start | bytes 221188
  323.8 10.0 %copy-start = (bf16[768,512]{1,0:T(8,128)(2,1)S(1)}, bf16[768,512]{1,0:T(8,128)(2,1)}, u32[]{:S(2)}) copy-start(bf16[768,512]{1,0:T(8,128)(2,1)} %get-tuple-element.44) | copy-start | bytes 2359300
  326.2 10.2 %copy-start.2 = (f32[2,48,768]{2,1,0:T(8,128)S(1)}, f32[2,48,768]{2,1,0:T(8,128)}, u32[]{:S(2)}) copy-start(f32[2,48,768]{2,1,0:T(8,128)} %get-tuple-element.60) | copy-start | bytes 884740

commit v4 on v3

--- a/solution.py
+++ b/solution.py
@@ -23,6 +23,7 @@
 COLUMNS = 10
 BIAS_OUT, BIAS_DOWN, GAIN_ONE, SHIFT_ONE, GAIN_TWO, SHIFT_TWO = (slice(k, k + 1) for k in range(6))
 GROUPS_OF_HEADS = 4
+FRONT_COPIES, BACK_COPIES = 128, 128
 
 
 def dg(left, right, left_dim, right_dim):
@@ -167,14 +168,14 @@
 
 
 def attend_back_step(
-    i, chip_x, q_ref, kv_ref, out_ref, lse_ref, dout_ref, bias_ref, dq_ref, put_key, put_value
+    i, chip_x, q_ref, kv_ref, delta_ref, lse_ref, dout_ref, bias_ref, dq_ref, put_key, put_value
 ):
     bands = kv_ref.shape[0]
     rows = q_ref.shape[1] // 2
     s, lanes, first, second = head_slices(i, rows)
     q = q_ref[first, lanes]
     dout = dout_ref[first, lanes]
-    delta = jnp.sum(out_ref[first, lanes] * dout.astype(F), axis=0, keepdims=True)
+    delta = delta_ref[pl.ds(i % HEADS, 1), lanes]
     lse = lse_ref[pl.ds(i, 1), :]
     dq = 0.0
     for b in range(bands):
@@ -191,7 +192,7 @@
 
 
 def attend_back_kernel(
-    unroll, scalars_ref, q_ref, kv_ref, out_ref, lse_ref, dout_ref, dq_ref, dkv_ref, bias_ref
+    unroll, scalars_ref, q_ref, kv_ref, delta_ref, lse_ref, dout_ref, dq_ref, dkv_ref, bias_ref
 ):
     fill_bias(scalars_ref, bias_ref, q_ref.shape[1] // 2)
 
@@ -208,12 +209,12 @@
                 dkv_ref[b, second, lanes] = values
 
             attend_back_step(
-                i, scalars_ref[2], q_ref, kv_ref, out_ref, lse_ref, dout_ref, bias_ref, dq_ref,
+                i, scalars_ref[2], q_ref, kv_ref, delta_ref, lse_ref, dout_ref, bias_ref, dq_ref,
                 put_key, put_value,
             )
 
 
-def attend_back(scalars, q, kv, out, lse, dout):
+def attend_back(scalars, q, kv, delta, lse, dout):
     return pl.pallas_call(
         functools.partial(attend_back_kernel, 4),
         name="attend_back",
@@ -222,7 +223,7 @@
         out_specs=(VM, VM),
         scratch_shapes=[pltpu.VMEM((8, q.shape[1] // 2), F)],
         compiler_params=pltpu.CompilerParams(vmem_limit_bytes=LIMIT),
-    )(scalars, q, kv, out, lse, dout)
+    )(scalars, q, kv, delta, lse, dout)
 
 
 def middle_kernel(
@@ -238,6 +239,7 @@
     out_ref,
     dmid_ref,
     datt_ref,
+    delta_ref,
     g_out_ref,
     g_up_ref,
     g_down_ref,
@@ -308,6 +310,8 @@
     dbranch_ref[...] = dmid.astype(BF)
     sums_ref[2:3] = row_sums(dbranch_ref[...])[:1]
     datt_ref[...] = dg(w_out_ref[...], dbranch_ref[...], 0, 0).astype(BF)
+    inner = att_ref[...] * datt_ref[...].astype(F)
+    delta_ref[...] = jnp.sum(inner.reshape(HEADS, width // HEADS, tokens), axis=1)
 
     @pl.loop(0, width // step)
     def _(j):
@@ -326,13 +330,14 @@
             shape(full, BF),
             shape(full, F),
             shape(full, BF),
+            shape((HEADS, tokens), F),
             shape(w_out.shape, BF),
             shape(w_up.shape, BF),
             shape(w_down.shape, BF),
             shape((SUM_ROWS, width), F),
         ),
         in_specs=[VM, VM, SM] + [VM] * 6,
-        out_specs=tuple([VM] * 7),
+        out_specs=tuple([VM] * 8),
         scratch_shapes=[
             pltpu.VMEM(full, F),
             pltpu.VMEM(full, F),
@@ -437,43 +442,48 @@
 
 
 class Spread:
-    def __init__(self, at, make, order, source, ref, local_sem):
+    def __init__(self, at, make, order, part, parts, source, ref, local_sem):
         depth, near, c = at.depth, at.depth // 2, at.c
         rows, half = ref.shape[2] // 2, ref.shape[3] // 2
         rows = pl.ds(pl.multiple_of(c * rows, 16), rows)
-        lanes = pl.ds(pl.multiple_of(at.x * half, 128), half)
+        size = half // parts
+        lanes = pl.ds(pl.multiple_of(at.x * half + part * size, 128), size)
+        both = [pl.ds(x * half + part * size, size) for x in range(2)]
+        if parts == 1:
+            both = [slice(None)]
         low, high = pl.ds(0, near), pl.ds(near, depth - near)
 
-        def same(part, peer):
-            return make(part, part, peer)
+        def same(index, peer):
+            if len(index) == 4:
+                return [make(ref.at[index], ref.at[index], peer)]
+            return [make(ref.at[index + (l,)], ref.at[index + (l,)], peer) for l in both]
 
         piece = ref.at[at.z, at.y, rows, lanes]
+        source = source.at[:, pl.ds(part * size, size)]
         self.keep = pltpu.make_async_copy(source, piece, local_sem)
+        z_first = [make(source, piece, peer) for peer, _ in at.z_peers]
         if order == "mixed":
             self.stages = [
-                [make(source, piece, peer) for peer, _ in at.z_peers],
-                [
-                    same(ref.at[low, at.y, rows, lanes], at.across_x),
-                    same(ref.at[high, at.y, rows, lanes], at.across_y),
-                ],
-                [
-                    same(ref.at[low, at.y, rows, :], at.across_y),
-                    same(ref.at[high, :, rows, lanes], at.across_x),
-                ],
+                z_first,
+                same((low, at.y, rows, lanes), at.across_x)
+                + same((high, at.y, rows, lanes), at.across_y),
+                same((low, at.y, rows), at.across_y)
+                + same((high, slice(None), rows, lanes), at.across_x),
             ]
         elif order == "zxy":
             self.stages = [
-                [make(source, piece, peer) for peer, _ in at.z_peers],
-                [same(ref.at[:, at.y, rows, lanes], at.across_x)],
-                [same(ref.at[:, at.y, rows, :], at.across_y)],
+                z_first,
+                same((slice(None), at.y, rows, lanes), at.across_x),
+                same((slice(None), at.y, rows), at.across_y),
             ]
         else:
+            last = [same((at.z, slice(None), rows), peer) for peer, _ in at.z_peers]
             self.stages = [
                 [make(source, piece, at.across_x)],
-                [same(ref.at[at.z, at.y, rows, :], at.across_y)],
-                [same(ref.at[at.z, :, rows, :], peer) for peer, _ in at.z_peers],
+                same((at.z, at.y, rows), at.across_y),
+                sum(last, []),
             ]
-        self.stages.append([same(ref.at[:, :, rows, :], at.partner)])
+        self.stages.append(same((slice(None), slice(None), rows), at.partner))
 
     def start(self):
         self.keep.start()
@@ -511,7 +521,7 @@
     images, bands, scalars_ref, narrow_ref, wide_ref, small_ref, x_ref,
     qkv_w_ref, out_w_ref, up_w_ref, down_w_ref, h_ref, q_ref, kv_ref, att_ref, lse_ref,
     cols_ref, up_col_ref,
-    theirs_ref, mine_ref, mine_wide_ref, smalls_ref, qv_col_ref, bias_ref,
+    theirs_ref, mine_ref, mine_wide_ref, smalls_ref, qv_col_ref, bias_ref, x_far_ref,
     local_sem, send_sem, recv_sem,
 ):
     at = Place(images)
@@ -521,7 +531,7 @@
     groups = kv_ref.shape[1]
     part = width // groups
     c = at.c
-    used = [0]
+    used = [0, 0]
 
     def make(src, dst, peer):
         k = used[0]
@@ -535,6 +545,10 @@
             device_id_type=MESH,
         )
 
+    def local():
+        used[1] += 1
+        return local_sem.at[used[1] - 1]
+
     others = [(lax.rem(at.img + k, images), at.band) for k in range(1, images)]
     half = wide_ref.shape[0] // 2
     wide = wide_ref.shape[1]
@@ -542,7 +556,7 @@
     own_wide = pltpu.make_async_copy(
         wide_ref.at[pl.ds(pl.multiple_of(c * half, 8), half), :],
         mine_wide_ref.at[:, own_lanes],
-        local_sem.at[0],
+        local(),
     )
     swap = make(narrow_ref.at[1 - c], theirs_ref, at.partner)
     swap_wide = make(
@@ -551,28 +565,42 @@
         at.partner,
     )
     lines = pl.ds(pl.multiple_of(at.img * 16, 16), 16)
-    keep_small = pltpu.make_async_copy(small_ref, smalls_ref.at[lines, :], local_sem.at[1])
+    keep_small = pltpu.make_async_copy(small_ref, smalls_ref.at[lines, :], local())
     small_copies = [make(small_ref, smalls_ref.at[lines, :], peer) for peer in others]
-    refs = (qkv_w_ref, out_w_ref, up_w_ref, down_w_ref)
     sources, row = [], 0
-    for ref in refs[:3]:
+    for ref in (qkv_w_ref, out_w_ref, up_w_ref):
         count = ref.shape[2] // 2
         sources.append(mine_ref.at[pl.ds(row, count), :])
         row += count
     sources.append(mine_wide_ref)
-    orders = ("mixed", "zxy", "zxy", "xyz")
-    spreads = [
-        Spread(at, make, orders[m], sources[m], refs[m], local_sem.at[2 + m]) for m in range(4)
+
+    def spread(ref, source, orders):
+        parts = len(orders)
+        return [
+            Spread(at, make, orders[k], k, parts, source, ref, local()) for k in range(parts)
+        ]
+
+    s_qkv = spread(qkv_w_ref, sources[0], ("mixed",) * 3)
+    (s_out,) = spread(out_w_ref, sources[1], ("mixed",))
+    s_up = spread(up_w_ref, sources[2], ("mixed", "zxy", "zxy"))
+    d_one, d_two = spread(down_w_ref, sources[3], ("xyz", "mixed"))
+    x_lanes = [pl.ds(s * rows, rows) for s in range(2)]
+    x_moves = [make(x_ref.at[:, l], x_far_ref.at[:, l], at.across_x) for l in x_lanes]
+    far = at.across_x[1]
+    kv_moves = [
+        [
+            [
+                make(kv_ref.at[b, g, :, x_lanes[s]], kv_ref.at[b, g, :, x_lanes[s]], at.partner)
+                for b in (at.band, far)
+            ]
+            for g in range(groups)
+        ]
+        for s in range(2)
     ]
-    s_qkv, s_out, s_up, s_down = spreads
-    mate = kv_ref.at[at.band]
-    far = kv_ref.at[at.across_x[1]]
-    to_x = [make(mate.at[g], mate.at[g], at.across_x) for g in range(groups)]
-    to_mate = [make(mate.at[g], mate.at[g], at.partner) for g in range(groups)]
-    passed = [make(far.at[g], far.at[g], at.partner) for g in range(groups)]
 
     greet([at.partner, at.across_x] + others)
     swap.start()
+    x_moves[0].start()
     own_wide.start()
     swap_wide.start()
     keep_small.start()
@@ -584,11 +612,14 @@
     lane_count = mine.shape[1]
     mine_ref[:, pl.ds(0, lane_count)] = jnp.where(c == 0, mine, theirs)
     mine_ref[:, pl.ds(lane_count, lane_count)] = jnp.where(c == 0, theirs, mine)
-    s_qkv.start()
+    for item in s_qkv:
+        item.start()
     own_wide.wait()
     swap_wide.wait_recv()
-    s_down.start()
-    s_up.start()
+    d_one.start()
+    for item in s_up:
+        item.start()
+    d_two.start()
     s_out.start()
 
     keep_small.wait()
@@ -607,61 +638,84 @@
             lane = singles + qv_units + u
             up_col_ref[pl.ds(unit * (up_units * j + u), unit), :] = block[:, lane : lane + 1]
 
-    s_down.step(1)
-    normed, _ = normalize(x_ref[...].astype(F))
-    h_ref[...] = (normed * cols_ref[:, GAIN_ONE] + cols_ref[:, SHIFT_ONE]).astype(BF)
-    s_qkv.step(1)
-    s_down.step(2)
-    s_qkv.step(2)
-    s_qkv.step(3)
-    s_qkv.wait()
+    def first_norm(s, ref, side):
+        normed, _ = normalize(ref[:, x_lanes[s]].astype(F))
+        to = pl.ds(side * tokens + s * rows, rows)
+        h_ref[:, to] = (normed * cols_ref[:, GAIN_ONE] + cols_ref[:, SHIFT_ONE]).astype(BF)
+
+    s_qkv[0].step(1)
+    s_qkv[1].step(1)
+    d_one.step(1)
+    s_qkv[0].step(2)
+    s_qkv[2].step(1)
+    for s in range(2):
+        first_norm(s, x_ref, 0)
+    s_qkv[1].step(2)
+    d_one.step(2)
+    s_qkv[0].step(3)
+    s_qkv[2].step(2)
+    x_moves[1].start()
+    x_moves[0].wait_recv()
+    first_norm(0, x_far_ref, 1)
+    s_qkv[1].step(3)
+    s_qkv[2].step(3)
+    s_up[0].step(1)
+    s_up[1].step(1)
+    for item in s_qkv:
+        item.wait()
 
     weights = qkv_w_ref.reshape(3 * width, width)
-
-    def project(row):
-        return dg(weights[pl.ds(row, part), :], h_ref[...], 1, 0)
-
-    for g in range(groups):
-        kv_ref[at.band, g, pl.ds(0, part), :] = project(width + g * part).astype(BF)
-        value = project(2 * width + g * part) + qv_col_ref[pl.ds(width + g * part, part), :]
-        kv_ref[at.band, g, pl.ds(part, part), :] = value.astype(BF)
-        to_x[g].start()
-        to_mate[g].start()
-        if g == 0:
-            s_up.step(1)
-            s_out.step(1)
     scale = 1.0 / math.sqrt(HEAD_DIM)
-    for g in range(groups):
-        block = pl.ds(g * part, part)
-        q_ref[block, :] = ((project(g * part) + qv_col_ref[block, :]) * scale).astype(BF)
-
-    def forward(g):
-        to_x[g].wait_recv()
-        passed[g].start()
-
-    def arrive(g):
-        to_mate[g].wait_recv()
-        passed[g].wait_recv()
+
+    def project(s):
+        for g in range(groups):
+            for k in range(2):
+                row = (1 + k) * width + g * part
+                to = pl.ds(k * part, part)
+                for side, band in enumerate((at.band, far)):
+                    lanes = pl.ds(side * tokens + s * rows, rows)
+                    out = dg(weights[pl.ds(row, part), :], h_ref[:, lanes], 1, 0)
+                    if k == 1:
+                        out = out + qv_col_ref[pl.ds(width + g * part, part), :]
+                    kv_ref[band, g, to, x_lanes[s]] = out.astype(BF)
+            for copy in kv_moves[s][g]:
+                copy.start()
+        for g in range(groups):
+            block = pl.ds(g * part, part)
+            out = dg(weights[block, :], h_ref[:, x_lanes[s]], 1, 0) + qv_col_ref[block, :]
+            q_ref[block, x_lanes[s]] = (out * scale).astype(BF)
+
+    def second_slot():
+        x_moves[1].wait_recv()
+        first_norm(1, x_far_ref, 1)
+        project(1)
+
+    def arrive(s, g):
+        for copy in kv_moves[s][g]:
+            copy.wait_recv()
 
     events = {}
 
     def when(j, *actions):
         events.setdefault(j, []).extend(actions)
 
-    for g in range(1, groups):
-        when(2 * g - 2, functools.partial(forward, g))
-        when(2 * g - 1, functools.partial(arrive, g))
-    when(1, functools.partial(s_up.step, 2))
-    when(2, functools.partial(s_out.step, 2))
-    when(4, functools.partial(s_out.step, 3))
-    when(6, functools.partial(s_up.step, 3))
-    forward(0)
-    arrive(0)
+    when(1, functools.partial(s_up[2].step, 1))
+    when(2, second_slot)
+    for j in range(1, 2 * groups):
+        when(j - 1, functools.partial(arrive, j // groups, j % groups))
+    when(1, functools.partial(s_up[0].step, 2))
+    when(2, functools.partial(d_two.step, 1), functools.partial(s_out.step, 1))
+    when(4, functools.partial(s_up[1].step, 2))
+    when(5, functools.partial(s_up[2].step, 2))
+    when(6, functools.partial(s_up[0].step, 3), functools.partial(s_out.step, 2))
+    when(7, functools.partial(d_two.step, 2), functools.partial(s_up[1].step, 3))
+    project(0)
+    arrive(0, 0)
     unroll = HEADS // groups
 
     @pl.loop(0, 2 * groups)
     def _(j):
-        g, s = j // 2, j % 2
+        s, g = j // groups, j % groups
         for k in range(unroll):
             attend_step(
                 s * HEADS + g * unroll + k, at.x, q_ref, kv_ref, bias_ref, att_ref, lse_ref
@@ -673,12 +727,17 @@
                 for action in actions:
                     action()
 
-    s_down.step(3)
-    for item in spreads[1:]:
+    s_up[2].step(3)
+    s_out.step(3)
+    d_two.step(3)
+    d_one.step(3)
+    for item in s_up + [s_out, d_one, d_two]:
         item.wait()
-    for item in spreads:
+    for item in s_qkv + s_up + [s_out, d_one, d_two]:
         item.end()
-    for copy in [swap, swap_wide] + small_copies + to_x + to_mate + passed:
+    for copy in [swap, swap_wide] + small_copies + x_moves:
+        copy.wait_send()
+    for copy in sum(sum(kv_moves, []), []):
         copy.wait_send()
 
 
@@ -687,14 +746,13 @@
     width, tokens = x.shape
     groups = GROUPS_OF_HEADS
     hidden = images * widths[2]
-    count = 2 + images - 1 + 2 * (depth + 5) + 2 * (depth + 2) + 3 * groups
     return pl.pallas_call(
         functools.partial(front_kernel, images, bands),
         name="front",
         out_shape=tuple(shape((depth, 2, w, width), BF) for w in widths)
         + (
             shape((depth, 2, wide.shape[0], 4 * wide.shape[1]), BF),
-            shape((width, tokens), BF),
+            shape((width, 2 * tokens), BF),
             shape((width, tokens), BF),
             shape((bands, groups, 2 * width // groups, tokens), BF),
             shape((width, tokens), F),
@@ -711,9 +769,10 @@
             pltpu.VMEM((16 * images, 128), F),
             pltpu.VMEM((2 * width, 1), F),
             pltpu.VMEM((8, tokens // 2), F),
-            pltpu.SemaphoreType.DMA((6,)),
-            pltpu.SemaphoreType.DMA((count,)),
-            pltpu.SemaphoreType.DMA((count,)),
+            pltpu.VMEM((width, tokens), BF),
+            pltpu.SemaphoreType.DMA((16,)),
+            pltpu.SemaphoreType.DMA((FRONT_COPIES,)),
+            pltpu.SemaphoreType.DMA((FRONT_COPIES,)),
         ],
         compiler_params=comm_params(0),
     )(scalars, narrow, wide, small, x)
@@ -817,80 +876,109 @@
 
 
 class Reduction:
-    def __init__(self, at, make, ref, bufs, target, away):
-        one, two_x, two_y, three, four = bufs
-        self.at, self.ref, self.one, self.two_x, self.two_y = at, ref, one, two_x, two_y
-        self.three, self.four, self.target, self.away = three, four, target, away
+    def __init__(self, at, make, order, part, parts, ref, one, bufs, total):
         depth, near, c = at.depth, at.depth // 2, at.c
-        self.near = near
         rows, half = ref.shape[2] // 2, ref.shape[3] // 2
+        size = half // parts
+        self.at, self.near, self.ref, self.one, self.order = at, near, ref, one, order
+        self.rows = pl.ds(pl.multiple_of(c * rows, 16), rows)
 
         def lanes_of(x):
-            return pl.ds(pl.multiple_of(x * half, 128), half)
-
-        self.rows = pl.ds(pl.multiple_of(c * rows, 16), rows)
-        self.lanes = lanes_of(at.x)
-        far_rows = pl.ds(pl.multiple_of((1 - c) * rows, 16), rows)
-        far_lanes = lanes_of(1 - at.x)
+            return pl.ds(pl.multiple_of(x * half + part * size, 128), size)
+
+        self.lanes, self.both = lanes_of(at.x), [lanes_of(x) for x in range(2)]
+        self.total = total.at[:, pl.ds(part * size, size)]
+        far = lanes_of(1 - at.x)
         upper = depth - near
-        self.zero = make(ref.at[:, :, far_rows, :], one, at.partner)
-        self.first = [
-            make(one.at[pl.ds(0, near), :, :, far_lanes], two_x, at.across_x),
-            make(one.at[pl.ds(near, upper), 1 - at.y], two_y, at.across_y),
-        ]
-        self.second = [
-            make(two_x.at[:, 1 - at.y], three.at[pl.ds(0, near)], at.across_y),
-            make(two_y.at[:, :, far_lanes], three.at[pl.ds(near, upper)], at.across_x),
-        ]
+        if order == "mixed":
+            two_x, two_y, three, four = bufs
+            self.two_x, self.two_y = two_x, two_y
+            low, high = pl.ds(0, near), pl.ds(near, upper)
+            self.first = [make(one.at[low, :, :, far], two_x, at.across_x)] + [
+                make(one.at[high, 1 - at.y, :, self.both[x]], two_y.at[x], at.across_y)
+                for x in range(2)
+            ]
+            self.second = [
+                make(two_x.at[:, 1 - at.y], three.at[low], at.across_y),
+                make(two_y.at[1 - at.x], three.at[high], at.across_x),
+            ]
+        else:
+            two, three, four = bufs
+            self.two = two
+            self.first = [
+                make(one.at[:, 1 - at.y, :, self.both[x]], two.at[x], at.across_y)
+                for x in range(2)
+            ]
+            self.second = [make(two.at[1 - at.x], three, at.across_x)]
+        self.three, self.four = three, four
         self.third = [
             make(three.at[z], four.at[k], peer) for k, (peer, z) in enumerate(at.z_peers)
         ]
-        self.last = make(away, target.at[c], at.partner)
-
-    def start(self):
-        self.zero.start()
 
     def step_one(self):
-        self.zero.wait_recv()
-
-        @pl.loop(0, self.ref.shape[0] * 2)
-        def _(j):
-            accumulate(
-                self.one.at[j // 2, j % 2], self.ref.at[j // 2, j % 2, self.rows, :]
-            )
+        for lanes in self.both:
+
+            @pl.loop(0, 2 * self.at.depth)
+            def _(j):
+                accumulate(
+                    self.one.at[j // 2, j % 2, :, lanes],
+                    self.ref.at[j // 2, j % 2, self.rows, lanes],
+                )
 
         for copy in self.first:
             copy.start()
 
     def step_two(self):
-        self.first[0].wait_recv()
-
-        @pl.loop(0, 2 * self.near)
-        def _(j):
-            accumulate(
-                self.two_x.at[j // 2, j % 2], self.one.at[j // 2, j % 2, :, self.lanes]
-            )
-
-        self.second[0].start()
-        self.first[1].wait_recv()
-
-        @pl.loop(0, self.at.depth - self.near)
-        def _(j):
-            accumulate(self.two_y.at[j], self.one.at[self.near + j, self.at.y])
-
-        self.second[1].start()
+        at = self.at
+        if self.order == "mixed":
+            self.first[0].wait_recv()
+
+            @pl.loop(0, 2 * self.near)
+            def _(j):
+                accumulate(
+                    self.two_x.at[j // 2, j % 2], self.one.at[j // 2, j % 2, :, self.lanes]
+                )
+
+            self.second[0].start()
+            for x in range(2):
+                self.first[1 + x].wait_recv()
+
+                @pl.loop(0, at.depth - self.near)
+                def _(j):
+                    accumulate(
+                        self.two_y.at[x, j], self.one.at[self.near + j, at.y, :, self.both[x]]
+                    )
+
+            self.second[1].start()
+        else:
+            for x in range(2):
+                self.first[x].wait_recv()
+
+                @pl.loop(0, at.depth)
+                def _(j):
+                    accumulate(self.two.at[x, j], self.one.at[j, at.y, :, self.both[x]])
+
+            self.second[0].start()
 
     def step_three(self):
+        at = self.at
         for copy in self.second:
             copy.wait_recv()
-
-        @pl.loop(0, self.near)
-        def _(j):
-            accumulate(self.three.at[j], self.two_x.at[j, self.at.y])
-
-        @pl.loop(0, self.at.depth - self.near)
-        def _(j):
-            accumulate(self.three.at[self.near + j], self.two_y.at[j, :, self.lanes])
+        if self.order == "mixed":
+
+            @pl.loop(0, self.near)
+            def _(j):
+                accumulate(self.three.at[j], self.two_x.at[j, at.y])
+
+            @pl.loop(0, at.depth - self.near)
+            def _(j):
+                accumulate(self.three.at[self.near + j], self.two_y.at[at.x, j])
+
+        else:
+
+            @pl.loop(0, at.depth)
+            def _(j):
+                accumulate(self.three.at[j], self.two.at[at.x, j])
 
         for copy in self.third:
             copy.start()
@@ -898,32 +986,39 @@
     def step_four(self):
         for copy in self.third:
             copy.wait_recv()
-        c = self.at.c
         total = self.three[self.at.z].astype(F)
         for k in range(len(self.third)):
             total = total + self.four[k].astype(F)
-        size = total.shape[1] // 2
-        low, high = total[:, :size], total[:, size:]
-        self.target[c] = jnp.where(c == 0, low, high)
-        self.away[...] = jnp.where(c == 0, high, low)
-        self.last.start()
+        self.total[...] = total
 
     def end(self):
-        self.last.wait()
-        for copy in [self.zero] + self.first + self.second + self.third:
+        for copy in self.first + self.second + self.third:
             copy.wait_send()
 
 
+def reduction_buffers(order, depth, rows, size):
+    near = depth // 2
+    if order == "mixed":
+        first = [(near, 2, rows, size), (2, depth - near, rows, size)]
+    else:
+        first = [(2, depth, rows, size)]
+    return [pltpu.VMEM(s, BF) for s in first + [(depth, rows, size), (depth - 1, rows, size)]]
+
+
+BACK_ORDERS = (("mixed",) * 2, ("mixed",) * 3, ("mixed",), ("yx",) * 3)
+
+
 def back_kernel(
-    images, bands, scalars_ref, q_ref, kv_ref, att_ref, lse_ref, datt_ref, x_ref, h_ref, dmid_ref,
+    images, bands, scalars_ref, q_ref, kv_ref, delta_ref, lse_ref, datt_ref, x_ref, h_ref, dmid_ref,
     w_ref, cols_ref, g_out_ref, g_up_ref, g_down_ref, sums_ref,
     gx_ref, p_qkv_ref, p_out_ref, p_up_ref, p_down_ref, total_ref,
-    bias_ref, dqkv_ref, dkv_ref, near_ref, far_ref, g_qkv_ref, err_ref,
+    bias_ref, dq_ref, dwide_ref, dkv_ref, near_ref, g_qkv_ref, err_ref, err_far_ref, err_in_ref,
     small_ref, small_in_ref, small_z_ref, *rest,
 ):
     at = Place(images)
     depth = at.depth
     send_sem, recv_sem = rest[-2:]
+    rest = list(rest[:-2])
     used = [0]
 
     def make(src, dst, peer):
@@ -949,17 +1044,40 @@
 
     sources = (four_d(g_down_ref), four_d(g_up_ref), four_d(g_out_ref), g_qkv_ref)
     targets = (p_down_ref, p_up_ref, p_out_ref, p_qkv_ref)
-    moves = []
+    swaps, moves, ends = [], [], []
     for m in range(4):
-        moves.append(
-            Reduction(at, make, sources[m], rest[6 * m : 6 * m + 5], targets[m], rest[6 * m + 5])
-        )
+        one, total, away = rest[:3]
+        rest = rest[3:]
+        block = sources[m].shape[2] // 2
+        far_rows = pl.ds(pl.multiple_of((1 - at.c) * block, 16), block)
+        swaps.append(make(sources[m].at[:, :, far_rows, :], one, at.partner))
+        orders = BACK_ORDERS[m]
+        moves.append([])
+        for k, order in enumerate(orders):
+            size = 4 if order == "mixed" else 3
+            moves[m].append(
+                Reduction(
+                    at, make, order, k, len(orders), sources[m], one, rest[:size], total
+                )
+            )
+            rest = rest[size:]
+        ends.append((total, away, targets[m], make(away, targets[m].at[at.c], at.partner)))
     down, up, out, qkv = moves
+
+    def deliver(m):
+        total_ref, away, target, copy = ends[m]
+        total = total_ref[...]
+        size = total.shape[1] // 2
+        low, high = total[:, :size], total[:, size:]
+        target[at.c] = jnp.where(at.c == 0, low, high)
+        away[...] = jnp.where(at.c == 0, high, low)
+        copy.start()
+
     mate, far = at.partner[1], at.across_x[1]
     far_mate = at.across_x[1] + 1 - 2 * at.c
     one = [make(dkv_ref.at[far_mate, g], near_ref.at[0, g], at.partner) for g in range(groups)]
     two = [make(dkv_ref.at[mate, g], near_ref.at[1, g], at.partner) for g in range(groups)]
-    three = [make(near_ref.at[0, g], far_ref.at[g], at.across_x) for g in range(groups)]
+    err_moves = [make(err_far_ref.at[s], err_in_ref.at[s], at.across_x) for s in range(2)]
     small_steps = [
         make(small_ref.at[k], small_in_ref.at[k], peer)
         for k, peer in enumerate((at.partner, at.across_x, at.across_y))
@@ -969,43 +1087,41 @@
     ]
 
     greet([at.partner, at.across_x, at.across_y] + [peer for peer, _ in at.z_peers])
-    for move in (down, up, out):
-        move.start()
+    for m in range(3):
+        swaps[m].start()
     fill_bias(scalars_ref, bias_ref, rows)
+
+    sides = [pl.ds(side * tokens, tokens) for side in range(2)]
 
     def share_one(g):
         one[g].start()
         two[g].start()
 
     def share_two(g):
-        one[g].wait_recv()
-        add_rows(near_ref.at[0, g], dkv_ref.at[far, g], part)
-        three[g].start()
-
-    def share_three(g):
-        two[g].wait_recv()
-        three[g].wait_recv()
-        for half in range(2):
-            block = pl.ds(half * part, part)
-            to = pl.ds((1 + half) * width + g * part, part)
-            dqkv_ref[to, :] = (
-                near_ref[1, g, block, :].astype(F)
-                + dkv_ref[at.band, g, block, :].astype(F)
-                + far_ref[g, block, :].astype(F)
-            ).astype(BF)
+        for copy, side, band in ((one[g], 1, far), (two[g], 0, at.band)):
+            copy.wait_recv()
+            for half in range(2):
+                block = pl.ds(half * part, part)
+                to = pl.ds(half * width + g * part, part)
+                value = (
+                    near_ref[1 - side, g, block, :].astype(F)
+                    + dkv_ref[band, g, block, :].astype(F)
+                ).astype(BF)
+                dwide_ref[to, sides[side]] = value
 
     events = {}
 
     def when(j, *actions):
         events.setdefault(j, []).extend(actions)
 
-    when(0, down.step_one)
-    when(1, lambda: share_one(0), up.step_one)
-    when(2, lambda: share_two(0))
-    when(3, lambda: share_one(1), down.step_two, out.step_one)
-    when(4, lambda: share_two(1))
-    when(5, lambda: share_one(2), down.step_three)
-    when(6, lambda: share_two(2), up.step_two)
+    when(0, swaps[0].wait_recv, down[0].step_one, down[1].step_one)
+    when(1, swaps[1].wait_recv, up[0].step_one, up[1].step_one, lambda: share_one(0))
+    when(2, up[2].step_one, down[0].step_two, lambda: share_two(0))
+    when(3, swaps[2].wait_recv, out[0].step_one, down[1].step_two, lambda: share_one(1))
+    when(4, up[0].step_two, down[0].step_three, lambda: share_two(1))
+    when(5, up[1].step_two, down[1].step_three, lambda: share_one(2))
+    when(6, up[2].step_two, up[0].step_three, lambda: share_two(2))
+    when(7, lambda: share_one(3), out[0].step_two, up[1].step_three)
 
     @pl.loop(0, 2 * groups)
     def _(j):
@@ -1021,7 +1137,7 @@
 
             attend_back_step(
                 s * HEADS + g * unroll + k,
-                at.x, q_ref, kv_ref, att_ref, lse_ref, datt_ref, bias_ref, dqkv_ref,
+                at.x, q_ref, kv_ref, delta_ref, lse_ref, datt_ref, bias_ref, dq_ref,
                 put_key, put_value,
             )
         for when_j, actions in events.items():
@@ -1031,98 +1147,127 @@
                 for action in actions:
                     action()
 
-    share_one(groups - 1)
-    block = w_ref.shape[0] // images
-
-    def weight_grad(j):
-        piece = dqkv_ref[pl.ds(pl.multiple_of(j * block, 16), block), :]
-        g_qkv_ref[j // 2, j % 2] = dg(piece, h_ref[...], 1, 1).astype(BF)
-
-    early = width // block
-
-    @pl.loop(0, early)
+    chunk = width // 2
+    g_flat = g_qkv_ref.reshape(3 * width, width)
+
+    @pl.loop(0, 2)
     def _(j):
-        weight_grad(j)
+        block = pl.ds(pl.multiple_of(j * chunk, 128), chunk)
+        g_flat[block, :] = dg(dq_ref[block, :], h_ref[:, sides[0]], 1, 1).astype(BF)
 
     share_two(groups - 1)
-    out.step_two()
-    down.step_four()
-    for g in range(groups - 1):
-        share_three(g)
-    up.step_three()
-    share_three(groups - 1)
-
-    @pl.loop(early, images)
+
+    @pl.loop(0, 4)
     def _(j):
-        weight_grad(j)
-
-    qkv.start()
-    err_ref[...] = jnp.zeros_like(err_ref)
-
-    @pl.loop(0, images)
+        block = pl.ds(pl.multiple_of(j * chunk, 128), chunk)
+        to = pl.ds(pl.multiple_of((2 + j) * chunk, 128), chunk)
+        g_flat[to, :] = dg(dwide_ref[block, :], h_ref[...], 1, 1).astype(BF)
+
+    swaps[3].start()
+    up[2].step_three()
+    out[0].step_three()
+
+    def back_through(side):
+        err_ref[...] = jnp.zeros_like(err_ref)
+
+        @pl.loop(0, 4)
+        def _(j):
+            block = pl.ds(pl.multiple_of(j * chunk, 128), chunk)
+            source = pl.ds(pl.multiple_of((2 + j) * chunk, 128), chunk)
+            err_ref[...] += dg(w_ref[source, :], dwide_ref[block, sides[side]], 0, 0)
+
+    back_through(1)
+    swaps[3].wait_recv()
+    for item in qkv:
+        item.step_one()
+    for s in range(2):
+        err_far_ref[s] = err_ref[:, pl.ds(s * rows, rows)].astype(BF)
+        err_moves[s].start()
+    back_through(0)
+
+    @pl.loop(0, 2)
     def _(j):
-        piece = pl.ds(pl.multiple_of(j * block, 16), block)
-        err_ref[...] += dg(w_ref[piece, :], dqkv_ref[piece, :], 0, 0)
-
-    out.step_three()
-    qkv.step_one()
-    normed, inverse = normalize(x_ref[...].astype(F))
-    err = err_ref[...]
+        block = pl.ds(pl.multiple_of(j * chunk, 128), chunk)
+        err_ref[...] += dg(w_ref[block, :], dq_ref[block, :], 0, 0)
+
+    for item in down:
+        item.step_four()
+    deliver(0)
+    qkv[0].step_two()
+    up[0].step_four()
+    up[1].step_four()
+    qkv[1].step_two()
+    up[2].step_four()
+    deliver(1)
+    qkv[0].step_three()
+    qkv[2].step_two()
+    out[0].step_four()
+    deliver(2)
+    qkv[1].step_three()
     small_ref[0] = sums_ref[...]
-    small_ref[0, 0:1] = row_sums(dqkv_ref[pl.ds(0, width), :])[:1]
-    small_ref[0, 1:2] = row_sums(dqkv_ref[pl.ds(2 * width, width), :])[:1]
-    small_ref[0, 4:5] = row_sums(err * normed)[:1]
-    small_ref[0, 5:6] = row_sums(err)[:1]
+    small_ref[0, 0:1] = row_sums(dq_ref[...])[:1]
+    small_ref[0, 1:2] = row_sums(dwide_ref[pl.ds(width, width), :])[:1]
+    gain_row, shift_row = 0.0, 0.0
+    for s in range(2):
+        err_moves[s].wait_recv()
+        lanes = slice(s * rows, (s + 1) * rows)
+        err = err_ref[:, lanes] + err_in_ref[s].astype(F)
+        normed, inverse = normalize(x_ref[:, lanes].astype(F))
+        gain_row = gain_row + row_sums(err * normed)[:1]
+        shift_row = shift_row + row_sums(err)[:1]
+        gx_ref[:, lanes] = (
+            dmid_ref[:, lanes] + norm_back(err, normed, inverse, cols_ref[:, GAIN_ONE])
+        ).astype(BF)
+    small_ref[0, 4:5] = gain_row
+    small_ref[0, 5:6] = shift_row
     small_steps[0].start()
-    gx_ref[...] = (dmid_ref[...] + norm_back(err, normed, inverse, cols_ref[:, GAIN_ONE])).astype(BF)
-    up.step_four()
+    qkv[2].step_three()
     small_steps[0].wait_recv()
     small_ref[1] = small_ref[0] + small_in_ref[0]
     small_steps[1].start()
-    qkv.step_two()
+    qkv[0].step_four()
     small_steps[1].wait_recv()
     small_ref[2] = small_ref[1] + small_in_ref[1]
     small_steps[2].start()
-    out.step_four()
+    qkv[1].step_four()
     small_steps[2].wait_recv()
     small_z_ref[at.z] = small_ref[2] + small_in_ref[2]
     for copy in small_last:
         copy.start()
-    qkv.step_three()
+    qkv[2].step_four()
+    deliver(3)
     for copy in small_last:
         copy.wait_recv()
     total = small_z_ref[0]
     for k in range(1, depth):
         total = total + small_z_ref[k]
     total_ref[...] = total
-    qkv.step_four()
-    for move in moves:
-        move.end()
-    for copy in one + two + three + small_steps + small_last:
+    for m in range(4):
+        ends[m][3].wait()
+        swaps[m].wait_send()
+        for item in moves[m]:
+            item.end()
+    for copy in one + two + err_moves + small_steps + small_last:
         copy.wait_send()
 
 
-def back(images, bands, scalars, q, kv, att, lse, datt, x, h, dmid, w, cols, grads, sums):
+def back(images, bands, scalars, q, kv, delta, lse, datt, x, h, dmid, w, cols, grads, sums):
     depth = images // 2
-    near = depth // 2
     width, tokens = x.shape
     g_out, g_up, g_down = grads
     groups = HEADS // 4
     results, buffers = [], []
-    count = 0
-    for item in (g_down, g_up, g_out, w):
+    for m, item in enumerate((g_down, g_up, g_out, w)):
         block, lanes = item.shape[0] // images // 2, item.shape[1]
         results.append(shape((2, block, lanes // 4), F))
         buffers += [
             pltpu.VMEM((depth, 2, block, lanes), BF),
-            pltpu.VMEM((near, 2, block, lanes // 2), BF),
-            pltpu.VMEM((depth - near, block, lanes), BF),
-            pltpu.VMEM((depth, block, lanes // 2), BF),
-            pltpu.VMEM((depth - 1, block, lanes // 2), BF),
+            pltpu.VMEM((block, lanes // 2), F),
             pltpu.VMEM((block, lanes // 4), F),
         ]
-        count += 6 + depth - 1
-    count += 3 * groups + 3 + depth - 1
+        orders = BACK_ORDERS[m]
+        for order in orders:
+            buffers += reduction_buffers(order, depth, block, lanes // 2 // len(orders))
     small = (SUM_ROWS, width)
     return pl.pallas_call(
         functools.partial(back_kernel, images, bands),
@@ -1132,20 +1277,22 @@
         out_specs=(VM,) * 6,
         scratch_shapes=[
             pltpu.VMEM((8, tokens // 2), F),
-            pltpu.VMEM((3 * width, tokens), BF),
+            pltpu.VMEM((width, tokens), BF),
+            pltpu.VMEM((2 * width, 2 * tokens), BF),
             pltpu.VMEM((bands, groups, 2 * width // groups, tokens), BF),
             pltpu.VMEM((2, groups, 2 * width // groups, tokens), BF),
-            pltpu.VMEM((groups, 2 * width // groups, tokens), BF),
             pltpu.VMEM((depth, 2, w.shape[0] // images, width), BF),
             pltpu.VMEM((width, tokens), F),
+            pltpu.VMEM((2, width, tokens // 2), BF),
+            pltpu.VMEM((2, width, tokens // 2), BF),
             pltpu.VMEM((3,) + small, F),
             pltpu.VMEM((3,) + small, F),
             pltpu.VMEM((depth,) + small, F),
         ]
         + buffers
-        + [pltpu.SemaphoreType.DMA((count,)), pltpu.SemaphoreType.DMA((count,))],
+        + [pltpu.SemaphoreType.DMA((BACK_COPIES,)), pltpu.SemaphoreType.DMA((BACK_COPIES,))],
         compiler_params=comm_params(3),
-    )(scalars, q, kv, att, lse, datt, x, h, dmid, w, cols, g_out, g_up, g_down, sums)
+    )(scalars, q, kv, delta, lse, datt, x, h, dmid, w, cols, g_out, g_up, g_down, sums)
 
 
 def body(
@@ -1213,17 +1360,17 @@
         all_kv = all_kv.reshape(bands, 2, GROUPS_OF_HEADS, -1, count).transpose(0, 2, 1, 3, 4)
         all_kv = all_kv.reshape(bands, GROUPS_OF_HEADS, -1, count)
         att, lse = attend(scalars, q, all_kv)
-    out, dmid, datt, g_out, g_up, g_down, sums = middle(
+    out, dmid, datt, delta, g_out, g_up, g_down, sums = middle(
         x, cot, scalars, att, full_out, full_up, full_down, cols, c_up
     )
     if direct:
         gx, *pieces, total = back(
-            images, bands, scalars, q, all_kv, att, lse, datt, x, h, dmid,
+            images, bands, scalars, q, all_kv, delta, lse, datt, x, h, dmid,
             full_qkv, cols, (g_out, g_up, g_down), sums,
         )
         matrices = [item.reshape(-1, item.shape[2]).T for item in pieces]
     else:
-        dq, dkv = attend_back(scalars, q, all_kv, att, lse, datt)
+        dq, dkv = attend_back(scalars, q, all_kv, delta, lse, datt)
         dkv = unshare(images, dkv)
         gx, g_qkv, sums_one = finish(x, h, dq, dkv, full_qkv, cols, dmid)
         matrices = [

time: 337 us -> 287 us (0.85)
  Pallas kernels: 311 us -> 261 us
    pallas_call x1, Pallas kernels: 137 us -> 99.9 us  [front(): pl.pallas_call(functools.partial(front_kernel, images, bands), name='fron...]
    pallas_call x1, Pallas kernels: 136 us -> 123 us  [back(): pl.pallas_call(functools.partial(back_kernel, images, bands), name='back'...]
where the time goes in v4:
time: 287 us
  Pallas kernels  261 us (91%)
  local copies, waits for them, and re-layouts  22.5 us (8%)
    pallas_call x1, Pallas kernels, back(): pl.pallas_call(functools.partial(back_kernel, images, bands), name='back'...  123 us
    pallas_call x1, Pallas kernels, front(): pl.pallas_call(functools.partial(front_kernel, images, bands), name='fron...  99.9 us
    pallas_call x1, Pallas kernels, middle(): pl.pallas_call(middle_kernel, name='middle', out_shape=(shape(full, BF),...  37.6 us
    reshape x4, local copies, waits for them, and re-layouts, turn_back(): return values.reshape(width, slots, rows).transpose(2, 1, 0)[None]  7.15 us

profile of v4, /device:TPU:0, one launch (start us, length us, event | category | flops | bytes accessed | tf_op | source)
XLA Modules:
  0.0 286.8 jit_solution(2799643660938680302)
XLA Ops:
  0.7 0.0 copy-start.3
  0.7 0.0 copy-start.5
  0.7 0.0 copy-start.7
  0.7 0.0 copy-start.14
  0.7 0.0 copy-start.8
  0.7 0.0 copy-start.9
  0.7 0.0 copy-start.10
  0.7 0.0 copy-start.11
  0.7 0.0 copy-start.12
  0.7 0.0 copy-start.13
  0.8 1.3 pad_add_fusion.scalars_ref
  2.1 2.8 copy.29
  4.9 1.1 copy.39
  5.9 1.0 copy.33
  7.0 0.0 copy-done.3
  7.0 0.1 copy.31
  7.1 0.0 copy-done.5
  7.1 0.1 copy.32
  7.2 0.8 pad_maximum_fusion.narrow_ref
  8.0 0.0 copy-done.7
  8.0 0.1 reshape.88
  8.1 0.0 copy-done.14
  8.1 0.1 reshape.87
  8.2 0.0 copy-done.8
  8.2 0.0 copy-done.9
  8.2 0.0 copy-done.10
  8.2 0.0 copy-done.11
  8.3 0.0 copy-done.12
  8.3 0.0 copy-done.13
  8.3 0.1 concatenate.11
  8.4 0.6 pad_convert_fusion.small_ref
  9.0 99.9 %front.1 = (bf16[4,2,288,768]{3,2,1,0:T(8,128)(2,1)}, bf16[4,2,96,768]{3,2,1,0:T(8,128)(2,1)}, bf16[4,2,384,768]{3,2,1,0:T(8,128)(2,1)}, bf16[4,2,96,3072]{3,2,1...) custom-call(s32[3]{0:T(128)} %pad_add_fusion.scalars_ref, ...), custom_call_target="tpu_custom_call" | custom-call | tf_op jit(solution)/shard_map/front/pallas_call | solution.py:749
  108.9 2.8 copy.30
  111.7 1.1 copy.40
  112.7 37.6 %middle.1 = (bf16[768,512]{1,0:T(8,128)(2,1)}, f32[768,512]{1,0:T(8,128)}, bf16[768,512]{1,0:T(8,128)(2,1)}, f32[16,512]{1,0:T(8,128)}, bf16[768,768]{1,0:T(8,12...) custom-call(bf16[768,512]{1,0:T(8,128)(2,1)} %bitcast.45, ...), custom_call_target="tpu_custom_call" | custom-call | tf_op jit(solution)/shard_map/middle/pallas_call | solution.py:326
  150.4 123.1 %back.1 = (bf16[768,512]{1,0:T(8,128)(2,1)}, f32[2,144,192]{2,1,0:T(8,128)}, f32[2,48,192]{2,1,0:T(8,128)}, f32[2,192,192]{2,1,0:T(8,128)}, f32[2,48,768]{2,1,0:T(8,128)}, /*index=5*/f32[16,768]{1,0:T(8,128)}) custom-call(s32[3]{0:T(128)} %pad_add_fusion.scalars_ref, bf16[768,512]{1,0:T(8,128)(2,1)} %get-tuple-element.46.q_ref, ...), custom_call_target="tpu_custom_call" | custom-call | tf_op jit(solution)/shard_map/back/pallas_call | solution.py:1272
  273.5 0.0 copy-start.1
  273.5 0.0 copy-start.6
  273.5 0.0 copy-start.4
  273.5 0.0 copy-start
  273.6 2.3 reshape.94
  275.9 0.0 copy-start.2
  275.9 2.3 copy.35
  278.2 1.8 copy.36
  280.0 0.0 copy-done.1
  280.0 0.9 copy.38
  280.9 0.0 copy-done.6
  280.9 0.6 fusion
  281.5 0.0 copy-done.4
  281.5 0.7 copy.37
  282.3 0.7 dynamic_slice.26
  282.9 0.6 dynamic_slice.24
  283.6 0.0 copy-done
  283.6 0.2 reshape.92
  283.7 2.3 copy.34
  286.1 0.0 copy-done.2
  286.1 0.7 copy.42
  (2 shorter events, 0.0 us)
Async XLA Ops:
  0.7 6.3 %copy-start.3 = (bf16[192,288]{1,0:T(8,128)(2,1)S(1)}, bf16[192,288]{1,0:T(8,128)(2,1)}, u32[]{:S(2)}) copy-start(bf16[192,288]{1,0:T(8,128)(2,1)} %param.17) | copy-start | bytes 331780
  0.7 6.5 %copy-start.5 = (bf16[192,96]{1,0:T(8,128)(2,1)S(1)}, bf16[192,96]{1,0:T(8,128)(2,1)}, u32[]{:S(2)}) copy-start(bf16[192,96]{1,0:T(8,128)(2,1)} %param.18) | copy-start | bytes 110596
  0.7 7.4 %copy-start.7 = (bf16[384]{0:T(512)(128)(2,1)S(1)}, bf16[384]{0:T(512)(128)(2,1)}, u32[]{:S(2)}) copy-start(bf16[384]{0:T(512)(128)(2,1)} %param.23) | copy-start | bytes 2308
  0.7 7.5 %copy-start.14 = (bf16[192]{0:T(256)(128)(2,1)S(1)}, bf16[192]{0:T(256)(128)(2,1)}, u32[]{:S(2)}) copy-start(bf16[192]{0:T(256)(128)(2,1)} %param.21) | copy-start | bytes 1156
  0.7 7.5 %copy-start.8 = (bf16[96]{0:T(256)(128)(2,1)S(1)}, bf16[96]{0:T(256)(128)(2,1)}, u32[]{:S(2)}) copy-start(bf16[96]{0:T(256)(128)(2,1)} %param.22) | copy-start | bytes 580
  0.7 7.5 %copy-start.9 = (bf16[96]{0:T(256)(128)(2,1)S(1)}, bf16[96]{0:T(256)(128)(2,1)}, u32[]{:S(2)}) copy-start(bf16[96]{0:T(256)(128)(2,1)} %param.24) | copy-start | bytes 580
  0.7 7.5 %copy-start.10 = (bf16[96]{0:T(256)(128)(2,1)S(1)}, bf16[96]{0:T(256)(128)(2,1)}, u32[]{:S(2)}) copy-start(bf16[96]{0:T(256)(128)(2,1)} %param.25) | copy-start | bytes 580
  0.7 7.5 %copy-start.11 = (bf16[96]{0:T(256)(128)(2,1)S(1)}, bf16[96]{0:T(256)(128)(2,1)}, u32[]{:S(2)}) copy-start(bf16[96]{0:T(256)(128)(2,1)} %param.26) | copy-start | bytes 580
  0.7 7.5 %copy-start.12 = (bf16[96]{0:T(256)(128)(2,1)S(1)}, bf16[96]{0:T(256)(128)(2,1)}, u32[]{:S(2)}) copy-start(bf16[96]{0:T(256)(128)(2,1)} %param.27) | copy-start | bytes 580
  0.7 7.5 %copy-start.13 = (bf16[96]{0:T(256)(128)(2,1)S(1)}, bf16[96]{0:T(256)(128)(2,1)}, u32[]{:S(2)}) copy-start(bf16[96]{0:T(256)(128)(2,1)} %param.28) | copy-start | bytes 580
  273.5 6.5 %copy-start.1 = (f32[2,192,192]{2,1,0:T(8,128)S(1)}, f32[2,192,192]{2,1,0:T(8,128)}, u32[]{:S(2)}) copy-start(f32[2,192,192]{2,1,0:T(8,128)} %get-tuple-element.61) | copy-start | bytes 884740
  273.5 7.4 %copy-start.6 = (f32[16,768]{1,0:T(8,128)S(1)}, f32[16,768]{1,0:T(8,128)}, u32[]{:S(2)}) copy-start(f32[16,768]{1,0:T(8,128)} %get-tuple-element.63) | copy-start | bytes 147460
  273.5 8.0 %copy-start.4 = (f32[2,48,192]{2,1,0:T(8,128)S(1)}, f32[2,48,192]{2,1,0:T(8,128)}, u32[]{:S(2)}) copy-start(f32[2,48,192]{2,1,0:T(8,128)} %get-tuple-element.60) | copy-start | bytes 221188
  273.5 10.0 %copy-start = (bf16[768,512]{1,0:T(8,128)(2,1)S(1)}, bf16[768,512]{1,0:T(8,128)(2,1)}, u32[]{:S(2)}) copy-start(bf16[768,512]{1,0:T(8,128)(2,1)} %get-tuple-element.45) | copy-start | bytes 2359300
  275.9 10.2 %copy-start.2 = (f32[2,48,768]{2,1,0:T(8,128)S(1)}, f32[2,48,768]{2,1,0:T(8,128)}, u32[]{:S(2)}) copy-start(f32[2,48,768]{2,1,0:T(8,128)} %get-tuple-element.62) | copy-start | bytes 884740

commit v5 on v4

--- a/solution.py
+++ b/solution.py
@@ -227,35 +227,23 @@
 
 
 def middle_kernel(
-    x_ref,
-    cot_ref,
-    scalars_ref,
-    att_ref,
-    w_out_ref,
-    w_up_ref,
-    w_down_ref,
-    cols_ref,
-    bias_up_ref,
-    out_ref,
-    dmid_ref,
-    datt_ref,
-    delta_ref,
-    g_out_ref,
-    g_up_ref,
-    g_down_ref,
-    sums_ref,
-    mid_ref,
-    norm_ref,
-    h_ref,
-    dmlp_ref,
-    mlp_ref,
-    err_ref,
-    attb_ref,
-    dbranch_ref,
+    x_ref, cot_ref, scalars_ref, att_ref, w_out_in, w_up_in, w_down_in, cols_ref, bias_up_ref,
+    out_ref, dmid_ref, datt_ref, delta_ref, g_out_ref, g_up_out, g_down_out, sums_ref,
+    w_out_ref, w_up_ref, w_down_ref, g_up_ref, g_down_ref,
+    mid_ref, norm_ref, h_ref, dmlp_ref, mlp_ref, err_ref, attb_ref, dbranch_ref,
+    in_sem, up_sem, down_sem,
 ):
     width, tokens = x_ref.shape
     hidden = w_up_ref.shape[0]
     step = 256
+    loads = [
+        pltpu.make_async_copy(source, target, in_sem.at[k])
+        for k, (source, target) in enumerate(
+            ((w_out_in, w_out_ref), (w_up_in, w_up_ref), (w_down_in, w_down_ref))
+        )
+    ]
+    for copy in loads:
+        copy.start()
     first_slot = lax.broadcasted_iota(jnp.int32, (1, tokens), 1) < tokens // 2
     valid = jnp.where(
         first_slot,
@@ -263,7 +251,11 @@
         jnp.where(scalars_ref[1] > 0, 1.0, 0.0),
     )
     attb_ref[...] = att_ref[...].astype(BF)
+    dmlp_ref[...] = (cot_ref[...].astype(F) * valid).astype(BF)
     sums_ref[...] = jnp.zeros_like(sums_ref)
+    mlp_ref[...] = jnp.zeros_like(mlp_ref)
+    err_ref[...] = jnp.zeros_like(err_ref)
+    loads[0].wait()
 
     @pl.loop(0, width // step)
     def _(j):
@@ -277,9 +269,15 @@
     normed, inverse = normalize(mid_ref[...])
     norm_ref[...] = normed
     h_ref[...] = (normed * cols_ref[:, GAIN_TWO] + cols_ref[:, SHIFT_TWO]).astype(BF)
-    dmlp_ref[...] = (cot_ref[...].astype(F) * valid).astype(BF)
-    mlp_ref[...] = jnp.zeros_like(mlp_ref)
-    err_ref[...] = jnp.zeros_like(err_ref)
+    loads[1].wait()
+    loads[2].wait()
+
+    def stores(j):
+        rows = pl.ds(pl.multiple_of(j * step, step), step)
+        return (
+            pltpu.make_async_copy(g_up_ref.at[rows, :], g_up_out.at[rows, :], up_sem.at[j]),
+            pltpu.make_async_copy(g_down_ref.at[:, rows], g_down_out.at[:, rows], down_sem.at[j]),
+        )
 
     @pl.loop(0, hidden // step)
     def _(j):
@@ -297,6 +295,8 @@
         lanes = pl.ds(pl.multiple_of(j % per * step, step), step)
         sums_ref[pl.ds(UP_ROW + j // per, 1), lanes] = row_sums(dhid)[:1]
         err_ref[...] += dg(w_up_ref[rows, :], dhid, 0, 0)
+        for copy in stores(j):
+            copy.start()
 
     out_ref[...] = ((mid_ref[...] + mlp_ref[...] + cols_ref[:, BIAS_DOWN]) * valid).astype(BF)
     err = err_ref[...]
@@ -318,11 +318,17 @@
         rows = pl.ds(pl.multiple_of(j * step, step), step)
         g_out_ref[rows, :] = dg(dbranch_ref[rows, :], attb_ref[...], 1, 1).astype(BF)
 
+    @pl.loop(0, hidden // step)
+    def _(j):
+        for copy in stores(j):
+            copy.wait()
+
 
 def middle(x, cot, scalars, att, w_out, w_up, w_down, cols, bias_up):
     width, tokens = x.shape
     hidden = w_up.shape[0]
     full = (width, tokens)
+    weights = [w_out.shape, w_up.shape, w_down.shape]
     return pl.pallas_call(
         middle_kernel,
         name="middle",
@@ -336,9 +342,10 @@
             shape(w_down.shape, BF),
             shape((SUM_ROWS, width), F),
         ),
-        in_specs=[VM, VM, SM] + [VM] * 6,
-        out_specs=tuple([VM] * 8),
-        scratch_shapes=[
+        in_specs=[VM, VM, SM, VM] + [ANY] * 3 + [VM] * 2,
+        out_specs=(VM,) * 5 + (ANY, ANY, VM),
+        scratch_shapes=[pltpu.VMEM(s, BF) for s in weights + weights[1:]]
+        + [
             pltpu.VMEM(full, F),
             pltpu.VMEM(full, F),
             pltpu.VMEM(full, BF),
@@ -347,6 +354,9 @@
             pltpu.VMEM(full, F),
             pltpu.VMEM(full, BF),
             pltpu.VMEM(full, BF),
+            pltpu.SemaphoreType.DMA((3,)),
+            pltpu.SemaphoreType.DMA((hidden // 256,)),
+            pltpu.SemaphoreType.DMA((hidden // 256,)),
         ],
         compiler_params=pltpu.CompilerParams(vmem_limit_bytes=LIMIT),
     )(x, cot, scalars, att, w_out, w_up, w_down, cols, bias_up)
@@ -461,7 +471,9 @@
         piece = ref.at[at.z, at.y, rows, lanes]
         source = source.at[:, pl.ds(part * size, size)]
         self.keep = pltpu.make_async_copy(source, piece, local_sem)
-        z_first = [make(source, piece, peer) for peer, _ in at.z_peers]
+        z_first = []
+        if order != "xyz":
+            z_first = [make(source, piece, peer) for peer, _ in at.z_peers]
         if order == "mixed":
             self.stages = [
                 z_first,
@@ -519,8 +531,9 @@
 
 def front_kernel(
     images, bands, scalars_ref, narrow_ref, wide_ref, small_ref, x_ref,
-    qkv_w_ref, out_w_ref, up_w_ref, down_w_ref, h_ref, q_ref, kv_ref, att_ref, lse_ref,
-    cols_ref, up_col_ref,
+    qkv_w_out, out_w_ref, up_w_ref, down_w_ref, h_out, kv_out, x_far_out,
+    q_ref, att_ref, lse_ref, cols_ref, up_col_ref,
+    qkv_w_ref, h_ref, kv_ref,
     theirs_ref, mine_ref, mine_wide_ref, smalls_ref, qv_col_ref, bias_ref, x_far_ref,
     local_sem, send_sem, recv_sem,
 ):
@@ -584,6 +597,12 @@
     (s_out,) = spread(out_w_ref, sources[1], ("mixed",))
     s_up = spread(up_w_ref, sources[2], ("mixed", "zxy", "zxy"))
     d_one, d_two = spread(down_w_ref, sources[3], ("xyz", "mixed"))
+    save_w = pltpu.make_async_copy(qkv_w_ref, qkv_w_out, local())
+    save_h = pltpu.make_async_copy(h_ref, h_out, local())
+    save_x = pltpu.make_async_copy(x_far_ref, x_far_out, local())
+    save_kv = [
+        pltpu.make_async_copy(kv_ref.at[:, g], kv_out.at[:, g], local()) for g in range(groups)
+    ]
     x_lanes = [pl.ds(s * rows, rows) for s in range(2)]
     x_moves = [make(x_ref.at[:, l], x_far_ref.at[:, l], at.across_x) for l in x_lanes]
     far = at.across_x[1]
@@ -663,6 +682,7 @@
     s_up[1].step(1)
     for item in s_qkv:
         item.wait()
+    save_w.start()
 
     weights = qkv_w_ref.reshape(3 * width, width)
     scale = 1.0 / math.sqrt(HEAD_DIM)
@@ -689,10 +709,14 @@
         x_moves[1].wait_recv()
         first_norm(1, x_far_ref, 1)
         project(1)
+        save_h.start()
+        save_x.start()
 
     def arrive(s, g):
         for copy in kv_moves[s][g]:
             copy.wait_recv()
+        if s == 1:
+            save_kv[g].start()
 
     events = {}
 
@@ -735,6 +759,8 @@
         item.wait()
     for item in s_qkv + s_up + [s_out, d_one, d_two]:
         item.end()
+    for copy in [save_w, save_h, save_x] + save_kv:
+        copy.wait()
     for copy in [swap, swap_wide] + small_copies + x_moves:
         copy.wait_send()
     for copy in sum(sum(kv_moves, []), []):
@@ -753,16 +779,20 @@
         + (
             shape((depth, 2, wide.shape[0], 4 * wide.shape[1]), BF),
             shape((width, 2 * tokens), BF),
+            shape((bands, groups, 2 * width // groups, tokens), BF),
             shape((width, tokens), BF),
-            shape((bands, groups, 2 * width // groups, tokens), BF),
+            shape((width, tokens), BF),
             shape((width, tokens), F),
             shape((2 * HEADS, tokens // 2), F),
             shape((width, COLUMNS), F),
             shape((hidden, 1), F),
         ),
         in_specs=[SM] + [VM] * 4,
-        out_specs=(VM, ANY, ANY, ANY) + (VM,) * 7,
+        out_specs=(ANY,) * 7 + (VM,) * 5,
         scratch_shapes=[
+            pltpu.VMEM((depth, 2, widths[0], width), BF),
+            pltpu.VMEM((width, 2 * tokens), BF),
+            pltpu.VMEM((bands, groups, 2 * width // groups, tokens), BF),
             pltpu.VMEM(narrow.shape[1:], BF),
             pltpu.VMEM((narrow.shape[1], 2 * narrow.shape[2]), BF),
             pltpu.VMEM((wide.shape[0] // 2, 2 * wide.shape[1]), BF),
@@ -770,7 +800,7 @@
             pltpu.VMEM((2 * width, 1), F),
             pltpu.VMEM((8, tokens // 2), F),
             pltpu.VMEM((width, tokens), BF),
-            pltpu.SemaphoreType.DMA((16,)),
+            pltpu.SemaphoreType.DMA((24,)),
             pltpu.SemaphoreType.DMA((FRONT_COPIES,)),
             pltpu.SemaphoreType.DMA((FRONT_COPIES,)),
         ],
@@ -872,22 +902,20 @@
 
 
 def accumulate(total, other):
-    total[...] = (total[...].astype(F) + other[...].astype(F)).astype(total.dtype)
+    total[...] = total[...] + other[...]
 
 
 class Reduction:
-    def __init__(self, at, make, order, part, parts, ref, one, bufs, total):
-        depth, near, c = at.depth, at.depth // 2, at.c
-        rows, half = ref.shape[2] // 2, ref.shape[3] // 2
-        size = half // parts
-        self.at, self.near, self.ref, self.one, self.order = at, near, ref, one, order
-        self.rows = pl.ds(pl.multiple_of(c * rows, 16), rows)
+    def __init__(self, at, make, order, start, size, ref, one, other, bufs, total):
+        depth, near = at.depth, at.depth // 2
+        half = ref.shape[3] // 2
+        self.at, self.near, self.one, self.other, self.order = at, near, one, other, order
 
         def lanes_of(x):
-            return pl.ds(pl.multiple_of(x * half + part * size, 128), size)
+            return pl.ds(pl.multiple_of(x * half + start, 128), size)
 
         self.lanes, self.both = lanes_of(at.x), [lanes_of(x) for x in range(2)]
-        self.total = total.at[:, pl.ds(part * size, size)]
+        self.total = total.at[:, pl.ds(start, size)]
         far = lanes_of(1 - at.x)
         upper = depth - near
         if order == "mixed":
@@ -922,7 +950,7 @@
             def _(j):
                 accumulate(
                     self.one.at[j // 2, j % 2, :, lanes],
-                    self.ref.at[j // 2, j % 2, self.rows, lanes],
+                    self.other.at[j // 2, j % 2, :, lanes],
                 )
 
         for copy in self.first:
@@ -1005,21 +1033,36 @@
     return [pltpu.VMEM(s, BF) for s in first + [(depth, rows, size), (depth - 1, rows, size)]]
 
 
-BACK_ORDERS = (("mixed",) * 2, ("mixed",) * 3, ("mixed",), ("yx",) * 3)
+BACK_ORDERS = (
+    (("mixed", 1), ("mixed", 1)),
+    (("mixed", 1), ("mixed", 1), ("mixed", 1)),
+    (("mixed", 1),),
+    (("mixed", 2), ("yx", 1)),
+)
+
+
+def lane_parts(orders, half):
+    unit = half // sum(share for _, share in orders)
+    parts, start = [], 0
+    for order, share in orders:
+        parts.append((order, start, share * unit))
+        start += share * unit
+    return parts
 
 
 def back_kernel(
-    images, bands, scalars_ref, q_ref, kv_ref, delta_ref, lse_ref, datt_ref, x_ref, h_ref, dmid_ref,
-    w_ref, cols_ref, g_out_ref, g_up_ref, g_down_ref, sums_ref,
+    images, bands, scalars_ref, q_ref, delta_ref, lse_ref, datt_ref, cols_ref, sums_ref,
+    kv_in, x_in, x_far_in, h_in, dmid_in, w_in, g_out_ref, g_up_ref, g_down_ref,
     gx_ref, p_qkv_ref, p_out_ref, p_up_ref, p_down_ref, total_ref,
+    kv_ref, x_ref, x_far_ref, h_ref, dmid_ref, w_ref,
     bias_ref, dq_ref, dwide_ref, dkv_ref, near_ref, g_qkv_ref, err_ref, err_far_ref, err_in_ref,
     small_ref, small_in_ref, small_z_ref, *rest,
 ):
     at = Place(images)
     depth = at.depth
-    send_sem, recv_sem = rest[-2:]
-    rest = list(rest[:-2])
-    used = [0]
+    local_sem, send_sem, recv_sem = rest[-3:]
+    rest = list(rest[:-3])
+    used = [0, 0]
 
     def make(src, dst, peer):
         k = used[0]
@@ -1033,6 +1076,10 @@
             device_id_type=MESH,
         )
 
+    def load(src, dst):
+        used[1] += 1
+        return pltpu.make_async_copy(src, dst, local_sem.at[used[1] - 1])
+
     width, tokens = x_ref.shape
     rows = tokens // 2
     unroll = 4
@@ -1044,23 +1091,37 @@
 
     sources = (four_d(g_down_ref), four_d(g_up_ref), four_d(g_out_ref), g_qkv_ref)
     targets = (p_down_ref, p_up_ref, p_out_ref, p_qkv_ref)
-    swaps, moves, ends = [], [], []
+    swaps, owns, moves, ends = [], [], [], []
     for m in range(4):
         one, total, away = rest[:3]
         rest = rest[3:]
-        block = sources[m].shape[2] // 2
+        block, lanes = sources[m].shape[2] // 2, sources[m].shape[3]
+        near_rows = pl.ds(pl.multiple_of(at.c * block, 16), block)
         far_rows = pl.ds(pl.multiple_of((1 - at.c) * block, 16), block)
-        swaps.append(make(sources[m].at[:, :, far_rows, :], one, at.partner))
-        orders = BACK_ORDERS[m]
+        parts = lane_parts(BACK_ORDERS[m], lanes // 2)
+        if m < 3:
+            other = rest.pop(0)
+            owns.append(load(sources[m].at[:, :, near_rows, :], one))
+            swaps.append([make(sources[m].at[:, :, far_rows, :], other, at.partner)])
+        else:
+            other = sources[m].at[:, :, near_rows, :]
+            for _, start, size in parts:
+                both = [pl.ds(x * (lanes // 2) + start, size) for x in range(2)]
+                swaps.append(
+                    [
+                        make(sources[m].at[:, :, far_rows, l], one.at[:, :, :, l], at.partner)
+                        for l in both
+                    ]
+                )
         moves.append([])
-        for k, order in enumerate(orders):
-            size = 4 if order == "mixed" else 3
+        for order, start, size in parts:
+            count = 4 if order == "mixed" else 3
             moves[m].append(
                 Reduction(
-                    at, make, order, k, len(orders), sources[m], one, rest[:size], total
+                    at, make, order, start, size, sources[m], one, other, rest[:count], total
                 )
             )
-            rest = rest[size:]
+            rest = rest[count:]
         ends.append((total, away, targets[m], make(away, targets[m].at[at.c], at.partner)))
     down, up, out, qkv = moves
 
@@ -1086,9 +1147,21 @@
         make(small_z_ref.at[at.z], small_z_ref.at[at.z], peer) for peer, _ in at.z_peers
     ]
 
+    kv_loads = [load(kv_in.at[:, g], kv_ref.at[:, g]) for g in range(groups)]
+    late_loads = [
+        load(h_in, h_ref),
+        load(w_in, w_ref),
+        load(x_in, x_ref),
+        load(x_far_in, x_far_ref),
+        load(dmid_in, dmid_ref),
+    ]
+    kv_loads[0].start()
+    owns[0].start()
     greet([at.partner, at.across_x, at.across_y] + [peer for peer, _ in at.z_peers])
     for m in range(3):
-        swaps[m].start()
+        swaps[m][0].start()
+    for copy in owns[1:] + kv_loads[1:] + late_loads:
+        copy.start()
     fill_bias(scalars_ref, bias_ref, rows)
 
     sides = [pl.ds(side * tokens, tokens) for side in range(2)]
@@ -1114,14 +1187,24 @@
     def when(j, *actions):
         events.setdefault(j, []).extend(actions)
 
-    when(0, swaps[0].wait_recv, down[0].step_one, down[1].step_one)
-    when(1, swaps[1].wait_recv, up[0].step_one, up[1].step_one, lambda: share_one(0))
+    def received(m):
+        owns[m].wait()
+        swaps[m][0].wait_recv()
+
+    for g in range(1, groups):
+        when(2 * g - 1, kv_loads[g].wait)
+    when(0, down[1].step_one)
+    when(0, lambda: received(1), up[0].step_one)
+    when(1, up[1].step_one, lambda: share_one(0))
     when(2, up[2].step_one, down[0].step_two, lambda: share_two(0))
-    when(3, swaps[2].wait_recv, out[0].step_one, down[1].step_two, lambda: share_one(1))
+    when(3, lambda: received(2), out[0].step_one, down[1].step_two, lambda: share_one(1))
     when(4, up[0].step_two, down[0].step_three, lambda: share_two(1))
     when(5, up[1].step_two, down[1].step_three, lambda: share_one(2))
     when(6, up[2].step_two, up[0].step_three, lambda: share_two(2))
     when(7, lambda: share_one(3), out[0].step_two, up[1].step_three)
+    received(0)
+    down[0].step_one()
+    kv_loads[0].wait()
 
     @pl.loop(0, 2 * groups)
     def _(j):
@@ -1149,23 +1232,20 @@
 
     chunk = width // 2
     g_flat = g_qkv_ref.reshape(3 * width, width)
-
-    @pl.loop(0, 2)
-    def _(j):
-        block = pl.ds(pl.multiple_of(j * chunk, 128), chunk)
-        g_flat[block, :] = dg(dq_ref[block, :], h_ref[:, sides[0]], 1, 1).astype(BF)
-
-    share_two(groups - 1)
-
-    @pl.loop(0, 4)
-    def _(j):
-        block = pl.ds(pl.multiple_of(j * chunk, 128), chunk)
-        to = pl.ds(pl.multiple_of((2 + j) * chunk, 128), chunk)
-        g_flat[to, :] = dg(dwide_ref[block, :], h_ref[...], 1, 1).astype(BF)
-
-    swaps[3].start()
-    up[2].step_three()
-    out[0].step_three()
+    parts = lane_parts(BACK_ORDERS[3], width // 2)
+
+    def weight_grad(part, source_ref, first, count, tokens_at):
+        _, start, size = parts[part]
+        lanes = [pl.ds(x * (width // 2) + start, size) for x in range(2)]
+
+        @pl.loop(0, count)
+        def _(j):
+            block = pl.ds(pl.multiple_of(j * chunk, 128), chunk)
+            to = pl.ds(pl.multiple_of((first + j) * chunk, 128), chunk)
+            both = jnp.concatenate([h_ref[l, tokens_at] for l in lanes], axis=0)
+            result = dg(source_ref[block, :], both, 1, 1).astype(BF)
+            g_flat[to, lanes[0]] = result[:, :size]
+            g_flat[to, lanes[1]] = result[:, size:]
 
     def back_through(side):
         err_ref[...] = jnp.zeros_like(err_ref)
@@ -1176,13 +1256,36 @@
             source = pl.ds(pl.multiple_of((2 + j) * chunk, 128), chunk)
             err_ref[...] += dg(w_ref[source, :], dwide_ref[block, sides[side]], 0, 0)
 
+    def start_swap(part):
+        for copy in swaps[3 + part]:
+            copy.start()
+
+    def first_sum(part):
+        for copy in swaps[3 + part]:
+            copy.wait_recv()
+        qkv[part].step_one()
+
+    for copy in late_loads:
+        copy.wait()
+    for p in range(2):
+        weight_grad(p, dq_ref, 0, 2, sides[0])
+    share_two(groups - 1)
+    weight_grad(0, dwide_ref, 2, 4, slice(None))
+    start_swap(0)
     back_through(1)
-    swaps[3].wait_recv()
-    for item in qkv:
-        item.step_one()
+    err_far = err_ref[...]
     for s in range(2):
-        err_far_ref[s] = err_ref[:, pl.ds(s * rows, rows)].astype(BF)
-        err_moves[s].start()
+        err_far_ref[s] = err_far[:, s * rows : (s + 1) * rows].astype(BF)
+    first_sum(0)
+    err_moves[0].start()
+    weight_grad(1, dwide_ref, 2, 4, slice(None))
+    start_swap(1)
+    normed_far, _ = normalize(x_far_ref[...].astype(F))
+    gain_row = row_sums(err_ref[...] * normed_far)[:1]
+    shift_row = row_sums(err_ref[...])[:1]
+    first_sum(1)
+    up[2].step_three()
+    out[0].step_three()
     back_through(0)
 
     @pl.loop(0, 2)
@@ -1190,68 +1293,68 @@
         block = pl.ds(pl.multiple_of(j * chunk, 128), chunk)
         err_ref[...] += dg(w_ref[block, :], dq_ref[block, :], 0, 0)
 
+    small_ref[0] = sums_ref[...]
+    small_ref[0, 0:1] = row_sums(dq_ref[...])[:1]
+    small_ref[0, 1:2] = row_sums(dwide_ref[pl.ds(width, width), :])[:1]
+    normed, _ = normalize(x_ref[...].astype(F))
+    small_ref[0, 4:5] = gain_row + row_sums(err_ref[...] * normed)[:1]
+    small_ref[0, 5:6] = shift_row + row_sums(err_ref[...])[:1]
+    small_steps[0].start()
+    qkv[0].step_two()
+    err_moves[1].start()
     for item in down:
         item.step_four()
     deliver(0)
-    qkv[0].step_two()
-    up[0].step_four()
-    up[1].step_four()
+    small_steps[0].wait_recv()
+    small_ref[1] = small_ref[0] + small_in_ref[0]
+    small_steps[1].start()
     qkv[1].step_two()
-    up[2].step_four()
+    qkv[0].step_three()
+    small_steps[1].wait_recv()
+    small_ref[2] = small_ref[1] + small_in_ref[1]
+    small_steps[2].start()
+    for item in up:
+        item.step_four()
     deliver(1)
-    qkv[0].step_three()
-    qkv[2].step_two()
+    small_steps[2].wait_recv()
+    small_z_ref[at.z] = small_ref[2] + small_in_ref[2]
+    for copy in small_last:
+        copy.start()
     out[0].step_four()
     deliver(2)
     qkv[1].step_three()
-    small_ref[0] = sums_ref[...]
-    small_ref[0, 0:1] = row_sums(dq_ref[...])[:1]
-    small_ref[0, 1:2] = row_sums(dwide_ref[pl.ds(width, width), :])[:1]
-    gain_row, shift_row = 0.0, 0.0
-    for s in range(2):
+
+    def finish_slot(s):
         err_moves[s].wait_recv()
         lanes = slice(s * rows, (s + 1) * rows)
         err = err_ref[:, lanes] + err_in_ref[s].astype(F)
         normed, inverse = normalize(x_ref[:, lanes].astype(F))
-        gain_row = gain_row + row_sums(err * normed)[:1]
-        shift_row = shift_row + row_sums(err)[:1]
         gx_ref[:, lanes] = (
             dmid_ref[:, lanes] + norm_back(err, normed, inverse, cols_ref[:, GAIN_ONE])
         ).astype(BF)
-    small_ref[0, 4:5] = gain_row
-    small_ref[0, 5:6] = shift_row
-    small_steps[0].start()
-    qkv[2].step_three()
-    small_steps[0].wait_recv()
-    small_ref[1] = small_ref[0] + small_in_ref[0]
-    small_steps[1].start()
+
+    finish_slot(0)
     qkv[0].step_four()
-    small_steps[1].wait_recv()
-    small_ref[2] = small_ref[1] + small_in_ref[1]
-    small_steps[2].start()
-    qkv[1].step_four()
-    small_steps[2].wait_recv()
-    small_z_ref[at.z] = small_ref[2] + small_in_ref[2]
-    for copy in small_last:
-        copy.start()
-    qkv[2].step_four()
-    deliver(3)
     for copy in small_last:
         copy.wait_recv()
     total = small_z_ref[0]
     for k in range(1, depth):
         total = total + small_z_ref[k]
     total_ref[...] = total
+    qkv[1].step_four()
+    deliver(3)
+    finish_slot(1)
     for m in range(4):
         ends[m][3].wait()
-        swaps[m].wait_send()
         for item in moves[m]:
             item.end()
-    for copy in one + two + err_moves + small_steps + small_last:
+    for copy in sum(swaps, []) + one + two + err_moves + small_steps + small_last:
         copy.wait_send()
 
 
-def back(images, bands, scalars, q, kv, delta, lse, datt, x, h, dmid, w, cols, grads, sums):
+def back(
+    images, bands, scalars, q, kv, delta, lse, datt, x, x_far, h, dmid, w, cols, grads, sums
+):
     depth = images // 2
     width, tokens = x.shape
     g_out, g_up, g_down = grads
@@ -1265,17 +1368,24 @@
             pltpu.VMEM((block, lanes // 2), F),
             pltpu.VMEM((block, lanes // 4), F),
         ]
-        orders = BACK_ORDERS[m]
-        for order in orders:
-            buffers += reduction_buffers(order, depth, block, lanes // 2 // len(orders))
+        if m < 3:
+            buffers.append(pltpu.VMEM((depth, 2, block, lanes), BF))
+        for order, _, size in lane_parts(BACK_ORDERS[m], lanes // 2):
+            buffers += reduction_buffers(order, depth, block, size)
     small = (SUM_ROWS, width)
     return pl.pallas_call(
         functools.partial(back_kernel, images, bands),
         name="back",
         out_shape=(shape(x.shape, BF), results[3], results[2], results[1], results[0], shape(small, F)),
-        in_specs=[SM] + [VM] * 14,
+        in_specs=[SM] + [VM] * 6 + [ANY] * 9,
         out_specs=(VM,) * 6,
         scratch_shapes=[
+            pltpu.VMEM(kv.shape, BF),
+            pltpu.VMEM((width, tokens), BF),
+            pltpu.VMEM((width, tokens), BF),
+            pltpu.VMEM((width, 2 * tokens), BF),
+            pltpu.VMEM((width, tokens), F),
+            pltpu.VMEM(w.shape, BF),
             pltpu.VMEM((8, tokens // 2), F),
             pltpu.VMEM((width, tokens), BF),
             pltpu.VMEM((2 * width, 2 * tokens), BF),
@@ -1290,9 +1400,15 @@
             pltpu.VMEM((depth,) + small, F),
         ]
         + buffers
-        + [pltpu.SemaphoreType.DMA((BACK_COPIES,)), pltpu.SemaphoreType.DMA((BACK_COPIES,))],
+        + [
+            pltpu.SemaphoreType.DMA((16,)),
+            pltpu.SemaphoreType.DMA((BACK_COPIES,)),
+            pltpu.SemaphoreType.DMA((BACK_COPIES,)),
+        ],
         compiler_params=comm_params(3),
-    )(scalars, q, kv, delta, lse, datt, x, h, dmid, w, cols, g_out, g_up, g_down, sums)
+    )(
+        scalars, q, delta, lse, datt, cols, sums, kv, x, x_far, h, dmid, w, g_out, g_up, g_down
+    )
 
 
 def body(
@@ -1340,7 +1456,7 @@
         units = [jnp.stack(single), jnp.zeros((4, unit), BF)]
         units += [bias_qv.reshape(2, unit), bias_up.reshape(4, unit)]
         small = jnp.pad(jnp.concatenate(units), ((0, 0), (0, 128 - unit))).astype(F)
-        *full, h, q, all_kv, att, lse, cols, c_up = front(
+        *full, h, all_kv, x_far, q, att, lse, cols, c_up = front(
             images, bands, scalars, narrow, w_down.T, small, x, widths
         )
         full_qkv, full_out, full_up, full_down = (item.reshape(-1, item.shape[3]) for item in full)
@@ -1365,7 +1481,7 @@
     )
     if direct:
         gx, *pieces, total = back(
-            images, bands, scalars, q, all_kv, delta, lse, datt, x, h, dmid,
+            images, bands, scalars, q, all_kv, delta, lse, datt, x, x_far, h, dmid,
             full_qkv, cols, (g_out, g_up, g_down), sums,
         )
         matrices = [item.reshape(-1, item.shape[2]).T for item in pieces]

time: 287 us -> 271 us (0.944)
  Pallas kernels: 261 us -> 245 us
    pallas_call x1, Pallas kernels: 123 us -> 114 us  [back(): pl.pallas_call(functools.partial(back_kernel, images, bands), name='back'...]
    pallas_call x1, Pallas kernels: 99.9 us -> 96.3 us  [front(): pl.pallas_call(functools.partial(front_kernel, images, bands), name='fron...]
    pallas_call x1, Pallas kernels: 37.6 us -> 34.2 us  [middle(): pl.pallas_call(middle_kernel, name='middle', out_shape=(shape(full, BF),...]
where the time goes in v5:
time: 271 us
  Pallas kernels  245 us (90%)
  local copies, waits for them, and re-layouts  22.5 us (8%)
  other arithmetic  2.74 us (1%)
    pallas_call x1, Pallas kernels, back(): pl.pallas_call(functools.partial(back_kernel, images, bands), name='back'...  114 us
    pallas_call x1, Pallas kernels, front(): pl.pallas_call(functools.partial(front_kernel, images, bands), name='fron...  96.3 us
    pallas_call x1, Pallas kernels, middle(): pl.pallas_call(middle_kernel, name='middle', out_shape=(shape(full, BF),...  34.2 us
    reshape x4, local copies, waits for them, and re-layouts, turn_back(): return values.reshape(width, slots, rows).transpose(2, 1, 0)[None]  7.15 us
    transpose x2, local copies, waits for them, and re-layouts, turn(): return values[0].transpose(2, 1, 0).reshape(width, count)  5.59 us

profile of v5, /device:TPU:0, one launch (start us, length us, event | category | flops | bytes accessed | tf_op | source)
XLA Modules:
  0.0 270.7 jit_solution(11895826963127288085)
XLA Ops:
  0.7 0.0 copy-start.3
  0.7 0.0 copy-start.5
  0.7 0.0 copy-start.7
  0.7 0.0 copy-start.14
  0.7 0.0 copy-start.8
  0.7 0.0 copy-start.9
  0.7 0.0 copy-start.10
  0.7 0.0 copy-start.11
  0.7 0.0 copy-start.12
  0.7 0.0 copy-start.13
  0.8 1.3 pad_add_fusion.scalars_ref
  2.1 2.8 %copy.29 = bf16[768,2,256]{2,1,0:T(2,128)(2,1)S(1)} copy(bf16[768,2,256]{0,1,2:T(2,128)(2,1)} %bitcast.54) | data formatting | bytes 1572864 | tf_op jit(solution)/shard_map/transpose | solution.py:1444
  4.9 1.1 copy.39
  5.9 1.0 copy.33
  7.0 0.0 copy-done.3
  7.0 0.1 copy.31
  7.1 0.0 copy-done.5
  7.1 0.1 copy.32
  7.2 0.8 pad_maximum_fusion.narrow_ref
  8.0 0.0 copy-done.7
  8.0 0.1 reshape.88
  8.1 0.0 copy-done.14
  8.1 0.1 reshape.87
  8.2 0.0 copy-done.8
  8.2 0.0 copy-done.9
  8.2 0.0 copy-done.10
  8.2 0.0 copy-done.11
  8.3 0.0 copy-done.12
  8.3 0.0 copy-done.13
  8.3 0.1 concatenate.11
  8.4 0.6 pad_convert_fusion.small_ref
  9.0 96.3 %front.1 = (bf16[4,2,288,768]{3,2,1,0:T(8,128)(2,1)}, bf16[4,2,96,768]{3,2,1,0:T(8,128)(2,1)}, bf16[4,2,384,768]{3,2,1,0:T(8,128)(2,1)}, bf16[4,2,96,3072]{3,2,1...) custom-call(s32[3]{0:T(128)} %pad_add_fusion.scalars_ref, ...), custom_call_target="tpu_custom_call" | custom-call | tf_op jit(solution)/shard_map/front/pallas_call | solution.py:775
  105.3 2.8 %copy.30 = bf16[768,2,256]{2,1,0:T(2,128)(2,1)S(1)} copy(bf16[768,2,256]{0,1,2:T(2,128)(2,1)} %bitcast.55) | data formatting | bytes 1572864 | tf_op jit(solution)/shard_map/transpose | solution.py:1444
  108.1 1.1 copy.40
  109.2 34.2 %middle.1 = (bf16[768,512]{1,0:T(8,128)(2,1)}, f32[768,512]{1,0:T(8,128)}, bf16[768,512]{1,0:T(8,128)(2,1)}, f32[16,512]{1,0:T(8,128)}, bf16[768,768]{1,0:T(8,12...) custom-call(bf16[768,512]{1,0:T(8,128)(2,1)} %bitcast.45, ...), custom_call_target="tpu_custom_call" | custom-call | tf_op jit(solution)/shard_map/middle/pallas_call | solution.py:332
  143.4 114.0 %back.1 = (bf16[768,512]{1,0:T(8,128)(2,1)}, f32[2,144,192]{2,1,0:T(8,128)}, f32[2,48,192]{2,1,0:T(8,128)}, f32[2,192,192]{2,1,0:T(8,128)}, f32[2,48,768]{2,1,0:T(8,128)}, /*index=5*/f32[16,768]{1,0:T(8,128)}) custom-call(s32[3]{0:T(128)} %pad_add_fusion.scalars_ref, bf16[768,512]{1,0:T(8,128)(2,1)} %get-tuple-element.47.q_ref, ...), custom_call_target="tpu_custom_call" | custom-call | tf_op jit(solution)/shard_map/back/pallas_call | solution.py:1376
  257.5 0.0 copy-start.1
  257.5 0.0 copy-start.6
  257.5 0.0 copy-start.4
  257.5 0.0 copy-start
  257.5 2.3 reshape.94
  259.8 0.0 copy-start.2
  259.8 2.3 copy.35
  262.1 1.8 copy.36
  264.0 0.0 copy-done.1
  264.0 0.9 copy.38
  264.8 0.0 copy-done.6
  264.9 0.6 fusion
  265.5 0.0 copy-done.4
  265.5 0.7 copy.37
  266.2 0.7 dynamic_slice.26
  266.9 0.6 dynamic_slice.24
  267.5 0.0 copy-done
  267.5 0.2 reshape.92
  267.7 2.3 copy.34
  270.0 0.0 copy-done.2
  270.0 0.7 copy.42
  (2 shorter events, 0.0 us)
Async XLA Ops:
  0.7 6.3 %copy-start.3 = (bf16[192,288]{1,0:T(8,128)(2,1)S(1)}, bf16[192,288]{1,0:T(8,128)(2,1)}, u32[]{:S(2)}) copy-start(bf16[192,288]{1,0:T(8,128)(2,1)} %param.17) | copy-start | bytes 331780
  0.7 6.5 %copy-start.5 = (bf16[192,96]{1,0:T(8,128)(2,1)S(1)}, bf16[192,96]{1,0:T(8,128)(2,1)}, u32[]{:S(2)}) copy-start(bf16[192,96]{1,0:T(8,128)(2,1)} %param.18) | copy-start | bytes 110596
  0.7 7.4 %copy-start.7 = (bf16[384]{0:T(512)(128)(2,1)S(1)}, bf16[384]{0:T(512)(128)(2,1)}, u32[]{:S(2)}) copy-start(bf16[384]{0:T(512)(128)(2,1)} %param.23) | copy-start | bytes 2308
  0.7 7.5 %copy-start.14 = (bf16[192]{0:T(256)(128)(2,1)S(1)}, bf16[192]{0:T(256)(128)(2,1)}, u32[]{:S(2)}) copy-start(bf16[192]{0:T(256)(128)(2,1)} %param.21) | copy-start | bytes 1156
  0.7 7.5 %copy-start.8 = (bf16[96]{0:T(256)(128)(2,1)S(1)}, bf16[96]{0:T(256)(128)(2,1)}, u32[]{:S(2)}) copy-start(bf16[96]{0:T(256)(128)(2,1)} %param.22) | copy-start | bytes 580
  0.7 7.5 %copy-start.9 = (bf16[96]{0:T(256)(128)(2,1)S(1)}, bf16[96]{0:T(256)(128)(2,1)}, u32[]{:S(2)}) copy-start(bf16[96]{0:T(256)(128)(2,1)} %param.24) | copy-start | bytes 580
  0.7 7.5 %copy-start.10 = (bf16[96]{0:T(256)(128)(2,1)S(1)}, bf16[96]{0:T(256)(128)(2,1)}, u32[]{:S(2)}) copy-start(bf16[96]{0:T(256)(128)(2,1)} %param.25) | copy-start | bytes 580
  0.7 7.5 %copy-start.11 = (bf16[96]{0:T(256)(128)(2,1)S(1)}, bf16[96]{0:T(256)(128)(2,1)}, u32[]{:S(2)}) copy-start(bf16[96]{0:T(256)(128)(2,1)} %param.26) | copy-start | bytes 580
  0.7 7.5 %copy-start.12 = (bf16[96]{0:T(256)(128)(2,1)S(1)}, bf16[96]{0:T(256)(128)(2,1)}, u32[]{:S(2)}) copy-start(bf16[96]{0:T(256)(128)(2,1)} %param.27) | copy-start | bytes 580
  0.7 7.5 %copy-start.13 = (bf16[96]{0:T(256)(128)(2,1)S(1)}, bf16[96]{0:T(256)(128)(2,1)}, u32[]{:S(2)}) copy-start(bf16[96]{0:T(256)(128)(2,1)} %param.28) | copy-start | bytes 580
  257.5 6.5 %copy-start.1 = (f32[2,192,192]{2,1,0:T(8,128)S(1)}, f32[2,192,192]{2,1,0:T(8,128)}, u32[]{:S(2)}) copy-start(f32[2,192,192]{2,1,0:T(8,128)} %get-tuple-element.63) | copy-start | bytes 884740
  257.5 7.4 %copy-start.6 = (f32[16,768]{1,0:T(8,128)S(1)}, f32[16,768]{1,0:T(8,128)}, u32[]{:S(2)}) copy-start(f32[16,768]{1,0:T(8,128)} %get-tuple-element.65) | copy-start | bytes 147460
  257.5 8.0 %copy-start.4 = (f32[2,48,192]{2,1,0:T(8,128)S(1)}, f32[2,48,192]{2,1,0:T(8,128)}, u32[]{:S(2)}) copy-start(f32[2,48,192]{2,1,0:T(8,128)} %get-tuple-element.62) | copy-start | bytes 221188
  257.5 10.0 %copy-start = (bf16[768,512]{1,0:T(8,128)(2,1)S(1)}, bf16[768,512]{1,0:T(8,128)(2,1)}, u32[]{:S(2)}) copy-start(bf16[768,512]{1,0:T(8,128)(2,1)} %get-tuple-element.46) | copy-start | bytes 2359300
  259.8 10.2 %copy-start.2 = (f32[2,48,768]{2,1,0:T(8,128)S(1)}, f32[2,48,768]{2,1,0:T(8,128)}, u32[]{:S(2)}) copy-start(f32[2,48,768]{2,1,0:T(8,128)} %get-tuple-element.64) | copy-start | bytes 884740

commit v6 on v5

--- a/solution.py
+++ b/solution.py
@@ -226,24 +226,16 @@
     )(scalars, q, kv, delta, lse, dout)
 
 
-def middle_kernel(
-    x_ref, cot_ref, scalars_ref, att_ref, w_out_in, w_up_in, w_down_in, cols_ref, bias_up_ref,
+def middle_body(
+    x_ref, cot_ref, scalars_ref, att_ref, w_out_ref, w_up_ref, w_down_ref, cols_ref, bias_up_ref,
     out_ref, dmid_ref, datt_ref, delta_ref, g_out_ref, g_up_out, g_down_out, sums_ref,
-    w_out_ref, w_up_ref, w_down_ref, g_up_ref, g_down_ref,
+    g_up_ref, g_down_ref,
     mid_ref, norm_ref, h_ref, dmlp_ref, mlp_ref, err_ref, attb_ref, dbranch_ref,
-    in_sem, up_sem, down_sem,
+    up_sem, down_sem, wait_out, wait_up, passes,
 ):
     width, tokens = x_ref.shape
     hidden = w_up_ref.shape[0]
     step = 256
-    loads = [
-        pltpu.make_async_copy(source, target, in_sem.at[k])
-        for k, (source, target) in enumerate(
-            ((w_out_in, w_out_ref), (w_up_in, w_up_ref), (w_down_in, w_down_ref))
-        )
-    ]
-    for copy in loads:
-        copy.start()
     first_slot = lax.broadcasted_iota(jnp.int32, (1, tokens), 1) < tokens // 2
     valid = jnp.where(
         first_slot,
@@ -255,7 +247,7 @@
     sums_ref[...] = jnp.zeros_like(sums_ref)
     mlp_ref[...] = jnp.zeros_like(mlp_ref)
     err_ref[...] = jnp.zeros_like(err_ref)
-    loads[0].wait()
+    wait_out()
 
     @pl.loop(0, width // step)
     def _(j):
@@ -269,8 +261,7 @@
     normed, inverse = normalize(mid_ref[...])
     norm_ref[...] = normed
     h_ref[...] = (normed * cols_ref[:, GAIN_TWO] + cols_ref[:, SHIFT_TWO]).astype(BF)
-    loads[1].wait()
-    loads[2].wait()
+    wait_up()
 
     def stores(j):
         rows = pl.ds(pl.multiple_of(j * step, step), step)
@@ -279,8 +270,7 @@
             pltpu.make_async_copy(g_down_ref.at[:, rows], g_down_out.at[:, rows], down_sem.at[j]),
         )
 
-    @pl.loop(0, hidden // step)
-    def _(j):
+    def block(j):
         rows = pl.ds(pl.multiple_of(j * step, step), step)
         pre = dg(w_up_ref[rows, :], h_ref[...], 1, 0) + bias_up_ref[rows, :]
         phi = 0.5 + 0.5 * lax.erf(pre * math.sqrt(0.5))
@@ -298,6 +288,13 @@
         for copy in stores(j):
             copy.start()
 
+    for wait, count, place in passes:
+        wait()
+
+        @pl.loop(0, count)
+        def _(t):
+            block(place(t))
+
     out_ref[...] = ((mid_ref[...] + mlp_ref[...] + cols_ref[:, BIAS_DOWN]) * valid).astype(BF)
     err = err_ref[...]
     sums_ref[3:4] = row_sums(dmlp_ref[...])[:1]
@@ -322,6 +319,26 @@
     def _(j):
         for copy in stores(j):
             copy.wait()
+
+
+def middle_kernel(*refs):
+    x_ref, cot_ref, scalars_ref, att_ref, w_out_in, w_up_in, w_down_in = refs[:7]
+    outputs = refs[7:17]
+    w_out_ref, w_up_ref, w_down_ref = refs[17:20]
+    scratch, in_sem = refs[20:30], refs[30]
+    loads = [
+        pltpu.make_async_copy(source, target, in_sem.at[k])
+        for k, (source, target) in enumerate(
+            ((w_out_in, w_out_ref), (w_up_in, w_up_ref), (w_down_in, w_down_ref))
+        )
+    ]
+    for copy in loads:
+        copy.start()
+    middle_body(
+        x_ref, cot_ref, scalars_ref, att_ref, w_out_ref, w_up_ref, w_down_ref, *outputs, *scratch,
+        *refs[31:], loads[0].wait, loads[1].wait,
+        [(loads[2].wait, w_up_ref.shape[0] // 256, lambda t: t)],
+    )
 
 
 def middle(x, cot, scalars, att, w_out, w_up, w_down, cols, bias_up):
@@ -530,13 +547,14 @@
 
 
 def front_kernel(
-    images, bands, scalars_ref, narrow_ref, wide_ref, small_ref, x_ref,
-    qkv_w_out, out_w_ref, up_w_ref, down_w_ref, h_out, kv_out, x_far_out,
-    q_ref, att_ref, lse_ref, cols_ref, up_col_ref,
-    qkv_w_ref, h_ref, kv_ref,
-    theirs_ref, mine_ref, mine_wide_ref, smalls_ref, qv_col_ref, bias_ref, x_far_ref,
-    local_sem, send_sem, recv_sem,
+    images, bands, scalars_ref, narrow_ref, wide_ref, small_ref, x_ref, cot_ref,
+    qkv_w_out, h_out, kv_out, x_far_out, q_ref, lse_ref, cols_ref, *rest,
 ):
+    results, rest = rest[:8], rest[8:]
+    qkv_w_ref, out_w_ref, up_w_ref, down_w_ref, h_ref, kv_ref, att_ref, up_col_ref = rest[:8]
+    theirs_ref, mine_ref, mine_wide_ref, smalls_ref, qv_col_ref, bias_ref, x_far_ref = rest[8:15]
+    local_sem, send_sem, recv_sem = rest[15:18]
+    middle_scratch = rest[18:]
     at = Place(images)
     width, tokens = x_ref.shape
     rows = tokens // 2
@@ -751,12 +769,35 @@
                 for action in actions:
                     action()
 
-    s_up[2].step(3)
-    s_out.step(3)
-    d_two.step(3)
-    d_one.step(3)
-    for item in s_up + [s_out, d_one, d_two]:
-        item.wait()
+    hidden = up_w_ref.shape[0] * 2 * up_w_ref.shape[2]
+    blocks = hidden // 256
+    quarter = blocks // 4
+
+    def wait_out():
+        s_out.step(3)
+        s_up[2].step(3)
+        s_out.wait()
+
+    def wait_up():
+        d_two.step(3)
+        for item in s_up:
+            item.wait()
+
+    def wait_one():
+        d_one.step(3)
+        d_one.wait()
+
+    def flat(ref):
+        return ref.reshape(ref.shape[0] * 2 * ref.shape[2], ref.shape[3])
+
+    middle_body(
+        x_ref, cot_ref, scalars_ref, att_ref, flat(out_w_ref), flat(up_w_ref), flat(down_w_ref),
+        cols_ref, up_col_ref, *results, *middle_scratch, wait_out, wait_up,
+        [
+            (d_two.wait, 2 * quarter, lambda t: t + t // quarter * quarter + quarter),
+            (wait_one, 2 * quarter, lambda t: t + t // quarter * quarter),
+        ],
+    )
     for item in s_qkv + s_up + [s_out, d_one, d_two]:
         item.end()
     for copy in [save_w, save_h, save_x] + save_kv:
@@ -767,45 +808,68 @@
         copy.wait_send()
 
 
-def front(images, bands, scalars, narrow, wide, small, x, widths):
+def front(images, bands, scalars, narrow, wide, small, x, cot, widths):
     depth = images // 2
     width, tokens = x.shape
     groups = GROUPS_OF_HEADS
     hidden = images * widths[2]
+    full = (width, tokens)
+    kv = (bands, groups, 2 * width // groups, tokens)
+    weights = [(depth, 2, w, width) for w in widths]
+    weights.append((depth, 2, wide.shape[0], 4 * wide.shape[1]))
     return pl.pallas_call(
         functools.partial(front_kernel, images, bands),
         name="front",
-        out_shape=tuple(shape((depth, 2, w, width), BF) for w in widths)
-        + (
-            shape((depth, 2, wide.shape[0], 4 * wide.shape[1]), BF),
+        out_shape=(
+            shape(weights[0], BF),
             shape((width, 2 * tokens), BF),
-            shape((bands, groups, 2 * width // groups, tokens), BF),
-            shape((width, tokens), BF),
-            shape((width, tokens), BF),
-            shape((width, tokens), F),
+            shape(kv, BF),
+            shape(full, BF),
+            shape(full, BF),
             shape((2 * HEADS, tokens // 2), F),
             shape((width, COLUMNS), F),
-            shape((hidden, 1), F),
+            shape(full, BF),
+            shape(full, F),
+            shape(full, BF),
+            shape((HEADS, tokens), F),
+            shape((width, width), BF),
+            shape((hidden, width), BF),
+            shape((width, hidden), BF),
+            shape((SUM_ROWS, width), F),
         ),
-        in_specs=[SM] + [VM] * 4,
-        out_specs=(ANY,) * 7 + (VM,) * 5,
-        scratch_shapes=[
-            pltpu.VMEM((depth, 2, widths[0], width), BF),
+        in_specs=[SM] + [VM] * 5,
+        out_specs=(ANY,) * 4 + (VM,) * 8 + (ANY, ANY, VM),
+        scratch_shapes=[pltpu.VMEM(s, BF) for s in weights]
+        + [
             pltpu.VMEM((width, 2 * tokens), BF),
-            pltpu.VMEM((bands, groups, 2 * width // groups, tokens), BF),
+            pltpu.VMEM(kv, BF),
+            pltpu.VMEM(full, F),
+            pltpu.VMEM((hidden, 1), F),
             pltpu.VMEM(narrow.shape[1:], BF),
             pltpu.VMEM((narrow.shape[1], 2 * narrow.shape[2]), BF),
             pltpu.VMEM((wide.shape[0] // 2, 2 * wide.shape[1]), BF),
             pltpu.VMEM((16 * images, 128), F),
             pltpu.VMEM((2 * width, 1), F),
             pltpu.VMEM((8, tokens // 2), F),
-            pltpu.VMEM((width, tokens), BF),
+            pltpu.VMEM(full, BF),
             pltpu.SemaphoreType.DMA((24,)),
             pltpu.SemaphoreType.DMA((FRONT_COPIES,)),
             pltpu.SemaphoreType.DMA((FRONT_COPIES,)),
+            pltpu.VMEM((hidden, width), BF),
+            pltpu.VMEM((width, hidden), BF),
+            pltpu.VMEM(full, F),
+            pltpu.VMEM(full, F),
+            pltpu.VMEM(full, BF),
+            pltpu.VMEM(full, BF),
+            pltpu.VMEM(full, F),
+            pltpu.VMEM(full, F),
+            pltpu.VMEM(full, BF),
+            pltpu.VMEM(full, BF),
+            pltpu.SemaphoreType.DMA((hidden // 256,)),
+            pltpu.SemaphoreType.DMA((hidden // 256,)),
         ],
         compiler_params=comm_params(0),
-    )(scalars, narrow, wide, small, x)
+    )(scalars, narrow, wide, small, x, cot)
 
 
 def share_kernel(images, kv_ref, all_ref, local_sem, send_sem, recv_sem):
@@ -1456,10 +1520,10 @@
         units = [jnp.stack(single), jnp.zeros((4, unit), BF)]
         units += [bias_qv.reshape(2, unit), bias_up.reshape(4, unit)]
         small = jnp.pad(jnp.concatenate(units), ((0, 0), (0, 128 - unit))).astype(F)
-        *full, h, all_kv, x_far, q, att, lse, cols, c_up = front(
-            images, bands, scalars, narrow, w_down.T, small, x, widths
+        full_qkv, h, all_kv, x_far, q, lse, cols, *rest = front(
+            images, bands, scalars, narrow, w_down.T, small, x, cot, widths
         )
-        full_qkv, full_out, full_up, full_down = (item.reshape(-1, item.shape[3]) for item in full)
+        full_qkv = full_qkv.reshape(-1, width)
     else:
         full_qkv, full_out, full_up, full_down = (
             lax.all_gather(lax.all_gather(item, "band", axis=0, tiled=True).T, "img", tiled=True)
@@ -1476,9 +1540,8 @@
         all_kv = all_kv.reshape(bands, 2, GROUPS_OF_HEADS, -1, count).transpose(0, 2, 1, 3, 4)
         all_kv = all_kv.reshape(bands, GROUPS_OF_HEADS, -1, count)
         att, lse = attend(scalars, q, all_kv)
-    out, dmid, datt, delta, g_out, g_up, g_down, sums = middle(
-        x, cot, scalars, att, full_out, full_up, full_down, cols, c_up
-    )
+        rest = middle(x, cot, scalars, att, full_out, full_up, full_down, cols, c_up)
+    out, dmid, datt, delta, g_out, g_up, g_down, sums = rest
     if direct:
         gx, *pieces, total = back(
             images, bands, scalars, q, all_kv, delta, lse, datt, x, x_far, h, dmid,

time: 271 us -> 267 us (0.985)
  Pallas kernels: 245 us -> 236 us
  local copies, waits for them, and re-layouts: 22.5 us -> 26.8 us
    pallas_call x1 -> x0, Pallas kernels: 34.2 us -> none  [middle(): pl.pallas_call(middle_kernel, name='middle', out_shape=(shape(full, BF),...]
    pallas_call x1, Pallas kernels: 96.3 us -> 123 us  [front(): pl.pallas_call(functools.partial(front_kernel, images, bands), name='fron...]
where the time goes in v6:
time: 267 us; the launch traced here: 266 us
  Pallas kernels  236 us (88%)
  local copies, waits for them, and re-layouts  26.8 us (10%)
  other arithmetic  2.75 us (1%)
    pallas_call x1, Pallas kernels, front(): pl.pallas_call(functools.partial(front_kernel, images, bands), name='fron...  123 us
    pallas_call x1, Pallas kernels, back(): pl.pallas_call(functools.partial(back_kernel, images, bands), name='back'...  113 us
    reshape x4, local copies, waits for them, and re-layouts, turn_back(): return values.reshape(width, slots, rows).transpose(2, 1, 0)[None]  9.16 us

profile of v6, /device:TPU:0, one launch (start us, length us, event | category | flops | bytes accessed | tf_op | source)
XLA Modules:
  0.0 266.1 jit_solution(1096240974082587554)
XLA Ops:
  0.6 0.0 copy-start
  0.7 1.3 pad_add_fusion.scalars_ref
  2.0 1.0 copy.31
  3.0 0.9 copy.30
  3.9 1.0 copy.29
  4.9 0.8 pad_maximum_fusion.narrow_ref
  5.8 0.7 reshape.76
  6.5 0.8 reshape.77
  7.3 0.9 concatenate.11
  8.2 0.6 pad_convert_fusion.small_ref
  8.8 2.8 %copy.32 = bf16[768,2,256]{2,1,0:T(2,128)(2,1)S(1)} copy(bf16[768,2,256]{0,1,2:T(2,128)(2,1)} %bitcast.47) | data formatting | bytes 1572864 | tf_op jit(solution)/shard_map/transpose | solution.py:1508
  11.6 1.1 copy.39
  12.6 0.0 copy-done
  12.6 1.3 copy.33
  14.0 1.1 copy.40
  15.0 122.8 %front.1 = (bf16[4,2,288,768]{3,2,1,0:T(8,128)(2,1)}, bf16[768,1024]{1,0:T(8,128)(2,1)}, bf16[4,4,384,512]{3,2,1,0:T(8,128)(2,1)}, bf16[768,512]{1,0:T(8,128)(2,...) custom-call(s32[3]{0:T(128)} %pad_add_fusion.scalars_ref, ...), custom_call_target="tpu_custom_call" | custom-call | tf_op jit(solution)/shard_map/front/pallas_call | solution.py:820
  137.8 2.2 reshape.80
  140.0 2.3 copy.34
  142.3 113.1 %back.1 = (bf16[768,512]{1,0:T(8,128)(2,1)}, f32[2,144,192]{2,1,0:T(8,128)}, f32[2,48,192]{2,1,0:T(8,128)}, f32[2,192,192]{2,1,0:T(8,128)}, f32[2,48,768]{2,1,0:T(8,128)}, /*index=5*/f32[16,768]{1,0:T(8,128)}) custom-call(s32[3]{0:T(128)} %pad_add_fusion.scalars_ref, bf16[768,512]{1,0:T(8,128)(2,1)} %get-tuple-element.36.q_ref, ...), custom_call_target="tpu_custom_call" | custom-call | tf_op jit(solution)/shard_map/back/pallas_call | solution.py:1440
  255.4 0.0 copy-start.3
  255.4 0.0 copy-start.1
  255.4 0.0 copy-start.4
  255.5 0.0 copy-start.2
  255.5 2.3 reshape.82
  257.8 2.3 copy.35
  260.1 1.8 copy.36
  261.9 0.0 copy-done.3
  261.9 0.7 copy.37
  262.7 0.0 copy-done.1
  262.7 0.9 copy.38
  263.5 0.0 copy-done.4
  263.5 0.6 dynamic_slice.24
  264.2 0.6 fusion
  264.8 0.7 dynamic_slice.26
  265.4 0.0 copy-done.2
  265.4 0.7 copy.42
  (2 shorter events, 0.0 us)
Async XLA Ops:
  0.6 12.0 %copy-start = (bf16[1,256,2,768]{3,2,1,0:T(2,128)(2,1)S(1)}, bf16[1,256,2,768]{3,2,1,0:T(2,128)(2,1)}, u32[]{:S(2)}) copy-start(bf16[1,256,2,768]{3,2,1,0:T(2,128)(2,1)} %param.29) | copy-start | bytes 2359300
  255.4 6.5 %copy-start.3 = (f32[2,48,192]{2,1,0:T(8,128)S(1)}, f32[2,48,192]{2,1,0:T(8,128)}, u32[]{:S(2)}) copy-start(f32[2,48,192]{2,1,0:T(8,128)} %get-tuple-element.52) | copy-start | bytes 221188
  255.4 7.2 %copy-start.1 = (f32[2,192,192]{2,1,0:T(8,128)S(1)}, f32[2,192,192]{2,1,0:T(8,128)}, u32[]{:S(2)}) copy-start(f32[2,192,192]{2,1,0:T(8,128)} %get-tuple-element.53) | copy-start | bytes 884740
  255.4 8.1 %copy-start.4 = (f32[16,768]{1,0:T(8,128)S(1)}, f32[16,768]{1,0:T(8,128)}, u32[]{:S(2)}) copy-start(f32[16,768]{1,0:T(8,128)} %get-tuple-element.55) | copy-start | bytes 147460
  255.5 10.0 %copy-start.2 = (f32[2,48,768]{2,1,0:T(8,128)S(1)}, f32[2,48,768]{2,1,0:T(8,128)}, u32[]{:S(2)}) copy-start(f32[2,48,768]{2,1,0:T(8,128)} %get-tuple-element.54) | copy-start | bytes 884740

commit v7 on v6

--- a/solution.py
+++ b/solution.py
@@ -89,7 +89,7 @@
 def fill_bias(scalars_ref, bias_ref, rows):
     lane_half = lax.broadcasted_iota(jnp.int32, (1, rows), 1) // (rows // 2)
     for s in range(2):
-        small = scalars_ref[s] == 2
+        small = scalars_ref[0, s] == 2
         for other in range(2):
             for half in range(2):
                 keep = jnp.logical_and(other == 0, lane_half == half)
@@ -150,7 +150,7 @@
     def _(j):
         for k in range(unroll):
             attend_step(
-                j * unroll + k, scalars_ref[2], q_ref, kv_ref, bias_ref, out_ref, lse_ref
+                j * unroll + k, scalars_ref[0, 2], q_ref, kv_ref, bias_ref, out_ref, lse_ref
             )
 
 
@@ -209,7 +209,7 @@
                 dkv_ref[b, second, lanes] = values
 
             attend_back_step(
-                i, scalars_ref[2], q_ref, kv_ref, delta_ref, lse_ref, dout_ref, bias_ref, dq_ref,
+                i, scalars_ref[0, 2], q_ref, kv_ref, delta_ref, lse_ref, dout_ref, bias_ref, dq_ref,
                 put_key, put_value,
             )
 
@@ -239,8 +239,8 @@
     first_slot = lax.broadcasted_iota(jnp.int32, (1, tokens), 1) < tokens // 2
     valid = jnp.where(
         first_slot,
-        jnp.where(scalars_ref[0] > 0, 1.0, 0.0),
-        jnp.where(scalars_ref[1] > 0, 1.0, 0.0),
+        jnp.where(scalars_ref[0, 0] > 0, 1.0, 0.0),
+        jnp.where(scalars_ref[0, 1] > 0, 1.0, 0.0),
     )
     attb_ref[...] = att_ref[...].astype(BF)
     dmlp_ref[...] = (cot_ref[...].astype(F) * valid).astype(BF)
@@ -295,7 +295,8 @@
         def _(t):
             block(place(t))
 
-    out_ref[...] = ((mid_ref[...] + mlp_ref[...] + cols_ref[:, BIAS_DOWN]) * valid).astype(BF)
+    out = (mid_ref[...] + mlp_ref[...] + cols_ref[:, BIAS_DOWN]) * valid
+    out_ref[...] = out.T.astype(BF)
     err = err_ref[...]
     sums_ref[3:4] = row_sums(dmlp_ref[...])[:1]
     sums_ref[6:7] = row_sums(err * norm_ref[...])[:1]
@@ -350,7 +351,7 @@
         middle_kernel,
         name="middle",
         out_shape=(
-            shape(full, BF),
+            shape((tokens, width), BF),
             shape(full, F),
             shape(full, BF),
             shape((HEADS, tokens), F),
@@ -402,7 +403,8 @@
     sums_ref[1:2] = row_sums(dkv_ref[pl.ds(width, width), :])[:1]
     sums_ref[4:5] = row_sums(err * normed)[:1]
     sums_ref[5:6] = row_sums(err)[:1]
-    gx_ref[...] = (dmid_ref[...] + norm_back(err, normed, inverse, cols_ref[:, GAIN_ONE])).astype(BF)
+    grad = dmid_ref[...] + norm_back(err, normed, inverse, cols_ref[:, GAIN_ONE])
+    gx_ref[...] = grad.T.astype(BF)
 
 
 def finish(x, h, dq, dkv, w, cols, dmid):
@@ -410,7 +412,7 @@
     return pl.pallas_call(
         finish_kernel,
         name="finish",
-        out_shape=(shape(x.shape, BF), shape(w.shape, BF), shape((SUM_ROWS, width), F)),
+        out_shape=(shape((tokens, width), BF), shape(w.shape, BF), shape((SUM_ROWS, width), F)),
         in_specs=[VM] * 7,
         out_specs=(VM, VM, VM),
         scratch_shapes=[pltpu.VMEM(x.shape, F)],
@@ -459,12 +461,6 @@
 def comm_params(collective_id):
     return pltpu.CompilerParams(
         collective_id=collective_id, has_side_effects=True, vmem_limit_bytes=LIMIT
-    )
-
-
-def split_rows(shards, parts):
-    return jnp.concatenate(
-        [item.reshape(parts, item.shape[0] // parts, item.shape[1]) for item in shards], axis=1
     )
 
 
@@ -547,10 +543,13 @@
 
 
 def front_kernel(
-    images, bands, scalars_ref, narrow_ref, wide_ref, small_ref, x_ref, cot_ref,
-    qkv_w_out, h_out, kv_out, x_far_out, q_ref, lse_ref, cols_ref, *rest,
+    images, bands, scalars_ref, shard_qkv_ref, shard_out_ref, shard_up_ref, shard_down_ref,
+    small_ref, tokens_ref, cot_tokens_ref,
+    qkv_w_out, h_out, kv_out, x_out, x_far_out, q_ref, lse_ref, cols_ref, *rest,
 ):
     results, rest = rest[:8], rest[8:]
+    narrow_ref, wide_ref, x_ref, cot_ref, far_tokens_ref = rest[:5]
+    rest = rest[5:]
     qkv_w_ref, out_w_ref, up_w_ref, down_w_ref, h_ref, kv_ref, att_ref, up_col_ref = rest[:8]
     theirs_ref, mine_ref, mine_wide_ref, smalls_ref, qv_col_ref, bias_ref, x_far_ref = rest[8:15]
     local_sem, send_sem, recv_sem = rest[15:18]
@@ -613,16 +612,17 @@
 
     s_qkv = spread(qkv_w_ref, sources[0], ("mixed",) * 3)
     (s_out,) = spread(out_w_ref, sources[1], ("mixed",))
-    s_up = spread(up_w_ref, sources[2], ("mixed", "zxy", "zxy"))
+    s_up = spread(up_w_ref, sources[2], ("mixed", "mixed", "zxy"))
     d_one, d_two = spread(down_w_ref, sources[3], ("xyz", "mixed"))
     save_w = pltpu.make_async_copy(qkv_w_ref, qkv_w_out, local())
     save_h = pltpu.make_async_copy(h_ref, h_out, local())
-    save_x = pltpu.make_async_copy(x_far_ref, x_far_out, local())
+    save_x = pltpu.make_async_copy(x_ref, x_out, local())
+    save_far = pltpu.make_async_copy(x_far_ref, x_far_out, local())
     save_kv = [
         pltpu.make_async_copy(kv_ref.at[:, g], kv_out.at[:, g], local()) for g in range(groups)
     ]
     x_lanes = [pl.ds(s * rows, rows) for s in range(2)]
-    x_moves = [make(x_ref.at[:, l], x_far_ref.at[:, l], at.across_x) for l in x_lanes]
+    x_moves = [make(tokens_ref.at[l], far_tokens_ref.at[l], at.across_x) for l in x_lanes]
     far = at.across_x[1]
     kv_moves = [
         [
@@ -635,9 +635,17 @@
         for s in range(2)
     ]
 
+    row = 0
+    for ref in (shard_qkv_ref, shard_out_ref, shard_up_ref):
+        turned = ref[...].astype(F).T.astype(BF)
+        count = turned.shape[0] // 2
+        for core in range(2):
+            narrow_ref[core, pl.ds(row, count), :] = turned[core * count : (core + 1) * count]
+        row += count
+    wide_ref[...] = shard_down_ref[...].astype(F).T.astype(BF)
     greet([at.partner, at.across_x] + others)
+    x_moves[0].start()
     swap.start()
-    x_moves[0].start()
     own_wide.start()
     swap_wide.start()
     keep_small.start()
@@ -654,10 +662,15 @@
     own_wide.wait()
     swap_wide.wait_recv()
     d_one.start()
+    s_out.start()
     for item in s_up:
         item.start()
     d_two.start()
-    s_out.start()
+
+    for s in range(2):
+        x_ref[:, x_lanes[s]] = tokens_ref[x_lanes[s], :].astype(F).T.astype(BF)
+        cot_ref[:, x_lanes[s]] = cot_tokens_ref[x_lanes[s], :].astype(F).T.astype(BF)
+    save_x.start()
 
     keep_small.wait()
     for copy in small_copies:
@@ -675,6 +688,10 @@
             lane = singles + qv_units + u
             up_col_ref[pl.ds(unit * (up_units * j + u), unit), :] = block[:, lane : lane + 1]
 
+    def far_tokens(s):
+        x_moves[s].wait_recv()
+        x_far_ref[:, x_lanes[s]] = far_tokens_ref[x_lanes[s], :].astype(F).T.astype(BF)
+
     def first_norm(s, ref, side):
         normed, _ = normalize(ref[:, x_lanes[s]].astype(F))
         to = pl.ds(side * tokens + s * rows, rows)
@@ -692,12 +709,15 @@
     s_qkv[0].step(3)
     s_qkv[2].step(2)
     x_moves[1].start()
-    x_moves[0].wait_recv()
+    s_out.step(1)
+    far_tokens(0)
     first_norm(0, x_far_ref, 1)
     s_qkv[1].step(3)
-    s_qkv[2].step(3)
     s_up[0].step(1)
     s_up[1].step(1)
+    s_qkv[2].step(3)
+    s_up[2].step(1)
+    d_two.step(1)
     for item in s_qkv:
         item.wait()
     save_w.start()
@@ -724,11 +744,11 @@
             q_ref[block, x_lanes[s]] = (out * scale).astype(BF)
 
     def second_slot():
-        x_moves[1].wait_recv()
+        far_tokens(1)
         first_norm(1, x_far_ref, 1)
         project(1)
         save_h.start()
-        save_x.start()
+        save_far.start()
 
     def arrive(s, g):
         for copy in kv_moves[s][g]:
@@ -741,16 +761,16 @@
     def when(j, *actions):
         events.setdefault(j, []).extend(actions)
 
-    when(1, functools.partial(s_up[2].step, 1))
     when(2, second_slot)
     for j in range(1, 2 * groups):
         when(j - 1, functools.partial(arrive, j // groups, j % groups))
+    when(0, functools.partial(s_out.step, 2))
     when(1, functools.partial(s_up[0].step, 2))
-    when(2, functools.partial(d_two.step, 1), functools.partial(s_out.step, 1))
-    when(4, functools.partial(s_up[1].step, 2))
-    when(5, functools.partial(s_up[2].step, 2))
-    when(6, functools.partial(s_up[0].step, 3), functools.partial(s_out.step, 2))
-    when(7, functools.partial(d_two.step, 2), functools.partial(s_up[1].step, 3))
+    when(3, functools.partial(s_up[1].step, 2), functools.partial(s_out.step, 3))
+    when(4, functools.partial(s_up[2].step, 2))
+    when(5, functools.partial(d_two.step, 2))
+    when(6, functools.partial(s_up[0].step, 3))
+    when(7, functools.partial(s_up[1].step, 3))
     project(0)
     arrive(0, 0)
     unroll = HEADS // groups
@@ -774,7 +794,6 @@
     quarter = blocks // 4
 
     def wait_out():
-        s_out.step(3)
         s_up[2].step(3)
         s_out.wait()
 
@@ -800,7 +819,7 @@
     )
     for item in s_qkv + s_up + [s_out, d_one, d_two]:
         item.end()
-    for copy in [save_w, save_h, save_x] + save_kv:
+    for copy in [save_w, save_h, save_x, save_far] + save_kv:
         copy.wait()
     for copy in [swap, swap_wide] + small_copies + x_moves:
         copy.wait_send()
@@ -808,15 +827,19 @@
         copy.wait_send()
 
 
-def front(images, bands, scalars, narrow, wide, small, x, cot, widths):
+def front(images, bands, scalars, shards, small, tokens_by_slot, cot_by_slot):
     depth = images // 2
-    width, tokens = x.shape
+    tokens, width = tokens_by_slot.shape
     groups = GROUPS_OF_HEADS
+    widths = [item.shape[1] for item in shards[:3]]
     hidden = images * widths[2]
     full = (width, tokens)
+    part = shards[0].shape[0]
+    narrow = (2, sum(widths) // 2, part)
+    wide = (shards[3].shape[1], shards[3].shape[0])
     kv = (bands, groups, 2 * width // groups, tokens)
     weights = [(depth, 2, w, width) for w in widths]
-    weights.append((depth, 2, wide.shape[0], 4 * wide.shape[1]))
+    weights.append((depth, 2, wide[0], 4 * wide[1]))
     return pl.pallas_call(
         functools.partial(front_kernel, images, bands),
         name="front",
@@ -826,9 +849,10 @@
             shape(kv, BF),
             shape(full, BF),
             shape(full, BF),
+            shape(full, BF),
             shape((2 * HEADS, tokens // 2), F),
             shape((width, COLUMNS), F),
-            shape(full, BF),
+            shape((tokens, width), BF),
             shape(full, F),
             shape(full, BF),
             shape((HEADS, tokens), F),
@@ -837,17 +861,18 @@
             shape((width, hidden), BF),
             shape((SUM_ROWS, width), F),
         ),
-        in_specs=[SM] + [VM] * 5,
-        out_specs=(ANY,) * 4 + (VM,) * 8 + (ANY, ANY, VM),
-        scratch_shapes=[pltpu.VMEM(s, BF) for s in weights]
+        in_specs=[SM] + [VM] * 7,
+        out_specs=(ANY,) * 5 + (VM,) * 8 + (ANY, ANY, VM),
+        scratch_shapes=[pltpu.VMEM(s, BF) for s in (narrow, wide, full, full, (tokens, width))]
+        + [pltpu.VMEM(s, BF) for s in weights]
         + [
             pltpu.VMEM((width, 2 * tokens), BF),
             pltpu.VMEM(kv, BF),
             pltpu.VMEM(full, F),
             pltpu.VMEM((hidden, 1), F),
-            pltpu.VMEM(narrow.shape[1:], BF),
-            pltpu.VMEM((narrow.shape[1], 2 * narrow.shape[2]), BF),
-            pltpu.VMEM((wide.shape[0] // 2, 2 * wide.shape[1]), BF),
+            pltpu.VMEM(narrow[1:], BF),
+            pltpu.VMEM((narrow[1], 2 * narrow[2]), BF),
+            pltpu.VMEM((wide[0] // 2, 2 * wide[1]), BF),
             pltpu.VMEM((16 * images, 128), F),
             pltpu.VMEM((2 * width, 1), F),
             pltpu.VMEM((8, tokens // 2), F),
@@ -869,7 +894,7 @@
             pltpu.SemaphoreType.DMA((hidden // 256,)),
         ],
         compiler_params=comm_params(0),
-    )(scalars, narrow, wide, small, x, cot)
+    )(scalars, *shards, small, tokens_by_slot, cot_by_slot)
 
 
 def share_kernel(images, kv_ref, all_ref, local_sem, send_sem, recv_sem):
@@ -1365,7 +1390,6 @@
     small_ref[0, 5:6] = shift_row + row_sums(err_ref[...])[:1]
     small_steps[0].start()
     qkv[0].step_two()
-    err_moves[1].start()
     for item in down:
         item.step_four()
     deliver(0)
@@ -1373,6 +1397,7 @@
     small_ref[1] = small_ref[0] + small_in_ref[0]
     small_steps[1].start()
     qkv[1].step_two()
+    err_moves[1].start()
     qkv[0].step_three()
     small_steps[1].wait_recv()
     small_ref[2] = small_ref[1] + small_in_ref[1]
@@ -1393,9 +1418,8 @@
         lanes = slice(s * rows, (s + 1) * rows)
         err = err_ref[:, lanes] + err_in_ref[s].astype(F)
         normed, inverse = normalize(x_ref[:, lanes].astype(F))
-        gx_ref[:, lanes] = (
-            dmid_ref[:, lanes] + norm_back(err, normed, inverse, cols_ref[:, GAIN_ONE])
-        ).astype(BF)
+        grad = dmid_ref[:, lanes] + norm_back(err, normed, inverse, cols_ref[:, GAIN_ONE])
+        gx_ref[lanes, :] = grad.T.astype(BF)
 
     finish_slot(0)
     qkv[0].step_four()
@@ -1440,7 +1464,7 @@
     return pl.pallas_call(
         functools.partial(back_kernel, images, bands),
         name="back",
-        out_shape=(shape(x.shape, BF), results[3], results[2], results[1], results[0], shape(small, F)),
+        out_shape=(shape((tokens, width), BF), results[3], results[2], results[1], results[0], shape(small, F)),
         in_specs=[SM] + [VM] * 6 + [ANY] * 9,
         out_specs=(VM,) * 6,
         scratch_shapes=[
@@ -1504,27 +1528,30 @@
     direct = direct and bias_qv.shape[0] == 2 * (width // images) <= 256
     direct = direct and bias_up.shape[0] == 4 * (width // images)
 
+    def by_slot(values):
+        return values[0].transpose(1, 0, 2).reshape(count, width)
+
     def turn(values):
-        return values[0].transpose(2, 1, 0).reshape(width, count)
+        return by_slot(values).T
 
     def turn_back(values):
-        return values.reshape(width, slots, rows).transpose(2, 1, 0)[None]
-
-    x, cot = turn(tokens), turn(cotangent)
-    kinds = slot_kind[0].astype(jnp.int32)
-    scalars = jnp.concatenate([kinds, (band // 2).astype(jnp.int32)[None]])
+        return values.reshape(slots, rows, width).transpose(1, 0, 2)[None]
+
+    scalars = slot_kind
     single = (bias_out, bias_down, gain_one, shift_one, gain_two, shift_two)
     if direct:
-        narrow = split_rows([item.T for item in own], 2)
         unit = width // images
-        units = [jnp.stack(single), jnp.zeros((4, unit), BF)]
-        units += [bias_qv.reshape(2, unit), bias_up.reshape(4, unit)]
-        small = jnp.pad(jnp.concatenate(units), ((0, 0), (0, 128 - unit))).astype(F)
-        full_qkv, h, all_kv, x_far, q, lse, cols, *rest = front(
-            images, bands, scalars, narrow, w_down.T, small, x, cot, widths
+        pieces = list(single) + [jnp.zeros((unit,), BF)] * 4
+        for item in (bias_qv, bias_up):
+            pieces += [item[k : k + unit] for k in range(0, item.shape[0], unit)]
+        small = jnp.stack([jnp.pad(item, (0, 128 - unit)) for item in pieces]).astype(F)
+        full_qkv, h, all_kv, x, x_far, q, lse, cols, *rest = front(
+            images, bands, scalars, (*own, w_down), small, by_slot(tokens), by_slot(cotangent)
         )
         full_qkv = full_qkv.reshape(-1, width)
     else:
+        scalars = jnp.concatenate([slot_kind, jnp.full((1, 1), band // 2, jnp.int32)], axis=1)
+        x, cot = turn(tokens), turn(cotangent)
         full_qkv, full_out, full_up, full_down = (
             lax.all_gather(lax.all_gather(item, "band", axis=0, tiled=True).T, "img", tiled=True)
             for item in (*own, w_down)

time: 267 us -> 257 us (0.963)
  Pallas kernels: 236 us -> 230 us
    pallas_call x1, Pallas kernels: 113 us -> 105 us  [back(): pl.pallas_call(functools.partial(back_kernel, images, bands), name='back'...]
    reshape x6 -> x2, local copies, waits for them, and re-layouts: 10.7 us -> 5.64 us  [turn_back(): return values.reshape(slots, rows, width).transpose(1, 0, 2)[None]]
    transpose x5 -> x2, local copies, waits for them, and re-layouts: 7.07 us -> 4.18 us  [by_slot(): return values[0].transpose(1, 0, 2).reshape(count, width)]
where the time goes in v7:
time: 257 us
  Pallas kernels  230 us (89%)
  local copies, waits for them, and re-layouts  25 us (10%)
    pallas_call x1, Pallas kernels, front(): pl.pallas_call(functools.partial(front_kernel, images, bands), name='fron...  125 us
    pallas_call x1, Pallas kernels, back(): pl.pallas_call(functools.partial(back_kernel, images, bands), name='back'...  105 us
    reshape x2, local copies, waits for them, and re-layouts, turn_back(): return values.reshape(slots, rows, width).transpose(1, 0, 2)[None]  5.64 us
    reshape x3, local copies, waits for them, and re-layouts, body(): matrices = [item.reshape(-1, item.shape[2]).T for item in pieces]  5.32 us

profile of v7, /device:TPU:0, one launch (start us, length us, event | category | flops | bytes accessed | tf_op | source)
XLA Modules:
  0.0 256.6 jit_solution(15888262487272863072)
XLA Ops:
  0.6 1.7 copy.31.shard_down_ref
  2.4 0.7 pad_bitcast_fusion.9
  3.0 0.7 pad_bitcast_fusion.7
  3.7 0.7 pad_bitcast_fusion.5
  4.4 0.7 slice.21
  5.1 0.9 fusion.1
  6.0 0.7 select_bitcast_fusion
  6.7 0.1 stack.58
  6.8 0.6 convert_element_type.20.small_ref
  7.4 2.1 copy.29
  9.5 2.1 copy.30
  11.6 125.0 %front.1 = (bf16[4,2,288,768]{3,2,1,0:T(8,128)(2,1)}, bf16[768,1024]{1,0:T(8,128)(2,1)}, bf16[4,4,384,512]{3,2,1,0:T(8,128)(2,1)}, bf16[768,512]{1,0:T(8,128)(2,...) custom-call(s32[1,2]{1,0:T(1,128)} %scalars_ref.3, ...), custom_call_target="tpu_custom_call" | custom-call | tf_op jit(solution)/shard_map/front/pallas_call | solution.py:843
  136.6 2.8 %copy.40 = bf16[2,256,768]{2,0,1:T(2,128)(2,1)} copy(bf16[2,256,768]{2,1,0:T(8,128)(2,1)} %bitcast.64) | data formatting | bytes 1572864 | tf_op jit(solution)/shard_map/reshape | solution.py:1538
  139.4 104.6 %back.1 = (bf16[512,768]{1,0:T(8,128)(2,1)}, f32[2,144,192]{2,1,0:T(8,128)}, f32[2,48,192]{2,1,0:T(8,128)}, f32[2,192,192]{2,1,0:T(8,128)}, f32[2,48,768]{2,1,0:T(8,128)}, /*index=5*/f32[16,768]{1,0:T(8,128)}) custom-call(s32[1,2]{1,0:T(1,128)} %scalars_ref.3, bf16[768,512]{1,0:T(8,128)(2,1)} %get-tuple-element.37.q_ref, ...), custom_call_target="tpu_custom_call" | custom-call | tf_op jit(solution)/shard_map/back/pallas_call | solution.py:1464
  244.0 2.8 %copy.39 = bf16[2,256,768]{2,0,1:T(2,128)(2,1)} copy(bf16[2,256,768]{2,1,0:T(8,128)(2,1)} %bitcast.63) | data formatting | bytes 1572864 | tf_op jit(solution)/shard_map/reshape | solution.py:1538
  246.9 1.8 copy.34
  248.7 1.6 copy.35
  250.3 1.9 copy.36
  252.2 0.8 reshape.67
  253.0 0.6 dynamic_slice.24
  253.6 0.6 fusion
  254.2 0.7 dynamic_slice.26
  254.9 1.7 copy.42
  (3 shorter events, 0.0 us)

commit v8 on v7

--- a/solution.py
+++ b/solution.py
@@ -612,8 +612,8 @@
 
     s_qkv = spread(qkv_w_ref, sources[0], ("mixed",) * 3)
     (s_out,) = spread(out_w_ref, sources[1], ("mixed",))
-    s_up = spread(up_w_ref, sources[2], ("mixed", "mixed", "zxy"))
-    d_one, d_two = spread(down_w_ref, sources[3], ("xyz", "mixed"))
+    s_up = spread(up_w_ref, sources[2], ("mixed", "mixed", "mixed"))
+    d_one, d_two = spread(down_w_ref, sources[3], ("mixed", "mixed"))
     save_w = pltpu.make_async_copy(qkv_w_ref, qkv_w_out, local())
     save_h = pltpu.make_async_copy(h_ref, h_out, local())
     save_x = pltpu.make_async_copy(x_ref, x_out, local())
@@ -645,6 +645,7 @@
     wide_ref[...] = shard_down_ref[...].astype(F).T.astype(BF)
     greet([at.partner, at.across_x] + others)
     x_moves[0].start()
+    x_moves[1].start()
     swap.start()
     own_wide.start()
     swap_wide.start()
@@ -661,11 +662,11 @@
         item.start()
     own_wide.wait()
     swap_wide.wait_recv()
-    d_one.start()
     s_out.start()
     for item in s_up:
         item.start()
     d_two.start()
+    d_one.start()
 
     for s in range(2):
         x_ref[:, x_lanes[s]] = tokens_ref[x_lanes[s], :].astype(F).T.astype(BF)
@@ -699,16 +700,13 @@
 
     s_qkv[0].step(1)
     s_qkv[1].step(1)
-    d_one.step(1)
     s_qkv[0].step(2)
     s_qkv[2].step(1)
     for s in range(2):
         first_norm(s, x_ref, 0)
     s_qkv[1].step(2)
-    d_one.step(2)
     s_qkv[0].step(3)
     s_qkv[2].step(2)
-    x_moves[1].start()
     s_out.step(1)
     far_tokens(0)
     first_norm(0, x_far_ref, 1)
@@ -720,6 +718,7 @@
     d_two.step(1)
     for item in s_qkv:
         item.wait()
+    d_one.step(1)
     save_w.start()
 
     weights = qkv_w_ref.reshape(3 * width, width)
@@ -766,9 +765,10 @@
         when(j - 1, functools.partial(arrive, j // groups, j % groups))
     when(0, functools.partial(s_out.step, 2))
     when(1, functools.partial(s_up[0].step, 2))
-    when(3, functools.partial(s_up[1].step, 2), functools.partial(s_out.step, 3))
-    when(4, functools.partial(s_up[2].step, 2))
-    when(5, functools.partial(d_two.step, 2))
+    when(2, functools.partial(s_up[1].step, 2))
+    when(3, functools.partial(s_up[2].step, 2), functools.partial(s_out.step, 3))
+    when(4, functools.partial(d_two.step, 2))
+    when(5, functools.partial(d_one.step, 2))
     when(6, functools.partial(s_up[0].step, 3))
     when(7, functools.partial(s_up[1].step, 3))
     project(0)
@@ -1142,7 +1142,8 @@
 def back_kernel(
     images, bands, scalars_ref, q_ref, delta_ref, lse_ref, datt_ref, cols_ref, sums_ref,
     kv_in, x_in, x_far_in, h_in, dmid_in, w_in, g_out_ref, g_up_ref, g_down_ref,
-    gx_ref, p_qkv_ref, p_out_ref, p_up_ref, p_down_ref, total_ref,
+    gx_ref, o_qkv_ref, o_out_ref, o_up_ref, o_down_ref, total_ref,
+    p_down_ref, p_up_ref, p_out_ref, p_qkv_ref,
     kv_ref, x_ref, x_far_ref, h_ref, dmid_ref, w_ref,
     bias_ref, dq_ref, dwide_ref, dkv_ref, near_ref, g_qkv_ref, err_ref, err_far_ref, err_in_ref,
     small_ref, small_in_ref, small_z_ref, *rest,
@@ -1432,8 +1433,9 @@
     qkv[1].step_four()
     deliver(3)
     finish_slot(1)
-    for m in range(4):
+    for m, ref in enumerate((o_down_ref, o_up_ref, o_out_ref, o_qkv_ref)):
         ends[m][3].wait()
+        ref[...] = jnp.concatenate([targets[m][k] for k in range(2)], axis=0).T
         for item in moves[m]:
             item.end()
     for copy in sum(swaps, []) + one + two + err_moves + small_steps + small_last:
@@ -1447,10 +1449,11 @@
     width, tokens = x.shape
     g_out, g_up, g_down = grads
     groups = HEADS // 4
-    results, buffers = [], []
+    results, placed, buffers = [], [], []
     for m, item in enumerate((g_down, g_up, g_out, w)):
         block, lanes = item.shape[0] // images // 2, item.shape[1]
-        results.append(shape((2, block, lanes // 4), F))
+        results.append(shape((lanes // 4, 2 * block), F))
+        placed.append(pltpu.VMEM((2, block, lanes // 4), F))
         buffers += [
             pltpu.VMEM((depth, 2, block, lanes), BF),
             pltpu.VMEM((block, lanes // 2), F),
@@ -1467,7 +1470,8 @@
         out_shape=(shape((tokens, width), BF), results[3], results[2], results[1], results[0], shape(small, F)),
         in_specs=[SM] + [VM] * 6 + [ANY] * 9,
         out_specs=(VM,) * 6,
-        scratch_shapes=[
+        scratch_shapes=placed
+        + [
             pltpu.VMEM(kv.shape, BF),
             pltpu.VMEM((width, tokens), BF),
             pltpu.VMEM((width, tokens), BF),
@@ -1541,10 +1545,15 @@
     single = (bias_out, bias_down, gain_one, shift_one, gain_two, shift_two)
     if direct:
         unit = width // images
-        pieces = list(single) + [jnp.zeros((unit,), BF)] * 4
+        gap = jnp.zeros((128 - unit,), BF)
+        pieces = []
+        for item in single:
+            pieces += [item, gap]
+        pieces.append(jnp.zeros((4 * 128,), BF))
         for item in (bias_qv, bias_up):
-            pieces += [item[k : k + unit] for k in range(0, item.shape[0], unit)]
-        small = jnp.stack([jnp.pad(item, (0, 128 - unit)) for item in pieces]).astype(F)
+            for k in range(0, item.shape[0], unit):
+                pieces += [item[k : k + unit], gap]
+        small = jnp.concatenate(pieces).astype(F).reshape(16, 128)
         full_qkv, h, all_kv, x, x_far, q, lse, cols, *rest = front(
             images, bands, scalars, (*own, w_down), small, by_slot(tokens), by_slot(cotangent)
         )
@@ -1570,11 +1579,10 @@
         rest = middle(x, cot, scalars, att, full_out, full_up, full_down, cols, c_up)
     out, dmid, datt, delta, g_out, g_up, g_down, sums = rest
     if direct:
-        gx, *pieces, total = back(
+        gx, *matrices, total = back(
             images, bands, scalars, q, all_kv, delta, lse, datt, x, x_far, h, dmid,
             full_qkv, cols, (g_out, g_up, g_down), sums,
         )
-        matrices = [item.reshape(-1, item.shape[2]).T for item in pieces]
     else:
         dq, dkv = attend_back(scalars, q, all_kv, delta, lse, datt)
         dkv = unshare(images, dkv)

time: 257 us -> 246 us (0.957)
  Pallas kernels: 230 us -> 218 us
    pallas_call x1, Pallas kernels: 125 us -> 114 us  [front(): pl.pallas_call(functools.partial(front_kernel, images, bands), name='fron...]
    reshape x3 -> x0, local copies, waits for them, and re-layouts: 5.32 us -> none  [body(): matrices = [item.reshape(-1, item.shape[2]).T for item in pieces]]
    unnamed x2 -> x5, local copies, waits for them, and re-layouts: 3.42 us -> 8.52 us
    concatenate x0 -> x1, local copies, waits for them, and re-layouts: none -> 4.1 us  [body(): small = jnp.concatenate(pieces).astype(F).reshape(16, 128)]
where the time goes in v8:
time: 246 us; the launch traced here: 245 us
  Pallas kernels  218 us (89%)
  local copies, waits for them, and re-layouts  26 us (11%)
    pallas_call x1, Pallas kernels, front(): pl.pallas_call(functools.partial(front_kernel, images, bands), name='fron...  114 us
    pallas_call x1, Pallas kernels, back(): pl.pallas_call(functools.partial(back_kernel, images, bands), name='back'...  104 us
    unnamed x5, local copies, waits for them, and re-layouts  8.52 us
    reshape x2, local copies, waits for them, and re-layouts, turn_back(): return values.reshape(slots, rows, width).transpose(1, 0, 2)[None]  5.64 us

profile of v8, /device:TPU:0, one launch (start us, length us, event | category | flops | bytes accessed | tf_op | source)
XLA Modules:
  0.0 244.9 jit_solution(9109575362660826243)
XLA Ops:
  0.6 1.7 copy.31.shard_down_ref
  2.4 0.9 fusion.1
  3.3 4.1 %concatenate.3 = bf16[2048]{0:T(1024)(128)(2,1)S(1)} concatenate(bf16[96]{0:T(256)(128)(2,1)} %param.22, bf16[32]{0:T(256)(128)(2,1)S(1)} %broadcast_in_dim.12, bf16[96]{0:T(256)(128)(2,1)} %param.24, bf16[32]{0:T(256)(128)(2,1)S(1)} %broadcast_in_dim.12, bf16[96]{0:T(256)(128)(2,1)} %param.25, bf16[32]{0:T(256)(128)(2,1)S(1)} %broadcast_in_dim.12, bf16[96]{0:T(256)(128)(2,1)} %param.26, ...), dimensions={0} | concatenate | bytes 8192 | tf_op jit(solution)/shard_map/concatenate | solution.py:1556
  7.4 0.6 bitcast_convert_fusion.small_ref
  8.0 2.1 copy.29
  10.1 2.1 copy.30
  12.2 113.6 %front.1 = (bf16[4,2,288,768]{3,2,1,0:T(8,128)(2,1)}, bf16[768,1024]{1,0:T(8,128)(2,1)}, bf16[4,4,384,512]{3,2,1,0:T(8,128)(2,1)}, bf16[768,512]{1,0:T(8,128)(2,...) custom-call(s32[1,2]{1,0:T(1,128)} %scalars_ref.3, ...), custom_call_target="tpu_custom_call" | custom-call | tf_op jit(solution)/shard_map/front/pallas_call | solution.py:843
  125.7 2.8 %copy.38 = bf16[2,256,768]{2,0,1:T(2,128)(2,1)} copy(bf16[2,256,768]{2,1,0:T(8,128)(2,1)} %bitcast.32) | data formatting | bytes 1572864 | tf_op jit(solution)/shard_map/reshape | solution.py:1542
  128.5 104.1 %back.1 = (bf16[512,768]{1,0:T(8,128)(2,1)}, f32[192,288]{1,0:T(8,128)}, f32[192,96]{1,0:T(8,128)}, f32[192,384]{1,0:T(8,128)}, f32[768,96]{1,0:T(8,128)}, /*index=5*/f32[16,768]{1,0:T(8,128)}) custom-call(s32[1,2]{1,0:T(1,128)} %scalars_ref.3, bf16[768,512]{1,0:T(8,128)(2,1)} %get-tuple-element.37.q_ref, f32[16,512]{1,0:T(8,128)} %get-tuple-element.38.delta_ref, ...), custom_call_target="tpu_custom_call" | custom-call | tf_op jit(solution)/shard_map/back/pallas_call | solution.py:1467
  232.6 2.8 %copy.37 = bf16[2,256,768]{2,0,1:T(2,128)(2,1)} copy(bf16[2,256,768]{2,1,0:T(8,128)(2,1)} %bitcast.31) | data formatting | bytes 1572864 | tf_op jit(solution)/shard_map/reshape | solution.py:1542
  235.4 1.9 copy.34
  237.3 0.8 reshape.55
  238.1 0.6 dynamic_slice.24
  238.8 0.6 fusion
  239.4 0.7 dynamic_slice.26
  240.0 1.7 copy.42
  241.7 1.5 copy.43
  243.2 1.7 copy.44
  (2 shorter events, 0.0 us)

commit v9 on v8

--- a/solution.py
+++ b/solution.py
@@ -548,8 +548,9 @@
     qkv_w_out, h_out, kv_out, x_out, x_far_out, q_ref, lse_ref, cols_ref, *rest,
 ):
     results, rest = rest[:8], rest[8:]
-    narrow_ref, wide_ref, x_ref, cot_ref, far_tokens_ref = rest[:5]
-    rest = rest[5:]
+    wide_ref = shard_down_ref
+    narrow_ref, x_ref, cot_ref, far_tokens_ref = rest[:4]
+    rest = rest[4:]
     qkv_w_ref, out_w_ref, up_w_ref, down_w_ref, h_ref, kv_ref, att_ref, up_col_ref = rest[:8]
     theirs_ref, mine_ref, mine_wide_ref, smalls_ref, qv_col_ref, bias_ref, x_far_ref = rest[8:15]
     local_sem, send_sem, recv_sem = rest[15:18]
@@ -642,7 +643,6 @@
         for core in range(2):
             narrow_ref[core, pl.ds(row, count), :] = turned[core * count : (core + 1) * count]
         row += count
-    wide_ref[...] = shard_down_ref[...].astype(F).T.astype(BF)
     greet([at.partner, at.across_x] + others)
     x_moves[0].start()
     x_moves[1].start()
@@ -836,7 +836,7 @@
     full = (width, tokens)
     part = shards[0].shape[0]
     narrow = (2, sum(widths) // 2, part)
-    wide = (shards[3].shape[1], shards[3].shape[0])
+    wide = shards[3].shape
     kv = (bands, groups, 2 * width // groups, tokens)
     weights = [(depth, 2, w, width) for w in widths]
     weights.append((depth, 2, wide[0], 4 * wide[1]))
@@ -863,7 +863,7 @@
         ),
         in_specs=[SM] + [VM] * 7,
         out_specs=(ANY,) * 5 + (VM,) * 8 + (ANY, ANY, VM),
-        scratch_shapes=[pltpu.VMEM(s, BF) for s in (narrow, wide, full, full, (tokens, width))]
+        scratch_shapes=[pltpu.VMEM(s, BF) for s in (narrow, full, full, (tokens, width))]
         + [pltpu.VMEM(s, BF) for s in weights]
         + [
             pltpu.VMEM((width, 2 * tokens), BF),
@@ -1362,6 +1362,8 @@
     share_two(groups - 1)
     weight_grad(0, dwide_ref, 2, 4, slice(None))
     start_swap(0)
+    up[2].step_three()
+    out[0].step_three()
     back_through(1)
     err_far = err_ref[...]
     for s in range(2):
@@ -1374,8 +1376,6 @@
     gain_row = row_sums(err_ref[...] * normed_far)[:1]
     shift_row = row_sums(err_ref[...])[:1]
     first_sum(1)
-    up[2].step_three()
-    out[0].step_three()
     back_through(0)
 
     @pl.loop(0, 2)
@@ -1435,7 +1435,8 @@
     finish_slot(1)
     for m, ref in enumerate((o_down_ref, o_up_ref, o_out_ref, o_qkv_ref)):
         ends[m][3].wait()
-        ref[...] = jnp.concatenate([targets[m][k] for k in range(2)], axis=0).T
+        whole = jnp.concatenate([targets[m][k] for k in range(2)], axis=0)
+        ref[...] = whole if m == 0 else whole.T
         for item in moves[m]:
             item.end()
     for copy in sum(swaps, []) + one + two + err_moves + small_steps + small_last:
@@ -1452,7 +1453,8 @@
     results, placed, buffers = [], [], []
     for m, item in enumerate((g_down, g_up, g_out, w)):
         block, lanes = item.shape[0] // images // 2, item.shape[1]
-        results.append(shape((lanes // 4, 2 * block), F))
+        placing = (lanes // 4, 2 * block) if m else (2 * block, lanes // 4)
+        results.append(shape(placing, F))
         placed.append(pltpu.VMEM((2, block, lanes // 4), F))
         buffers += [
             pltpu.VMEM((depth, 2, block, lanes), BF),
@@ -1545,17 +1547,11 @@
     single = (bias_out, bias_down, gain_one, shift_one, gain_two, shift_two)
     if direct:
         unit = width // images
-        gap = jnp.zeros((128 - unit,), BF)
-        pieces = []
-        for item in single:
-            pieces += [item, gap]
-        pieces.append(jnp.zeros((4 * 128,), BF))
-        for item in (bias_qv, bias_up):
-            for k in range(0, item.shape[0], unit):
-                pieces += [item[k : k + unit], gap]
-        small = jnp.concatenate(pieces).astype(F).reshape(16, 128)
+        units = [jnp.stack(single), jnp.zeros((4, unit), BF)]
+        units += [bias_qv.reshape(-1, unit), bias_up.reshape(-1, unit)]
+        small = jnp.pad(jnp.concatenate(units), ((0, 0), (0, 128 - unit))).astype(F)
         full_qkv, h, all_kv, x, x_far, q, lse, cols, *rest = front(
-            images, bands, scalars, (*own, w_down), small, by_slot(tokens), by_slot(cotangent)
+            images, bands, scalars, (*own, w_down.T), small, by_slot(tokens), by_slot(cotangent)
         )
         full_qkv = full_qkv.reshape(-1, width)
     else:
@@ -1579,10 +1575,11 @@
         rest = middle(x, cot, scalars, att, full_out, full_up, full_down, cols, c_up)
     out, dmid, datt, delta, g_out, g_up, g_down, sums = rest
     if direct:
-        gx, *matrices, total = back(
+        gx, *matrices, turned, total = back(
             images, bands, scalars, q, all_kv, delta, lse, datt, x, x_far, h, dmid,
             full_qkv, cols, (g_out, g_up, g_down), sums,
         )
+        matrices.append(turned.T)
     else:
         dq, dkv = attend_back(scalars, q, all_kv, delta, lse, datt)
         dkv = unshare(images, dkv)

time: 246 us -> 235 us (0.955)
  local copies, waits for them, and re-layouts: 26 us -> 16.2 us
    unnamed x5 -> x12, local copies, waits for them, and re-layouts: 8.52 us -> 2.8 us
    broadcast_in_dim x2, local copies, waits for them, and re-layouts: 0.01 us -> 4.21 us  [the longest x1 4.2 us: turn_back(): return values.reshape(slots, rows, width).transpose(1, 0, 2)[None]]
    reshape x2, local copies, waits for them, and re-layouts: 5.64 us -> 1.5 us  [body(): units += [bias_qv.reshape(-1, unit), bias_up.reshape(-1, unit)]]
    concatenate x1, local copies, waits for them, and re-layouts: 4.1 us -> 0.87 us  [body(): small = jnp.pad(jnp.concatenate(units), ((0, 0), (0, 128 - unit))).astype(F)]
where the time goes in v9:
time: 235 us
  Pallas kernels  217 us (92%)
  local copies, waits for them, and re-layouts  16.2 us (7%)
    pallas_call x1, Pallas kernels, front(): pl.pallas_call(functools.partial(front_kernel, images, bands), name='fron...  113 us
    pallas_call x1, Pallas kernels, back(): pl.pallas_call(functools.partial(back_kernel, images, bands), name='back'...  104 us

profile of v9, /device:TPU:0, one launch (start us, length us, event | category | flops | bytes accessed | tf_op | source)
XLA Modules:
  0.0 234.6 jit_solution(16770472473220557759)
XLA Ops:
  0.6 2.1 copy.30
  2.7 2.1 copy.29
  4.8 0.8 reshape.53
  5.6 0.7 reshape.52
  6.3 0.9 concatenate.3
  7.2 0.6 pad_convert_fusion.small_ref
  7.8 113.4 %front.1 = (bf16[4,2,288,768]{3,2,1,0:T(8,128)(2,1)}, bf16[768,1024]{1,0:T(8,128)(2,1)}, bf16[4,4,384,512]{3,2,1,0:T(8,128)(2,1)}, bf16[768,512]{1,0:T(8,128)(2,...) custom-call(s32[1,2]{1,0:T(1,128)} %scalars_ref.3, ...), custom_call_target="tpu_custom_call" | custom-call | tf_op jit(solution)/shard_map/front/pallas_call | solution.py:843
  121.2 103.6 %back.1 = (bf16[512,768]{1,0:T(8,128)(2,1)}, f32[192,288]{1,0:T(8,128)}, f32[192,96]{1,0:T(8,128)}, f32[192,384]{1,0:T(8,128)}, f32[96,768]{1,0:T(8,128)}, /*index=5*/f32[16,768]{1,0:T(8,128)}) custom-call(s32[1,2]{1,0:T(1,128)} %scalars_ref.3, bf16[768,512]{1,0:T(8,128)(2,1)} %get-tuple-element.37.q_ref, f32[16,512]{1,0:T(8,128)} %get-tuple-element.38.delta_ref, ...), custom_call_target="tpu_custom_call" | custom-call | tf_op jit(solution)/shard_map/back/pallas_call | solution.py:1469
  224.8 0.0 copy-start.2
  224.8 0.0 copy-start.3
  224.8 0.0 copy-start.1
  224.9 0.0 copy-start
  224.9 4.2 %copy_bitcast_fusion = (bf16[1,256,2,768]{3,2,1,0:T(2,128)(2,1)}, bf16[1,256,2,768]{3,2,1,0:T(2,128)(2,1)}) fusion(bf16[2,256,768]{2,1,0:T(8,128)(2,1)} %bitcast.33, bf16[2,256,768]{2,1,0:T(8,128)(2,1)} %bitcast.32), kind=kLoop, calls=%fused_computation | loop fusion | bytes 3145728 | tf_op jit(solution)/shard_map/broadcast_in_dim | solution.py:1544
  229.1 0.8 reshape.59
  229.9 0.6 fusion
  230.5 0.7 dynamic_slice.26
  231.1 0.6 dynamic_slice.24
  231.8 0.0 copy-done.2
  231.8 0.7 copy.39
  232.5 0.0 copy-done.3
  232.5 0.6 copy.40
  233.1 0.0 copy-done.1
  233.1 0.7 copy.41
  233.8 0.0 copy-done
  233.8 0.7 copy.42
  (1 shorter events, 0.0 us)
Async XLA Ops:
  224.8 6.9 %copy-start.2 = (f32[192,288]{1,0:T(8,128)S(1)}, f32[192,288]{1,0:T(8,128)}, u32[]{:S(2)}) copy-start(f32[192,288]{1,0:T(8,128)} %get-tuple-element.82) | copy-start | bytes 663556
  224.8 7.6 %copy-start.3 = (f32[192,96]{1,0:T(8,128)S(1)}, f32[192,96]{1,0:T(8,128)}, u32[]{:S(2)}) copy-start(f32[192,96]{1,0:T(8,128)} %get-tuple-element.83) | copy-start | bytes 221188
  224.8 8.3 %copy-start.1 = (f32[192,384]{1,0:T(8,128)S(1)}, f32[192,384]{1,0:T(8,128)}, u32[]{:S(2)}) copy-start(f32[192,384]{1,0:T(8,128)} %get-tuple-element.84) | copy-start | bytes 884740
  224.9 9.0 %copy-start = (f32[96,768]{1,0:T(8,128)S(1)}, f32[96,768]{1,0:T(8,128)}, u32[]{:S(2)}) copy-start(f32[96,768]{1,0:T(8,128)} %get-tuple-element.56) | copy-start | bytes 884740

commit v10 on v9

--- a/solution.py
+++ b/solution.py
@@ -763,14 +763,15 @@
     when(2, second_slot)
     for j in range(1, 2 * groups):
         when(j - 1, functools.partial(arrive, j // groups, j % groups))
-    when(0, functools.partial(s_out.step, 2))
-    when(1, functools.partial(s_up[0].step, 2))
-    when(2, functools.partial(s_up[1].step, 2))
-    when(3, functools.partial(s_up[2].step, 2), functools.partial(s_out.step, 3))
-    when(4, functools.partial(d_two.step, 2))
-    when(5, functools.partial(d_one.step, 2))
-    when(6, functools.partial(s_up[0].step, 3))
-    when(7, functools.partial(s_up[1].step, 3))
+    when(0, functools.partial(s_up[0].step, 2))
+    when(1, functools.partial(s_up[1].step, 2))
+    when(2, functools.partial(s_up[2].step, 2), functools.partial(s_out.step, 3))
+    when(3, functools.partial(d_two.step, 2))
+    when(4, functools.partial(d_one.step, 2))
+    when(5, functools.partial(s_up[0].step, 3))
+    when(6, functools.partial(s_up[1].step, 3))
+    when(7, functools.partial(s_up[2].step, 3))
+    s_out.step(2)
     project(0)
     arrive(0, 0)
     unroll = HEADS // groups
@@ -794,7 +795,6 @@
     quarter = blocks // 4
 
     def wait_out():
-        s_up[2].step(3)
         s_out.wait()
 
     def wait_up():

time: 235 us -> 234 us (level)
  no operation moved by 1% of the time
where the time goes in v10:
time: 234 us
  Pallas kernels  216 us (92%)
  local copies, waits for them, and re-layouts  16.2 us (7%)
    pallas_call x1, Pallas kernels, front(): pl.pallas_call(functools.partial(front_kernel, images, bands), name='fron...  114 us
    pallas_call x1, Pallas kernels, back(): pl.pallas_call(functools.partial(back_kernel, images, bands), name='back'...  102 us

profile of v10, /device:TPU:0, one launch (start us, length us, event | category | flops | bytes accessed | tf_op | source)
XLA Modules:
  0.0 233.6 jit_solution(12713988753567472844)
XLA Ops:
  0.6 2.1 copy.30
  2.7 2.1 copy.29
  4.8 0.8 reshape.53
  5.6 0.7 reshape.52
  6.3 0.9 concatenate.3
  7.2 0.6 pad_convert_fusion.small_ref
  7.8 114.3 %front.1 = (bf16[4,2,288,768]{3,2,1,0:T(8,128)(2,1)}, bf16[768,1024]{1,0:T(8,128)(2,1)}, bf16[4,4,384,512]{3,2,1,0:T(8,128)(2,1)}, bf16[768,512]{1,0:T(8,128)(2,...) custom-call(s32[1,2]{1,0:T(1,128)} %scalars_ref.3, ...), custom_call_target="tpu_custom_call" | custom-call | tf_op jit(solution)/shard_map/front/pallas_call | solution.py:843
  122.1 101.8 %back.1 = (bf16[512,768]{1,0:T(8,128)(2,1)}, f32[192,288]{1,0:T(8,128)}, f32[192,96]{1,0:T(8,128)}, f32[192,384]{1,0:T(8,128)}, f32[96,768]{1,0:T(8,128)}, /*index=5*/f32[16,768]{1,0:T(8,128)}) custom-call(s32[1,2]{1,0:T(1,128)} %scalars_ref.3, bf16[768,512]{1,0:T(8,128)(2,1)} %get-tuple-element.37.q_ref, f32[16,512]{1,0:T(8,128)} %get-tuple-element.38.delta_ref, ...), custom_call_target="tpu_custom_call" | custom-call | tf_op jit(solution)/shard_map/back/pallas_call | solution.py:1469
  223.8 0.0 copy-start.2
  223.9 0.0 copy-start.3
  223.9 0.0 copy-start.1
  223.9 0.0 copy-start
  223.9 4.2 %copy_bitcast_fusion = (bf16[1,256,2,768]{3,2,1,0:T(2,128)(2,1)}, bf16[1,256,2,768]{3,2,1,0:T(2,128)(2,1)}) fusion(bf16[2,256,768]{2,1,0:T(8,128)(2,1)} %bitcast.33, bf16[2,256,768]{2,1,0:T(8,128)(2,1)} %bitcast.32), kind=kLoop, calls=%fused_computation | loop fusion | bytes 3145728 | tf_op jit(solution)/shard_map/broadcast_in_dim | solution.py:1544
  228.1 0.8 reshape.59
  228.9 0.6 fusion
  229.5 0.7 dynamic_slice.26
  230.1 0.6 dynamic_slice.24
  230.8 0.0 copy-done.2
  230.8 0.7 copy.39
  231.5 0.0 copy-done.3
  231.5 0.6 copy.40
  232.1 0.0 copy-done.1
  232.1 0.7 copy.41
  232.9 0.0 copy-done
  232.9 0.7 copy.42
  (1 shorter events, 0.0 us)
Async XLA Ops:
  223.8 6.9 %copy-start.2 = (f32[192,288]{1,0:T(8,128)S(1)}, f32[192,288]{1,0:T(8,128)}, u32[]{:S(2)}) copy-start(f32[192,288]{1,0:T(8,128)} %get-tuple-element.82) | copy-start | bytes 663556
  223.9 7.6 %copy-start.3 = (f32[192,96]{1,0:T(8,128)S(1)}, f32[192,96]{1,0:T(8,128)}, u32[]{:S(2)}) copy-start(f32[192,96]{1,0:T(8,128)} %get-tuple-element.83) | copy-start | bytes 221188
  223.9 8.3 %copy-start.1 = (f32[192,384]{1,0:T(8,128)S(1)}, f32[192,384]{1,0:T(8,128)}, u32[]{:S(2)}) copy-start(f32[192,384]{1,0:T(8,128)} %get-tuple-element.84) | copy-start | bytes 884740
  223.9 9.0 %copy-start = (f32[96,768]{1,0:T(8,128)S(1)}, f32[96,768]{1,0:T(8,128)}, u32[]{:S(2)}) copy-start(f32[96,768]{1,0:T(8,128)} %get-tuple-element.56) | copy-start | bytes 884740
